TPU v7x, 32 devices: a whole 2x2x4 slice. The times are simulated.
32 devices in a mesh: groups: 2 (over x), wide: 4 (over y, core), pair: 4 (over z).
Axes of the slice: x: 2, y: 2, z: 4, core: 2. Of those that a mesh axis runs over, the one named last changes fastest.
Arguments:
- strips: bfloat16 [8, 2, 4096, 256], P(('groups', 'wide'), None, 'pair'), parts along dimension 0, may hold values from -80 to 80
- offsets: int32 [16, 4, 2], P('groups'), parts along dimension 0, may hold values from 0 to 3328, as said below
- block_subgrid: int32 [64], P(('groups', 'wide', 'pair')), parts along dimension 0, may hold values from 0 to 1
- block_kernel: int32 [64, 2], P(('groups', 'wide', 'pair')), parts along dimension 0, may hold values from 0 to 15
- vis_cells: int32 [64, 2, 2048], P(('groups', 'wide', 'pair')), parts along dimension 0, may hold values from 0 to 248
Outputs:
- predicted: float32 [64, 2, 2048], P(('groups', 'wide', 'pair')), parts along dimension 0
There are 2 independent parts, one for each index of `groups`. A program takes and returns all parts, laid end to end along the dimension named above; each array names one. Nothing has to cross between parts.
Inputs may be any that keep to these rules, and one draw needn't show every extreme that they name: offsets[..., 0] lies in 0 to 3328 and offsets[..., 1] in 0 to 255; both ends of both ranges occur.
All inputs are finite; a program needn't handle non-finite values.
Results may differ from a plain program's by a relative error of at most 0.0033.
The roundings to bfloat16 on the way count: a program that leaves them out, or rounds other values in their place, can miss the bound.
Values may be sent and summed in bfloat16 or wider, within the bound.
No kernel may reach another device: no remote copies, remote signals or barrier semaphores. Data moves between devices by JAX's collectives and lax.ppermute only.
A program may use at most 64 MiB of HBM per device.

v0:
```python
import math

import jax
import jax.numpy as jnp
from jax import lax
from jax.sharding import PartitionSpec as P

L = 4096
SUBW = 256
NVIS = 2048
SUPPORT = 8
OVERSAMPLE = 16
SG_WIDE = 2


def strip_block(row_ids, shift, row_index, length):
    frequency = row_ids - SUBW // 2 + shift
    product = frequency[:, None] * row_index[None, :] % length
    phase_arg = 2.0 * math.pi / length * product.astype(jnp.float32)
    centred = (2 * row_index + 1).astype(jnp.float32) / length - 1.0
    taper = (1.0 - 0.5 * centred * centred) / math.sqrt(length)
    cosine = jnp.cos(phase_arg) * taper[None, :]
    sine = jnp.sin(phase_arg) * taper[None, :]
    upper = jnp.concatenate([cosine, sine], axis=1)
    lower = jnp.concatenate([-sine, cosine], axis=1)
    return jnp.concatenate([upper, lower], axis=0).astype(jnp.bfloat16)


def column_ramp(stacked, shift):
    half = stacked.shape[0] // 2
    part_re = stacked[:half]
    part_im = stacked[half:]
    column_ids = jnp.arange(SUBW, dtype=jnp.int32)
    phase_arg = 2.0 * math.pi / SUBW * (shift * column_ids % SUBW).astype(jnp.float32)
    cosine = jnp.cos(phase_arg)[None, :]
    sine = jnp.sin(phase_arg)[None, :]
    out_re = part_re * cosine + part_im * sine
    out_im = part_im * cosine - part_re * sine
    return jnp.concatenate([out_re, out_im], axis=1)


def transform_table():
    grid_ids = jnp.arange(SUBW, dtype=jnp.int32)
    phase_arg = (
        2.0 * math.pi / SUBW * (grid_ids[:, None] * grid_ids[None, :] % SUBW).astype(jnp.float32)
    )
    cosine = jnp.cos(phase_arg) / math.sqrt(SUBW)
    sine = jnp.sin(phase_arg) / math.sqrt(SUBW)
    upper = jnp.concatenate([cosine, -sine], axis=1)
    lower = jnp.concatenate([sine, cosine], axis=1)
    return jnp.concatenate([upper, lower], axis=0).astype(jnp.bfloat16)


def kernel_taps(fraction):
    points = jnp.arange(SUPPORT, dtype=jnp.float32)
    centre = (SUPPORT - 1) / 2.0 + (fraction.astype(jnp.float32) + 0.5) / OVERSAMPLE - 0.5
    distance = points[None, :] - centre[:, None]
    values = jnp.exp(-distance * distance / 2.88)
    return values / jnp.sum(values, axis=-1, keepdims=True)


def column_sum(spread_rows, col_ids, col_taps):
    columns = jnp.arange(SUBW, dtype=jnp.int32)
    distance = columns[None, None, :] - col_ids[:, :, None]
    weights = jnp.zeros(distance.shape, jnp.float32)
    for tap_index in range(SUPPORT):
        weight = col_taps[:, tap_index][:, None, None]
        weights = jnp.where(distance == tap_index, weight, weights)
    real_part = jnp.sum(weights * spread_rows[..., :SUBW], axis=-1)
    imag_part = jnp.sum(weights * spread_rows[..., SUBW:], axis=-1)
    return jnp.stack([real_part, imag_part], axis=-2)


def on_device(strips, offsets, block_subgrid, block_kernel, vis_cells):
    pair_count = lax.axis_size("pair")
    facet_id = lax.axis_index("wide")
    pair_id = lax.axis_index("pair")
    rows_dev = SG_WIDE * SUBW // pair_count
    local_rows = strips.shape[2]
    xstack = strips.reshape(2 * local_rows, SUBW)
    row_index = pair_id * local_rows + jnp.arange(local_rows, dtype=jnp.int32)

    def single(block_no):
        first = block_no * rows_dev
        subgrid_id = first // SUBW
        row_ids = first % SUBW + jnp.arange(rows_dev, dtype=jnp.int32)
        factor = strip_block(row_ids, offsets[subgrid_id, facet_id, 0], row_index, L)
        product = jnp.dot(factor, xstack, preferred_element_type=jnp.float32)
        return column_ramp(product, offsets[subgrid_id, facet_id, 1])

    stacked = lax.map(
        single, jnp.arange(rows_dev * lax.axis_size(("wide", "pair")) // rows_dev, dtype=jnp.int32)
    )
    summed = lax.psum_scatter(
        stacked.reshape(rows_dev * lax.axis_size(("wide", "pair")), 2 * SUBW),
        ("wide", "pair"),
        scatter_dimension=0,
        tiled=True,
    )
    subgrid = summed.astype(jnp.bfloat16)
    spectrum = jnp.dot(subgrid, transform_table(), preferred_element_type=jnp.float32).astype(
        jnp.bfloat16
    )
    blocks = vis_cells.shape[0]
    row_taps = kernel_taps(block_kernel[:, 0]).astype(jnp.bfloat16)
    col_taps = kernel_taps(block_kernel[:, 1])
    row_base = block_subgrid[:, None] * SUBW + vis_cells[:, 0, :]
    portion = lax.all_gather(spectrum, "pair", axis=0, tiled=True)
    amount = portion.shape[0]
    row_ids = jnp.arange(amount, dtype=jnp.int32)
    distance = row_ids[None, None, :] - row_base[:, :, None]
    dense = jnp.zeros(distance.shape, jnp.float32)
    for tap_index in range(SUPPORT):
        weight = row_taps[:, tap_index].astype(jnp.float32)[:, None, None]
        dense = jnp.where(distance == tap_index, weight, dense)
    dense = dense.astype(jnp.bfloat16).reshape(blocks * NVIS, amount)
    gathered = jnp.dot(dense, portion, preferred_element_type=jnp.float32)
    spread = gathered.reshape(blocks, NVIS, 2 * SUBW)
    return column_sum(spread, vis_cells[:, 1, :], col_taps)


def solution(mesh):
    placed = (
        P(("groups", "wide"), None, "pair", None),
        P("groups", None, None),
        P(("groups", "wide", "pair")),
        P(("groups", "wide", "pair"), None),
        P(("groups", "wide", "pair"), None, None),
    )
    return jax.shard_map(
        on_device,
        mesh=mesh,
        in_specs=placed,
        out_specs=P(("groups", "wide", "pair"), None, None),
        check_vma=False,
    )
```

profile of v0, /device:TPU:0, one launch (start us, length us, event | category | flops | bytes accessed | tf_op | source)
XLA Modules:
  0.0 266.4 jit_solution(9362500942435788892)
XLA Ops:
  6.5 151.5 %while.14 = (s32[]{:T(128)}, f32[16,128,512]{2,1,0:T(8,128)}, s32[16]{0:T(128)S(1)}, s32[8,4,2]{0,2,1:T(2,128)}, s32[]{:T(128)}, /*index=5*/bf16[2048,256]{1,0:T...) while((s32[]{:T(128)}, f32[16,128,512]{2,1,0:T(8,128)}, ...), condition=%wide.region_3.4_spmd.clone, body=%wide.region_2.3_spmd.clone.sunk | while | flops 275528608 | bytes 5003174 | solution.py:91
  7.9 1.4 constant_dynamic-slice_fusion.3
  10.0 2.5 fusion.103
  12.4 1.8 fusion.104
  17.4 1.4 constant_dynamic-slice_fusion.3
  19.4 2.5 fusion.103
  21.9 1.8 fusion.104
  26.8 1.4 constant_dynamic-slice_fusion.3
  28.9 2.5 fusion.103
  31.4 1.8 fusion.104
  36.3 1.4 constant_dynamic-slice_fusion.3
  38.3 2.5 fusion.103
  40.8 1.8 fusion.104
  45.8 1.4 constant_dynamic-slice_fusion.3
  47.8 2.5 fusion.103
  50.3 1.8 fusion.104
  55.3 1.4 constant_dynamic-slice_fusion.3
  57.3 2.5 fusion.103
  59.8 1.8 fusion.104
  64.7 1.4 constant_dynamic-slice_fusion.3
  66.8 2.5 fusion.103
  69.2 1.8 fusion.104
  74.2 1.4 constant_dynamic-slice_fusion.3
  76.2 2.5 fusion.103
  78.7 1.8 fusion.104
  83.7 1.4 constant_dynamic-slice_fusion.3
  85.7 2.5 fusion.103
  88.2 1.8 fusion.104
  93.1 1.4 constant_dynamic-slice_fusion.3
  95.2 2.5 fusion.103
  97.7 1.8 fusion.104
  102.6 1.4 constant_dynamic-slice_fusion.3
  104.6 2.5 fusion.103
  107.1 1.8 fusion.104
  114.1 2.5 fusion.103
  116.6 1.8 fusion.104
  123.6 2.5 fusion.103
  126.1 1.8 fusion.104
  133.0 2.5 fusion.103
  135.5 1.8 fusion.104
  142.5 2.5 fusion.103
  145.0 1.8 fusion.104
  152.0 2.5 fusion.103
  154.5 1.8 fusion.104
  161.4 72.2 %reduce-scatter.2.cloned.1.call-done = f32[128,512]{1,0:T(8,128)} async-done(((f32[2048,512]{1,0:T(8,128)}), f32[128,512]{1,0:T(8,128)}) %reduce-scatter.2.cloned.1.call-update) | async-done | bytes 262160 | tf_op jit(solution)/shard_map/reduce_scatter | solution.py:94
  234.8 14.9 %all_gather.3 = bf16[512,512]{0,1:T(8,128)(2,1)S(1)} all-gather(bf16[128,512]{0,1:T(8,128)(2,1)S(1)} %convolution_convert_fusion), channel_id=1, replica_groups=mesh['groups'=2,'wide'=4,'pair'=4] {'pair'}, dimensions={0}, use_global_device_ids=true | all-gather | bytes 655360 | tf_op jit(solution)/shard_map/all_gather | solution.py:108
  249.7 6.0 %fusion.30 = f32[2,2048,512]{1,2,0:T(8,128)S(1)} fusion(bf16[2]{0:T(256)(128)(2,1)S(1)} %get-tuple-element.198, bf16[2]{0:T(256)(128)(2,1)S(1)} %get-tuple-element.199, bf16[2]{0:T(256)(128)(2,1)S(1)} %get-tuple-element.200, bf16[2]{0:T(256)(128)(2,1)S(1)} %get-tuple-element.201, bf16[2]{0:T(256)(128)(2,1)S(1)} %get-tuple-element.202, ...), kind=kOutput, calls=%fused_computation.51 | convolution fusion | flops 2183135232 | bytes 8929312 | tf_op jit(solution)/shard_map/dot_general | solution.py:117
  255.7 3.2 %fusion.32 = (f32[2,2048]{1,0:T(2,128)S(1)}, f32[2,2048]{1,0:T(2,128)S(1)}) fusion(f32[2,2048,512]{1,2,0:T(8,128)S(1)} %fusion.30, f32[2]{0:T(128)S(1)} %get-tuple-element.190, f32[2]{0:T(128)S(1)} %get-tuple-element.191, f32[2]{0:T(128)S(1)} %get-tuple-element.192, f32[2]{0:T(128)S(1)} %get-tuple-element.193, f32[2]{0:T(128)S(1)} %get-tuple-element.194, ...), kind=kLoop, calls=%fused_computation.55 | loop fusion | flops 22011904 | bytes 8437824 | tf_op jit(solution)/shard_map/reduce_sum | solution.py:69
  (174 shorter events, 60.4 us)
Async XLA Ops:
  6.5 227.0 %reduce-scatter.2.cloned.1.call-start = ((), (), s32[]{:S(2)}) async-start(), calls=%async_computation.1 | async-start | bytes 4456448 | tf_op jit(solution)/shard_map/reduce_scatter | solution.py:94
  158.0 0.8 copy-start
  158.0 0.8 copy-start.1
  158.0 3.2 %copy-start.2 = (s32[2]{0:T(128)S(1)}, s32[2]{0:T(128)}, u32[]{:S(2)}) copy-start(s32[2]{0:T(128)} %param.9) | copy-start | bytes 28
Sparse Core Ops, SparseCore 0:
  158.2 75.2 reduce-scatter.1
where the time goes:
time: 268 us; the launch traced here: 266 us
  waiting for transfers between devices  72.2 us (27%)
  other arithmetic  69.1 us (26%)
  local copies, waits for them, and re-layouts  48.5 us (18%)
  matrix products  35.7 us (13%)
  blocking collectives  14.9 us (6%)
  between operations  13.5 us (5%)
  loops' own time  12.6 us (5%)
    reduce_scatter x1, waiting for transfers between devices, on_device(): lax.psum_scatter(stacked.reshape(rows_dev * lax.axis_size(('wide', 'pair'...  72.2 us
    another operation x18, other arithmetic  41.8 us
    dot_general x16, matrix products, single(): product = jnp.dot(factor, xstack, preferred_element_type=jnp.float32)  28.4 us
    dynamic_slice x16, local copies, waits for them, and re-layouts, single(): return column_ramp(product, offsets[subgrid_id, facet_id, 1])  22.8 us
    all_gather x1, blocking collectives, on_device(): portion = lax.all_gather(spectrum, 'pair', axis=0, tiled=True)  14.9 us
    dynamic_update_slice x32, local copies, waits for them, and re-layouts, on_device(): lax.map(single, jnp.arange(rows_dev * lax.axis_size(('wide', 'pair')) //...  13.8 us
    another operation x1, loops' own time, on_device(): lax.map(single, jnp.arange(rows_dev * lax.axis_size(('wide', 'pair')) //...  12.6 us
    sin x16, other arithmetic, column_ramp(): sine = jnp.sin(phase_arg)[None, :]  11.8 us
  transfers between devices with their start and end apart: 1, of which 1 were waited for; matrix products, arithmetic and copies ran while one was open for 1% of the time, Pallas kernels for 0%

commit v1 on v0

v1 whole, which is shorter than its diff:
```python
import functools
import math

import jax
import jax.numpy as jnp
from jax import lax
from jax.experimental import pallas as pl
from jax.experimental.pallas import tpu as pltpu
from jax.sharding import PartitionSpec as P

L = 4096
SUBW = 256
NVIS = 2048
SUPPORT = 8
OVERSAMPLE = 16
SG_WIDE = 2
CHUNKS = 4
CW = SUBW // CHUNKS
LANES = 2 * CW
FINE = 16


def cos_sin(numerator, length):
    angle = 2.0 * math.pi / length * (numerator % length).astype(jnp.float32)
    return jnp.cos(angle), jnp.sin(angle)


def kernel_taps(fraction):
    points = jnp.arange(SUPPORT, dtype=jnp.float32)
    centre = (SUPPORT - 1) / 2.0 + (fraction.astype(jnp.float32) + 0.5) / OVERSAMPLE - 0.5
    distance = points[None, :] - centre[:, None]
    values = jnp.exp(-distance * distance / 2.88)
    return values / jnp.sum(values, axis=-1, keepdims=True)


def table_chunked():
    grid_ids = jnp.arange(SUBW, dtype=jnp.int32)
    cosine, sine = cos_sin(grid_ids[:, None] * grid_ids[None, :], SUBW)
    cosine = cosine / math.sqrt(SUBW)
    sine = sine / math.sqrt(SUBW)
    upper = jnp.concatenate([cosine, -sine], axis=1).reshape(CHUNKS, 1, CW, 2 * SUBW)
    lower = jnp.concatenate([sine, cosine], axis=1).reshape(CHUNKS, 1, CW, 2 * SUBW)
    both = jnp.concatenate([upper, lower], axis=1)
    return both.reshape(2 * SUBW, 2 * SUBW).astype(jnp.bfloat16)


def factor_kernel(turn_ref, coarse_ref, fine_ref, out_ref):
    length = turn_ref.shape[-1]
    turn_c = turn_ref[0, 0, 0:1]
    turn_s = turn_ref[0, 0, 1:2]
    fine_c = fine_ref[0]
    fine_s = fine_ref[1]
    for high in range(SUBW // FINE):
        coarse_c = coarse_ref[0, high : high + 1]
        coarse_s = coarse_ref[1, high : high + 1]
        base_c = turn_c * coarse_c - turn_s * coarse_s
        base_s = turn_s * coarse_c + turn_c * coarse_s
        rows = pl.ds(high * FINE, FINE)
        out_ref[0, 0, rows, :length] = (base_c * fine_c - base_s * fine_s).astype(jnp.bfloat16)
        out_ref[0, 0, rows, length:] = (base_s * fine_c + base_c * fine_s).astype(jnp.bfloat16)


def swap_halves(value):
    return pltpu.roll(value, CW, 1)


def ramped(factor, data, ramp_c, ramp_s):
    length = data.shape[0]
    direct = jnp.dot(factor[:, :length], data, preferred_element_type=jnp.float32)
    crossed = jnp.dot(factor[:, length:], data, preferred_element_type=jnp.float32)
    pieces = []
    for start in range(0, data.shape[1], LANES):
        lane = lax.broadcasted_iota(jnp.int32, (1, LANES), 1)
        sign = jnp.where(lane < CW, 1.0, -1.0).astype(jnp.float32)
        part = direct[:, start : start + LANES] + sign * swap_halves(
            crossed[:, start : start + LANES]
        )
        pieces.append(
            part * ramp_c[:, start : start + LANES]
            + swap_halves(part) * ramp_s[:, start : start + LANES]
        )
    return pieces


def own_kernel(factor_ref, data_ref, ramp_ref, out_ref):
    pieces = ramped(factor_ref[0, 0], data_ref[...], ramp_ref[0, 0, 0:1], ramp_ref[0, 0, 1:2])
    for index, piece in enumerate(pieces):
        out_ref[0, :, index * LANES : (index + 1) * LANES] = piece


def chunk_kernel(count, factor_ref, own_ref, ramp_ref, *refs):
    datas = refs[:count]
    keep_ref, send_ref = refs[count:]
    step = pl.program_id(0)
    total = own_ref[0]
    for index in range(count):
        total = total + ramped(
            factor_ref[index, 0], datas[index][...], ramp_ref[index, 0, 0:1], ramp_ref[index, 0, 1:2]
        )[0]
    rows = pl.ds(pl.multiple_of((step % SG_WIDE) * SUBW, SUBW), SUBW)

    @pl.when(step < SG_WIDE)
    def _():
        keep_ref[rows, :] = total

    @pl.when(step >= SG_WIDE)
    def _():
        send_ref[rows, :] = total


def degrid_kernel(pairs, pick_ref, coltap_ref, rowmat_ref, cells_ref, table_ref, *refs):
    count = CHUNKS * pairs
    pieces = refs[:count]
    out_ref, held, tall = refs[count:]
    block = pl.program_id(0)
    rows_dev = pieces[0].shape[0]

    @pl.when(block == 0)
    def _():
        place = pick_ref[1, 0]
        for chunk in range(CHUNKS):
            for step in range(pairs):
                at = pl.multiple_of((place ^ step) * rows_dev, rows_dev)
                held[pl.ds(at, rows_dev), chunk * LANES : (chunk + 1) * LANES] = pieces[
                    chunk * pairs + step
                ][...]

    first = pl.multiple_of(pick_ref[0, block] * SUBW, SUBW)
    subgrid = held[pl.ds(first, SUBW), :]
    spectrum = jnp.dot(subgrid, table_ref[...], preferred_element_type=jnp.float32).astype(
        jnp.bfloat16
    )
    tall[0 : 2 * SUBW, :] = lax.dot_general(
        spectrum, rowmat_ref[0], (((0,), (0,)), ((), ())), preferred_element_type=jnp.float32
    )
    tall[2 * SUBW :, :] = jnp.zeros((SUPPORT, SUBW), jnp.float32)
    smooth = coltap_ref[block, 0] * tall[0 : 2 * SUBW, :]
    for tap in range(1, SUPPORT):
        smooth = smooth + coltap_ref[block, tap] * tall[tap : tap + 2 * SUBW, :]
    high = smooth.astype(jnp.bfloat16)
    low = (smooth - high.astype(jnp.float32)).astype(jnp.bfloat16)
    width = 512
    for start in range(0, NVIS, width):
        row_at = cells_ref[0, 0:1, start : start + width]
        col_at = cells_ref[0, 1:2, start : start + width]
        ids = lax.broadcasted_iota(jnp.int32, (SUBW, width), 0)
        chosen = jnp.where(ids == row_at, 1.0, 0.0).astype(jnp.bfloat16)
        picked = jnp.dot(high, chosen, preferred_element_type=jnp.float32) + jnp.dot(
            low, chosen, preferred_element_type=jnp.float32
        )
        hit = ids == col_at
        out_ref[0, 0:1, start : start + width] = jnp.sum(
            jnp.where(hit, picked[:SUBW], 0.0), axis=0, keepdims=True
        )
        out_ref[0, 1:2, start : start + width] = jnp.sum(
            jnp.where(hit, picked[SUBW:], 0.0), axis=0, keepdims=True
        )


def on_device(strips, offsets, block_subgrid, block_kernel, vis_cells):
    pairs = lax.axis_size("pair")
    wides = lax.axis_size("wide")
    chips = wides // 2
    wide_id = lax.axis_index("wide")
    pair_id = lax.axis_index("pair")
    length = strips.shape[2]
    shown = 2 * SG_WIDE
    rows_dev = SG_WIDE * SUBW // pairs

    data = [
        jnp.concatenate(
            [strips[0, 0, :, i * CW : (i + 1) * CW], strips[0, 1, :, i * CW : (i + 1) * CW]], axis=1
        )
        for i in range(CHUNKS)
    ]
    arrived = [
        [
            lax.ppermute(
                part, "wide", [(w, (w + 2 * hop) % wides) for w in range(wides)]
            )
            for hop in range(1, chips)
        ]
        for part in data
    ]

    facets = (wide_id - 2 * jnp.arange(chips, dtype=jnp.int32)) % wides
    other = wide_id ^ 1
    lead = jnp.arange(SG_WIDE, dtype=jnp.int32)
    subgrids = jnp.concatenate([SG_WIDE * wide_id + lead, SG_WIDE * other + lead])
    shifts = offsets[subgrids[None, :], facets[:, None]]

    row_index = pair_id * length + jnp.arange(length, dtype=jnp.int32)
    centred = (2 * row_index + 1).astype(jnp.float32) / L - 1.0
    taper = (1.0 - 0.5 * centred * centred) / math.sqrt(L)
    turn = jnp.stack(
        cos_sin((shifts[:, :, 0] + L - SUBW // 2)[..., None] * row_index, L), axis=2
    ) * taper
    fine = jnp.stack(cos_sin(jnp.arange(FINE, dtype=jnp.int32)[:, None] * row_index, L))
    coarse = jnp.stack(
        cos_sin(jnp.arange(0, SUBW, FINE, dtype=jnp.int32)[:, None] * row_index, L)
    )
    factor = pl.pallas_call(
        factor_kernel,
        out_shape=jax.ShapeDtypeStruct((chips, shown, SUBW, 2 * length), jnp.bfloat16),
        grid=(chips, shown),
        in_specs=[
            pl.BlockSpec((1, 1, 2, length), lambda i, j: (i, j, 0, 0)),
            pl.BlockSpec((2, SUBW // FINE, length), lambda i, j: (0, 0, 0)),
            pl.BlockSpec((2, FINE, length), lambda i, j: (0, 0, 0)),
        ],
        out_specs=pl.BlockSpec((1, 1, SUBW, 2 * length), lambda i, j: (i, j, 0, 0)),
        name="factors",
    )(turn, coarse, fine)

    lanes = jnp.arange(2 * SUBW, dtype=jnp.int32)
    column = lanes // LANES * CW + lanes % CW
    ramp_c, ramp_s = cos_sin(shifts[:, :, 1][..., None] * column, SUBW)
    ramp = jnp.stack([ramp_c, jnp.where(lanes % LANES < CW, ramp_s, -ramp_s)], axis=2)

    own = pl.pallas_call(
        own_kernel,
        out_shape=jax.ShapeDtypeStruct((shown, SUBW, 2 * SUBW), jnp.float32),
        grid=(shown,),
        in_specs=[
            pl.BlockSpec((1, 1, SUBW, 2 * length), lambda j: (0, j, 0, 0)),
            pl.BlockSpec((length, 2 * SUBW), lambda j: (0, 0)),
            pl.BlockSpec((1, 1, 2, 2 * SUBW), lambda j: (0, j, 0, 0)),
        ],
        out_specs=pl.BlockSpec((1, SUBW, 2 * SUBW), lambda j: (j, 0, 0)),
        name="own_facet",
    )(factor, jnp.concatenate(data, axis=1), ramp)

    factor_rest = factor[1:]
    ramp_rest = ramp[1:]

    def chunk_sums(index):
        hops = chips - 1
        return pl.pallas_call(
            functools.partial(chunk_kernel, hops),
            out_shape=[jax.ShapeDtypeStruct((SG_WIDE * SUBW, LANES), jnp.float32)] * 2,
            grid=(shown,),
            in_specs=[
                pl.BlockSpec((hops, 1, SUBW, 2 * length), lambda j: (0, j, 0, 0)),
                pl.BlockSpec((1, SUBW, LANES), lambda j: (j, 0, index)),
                pl.BlockSpec((hops, 1, 2, LANES), lambda j: (0, j, 0, index)),
            ]
            + [pl.BlockSpec((length, LANES), lambda j: (0, 0))] * hops,
            out_specs=[pl.BlockSpec((SG_WIDE * SUBW, LANES), lambda j: (0, 0))] * 2,
            name="chunk_sums",
        )(factor_rest, own, ramp_rest, *arrived[index])

    def reduce_rows(index):
        keep, send = chunk_sums(index)
        total = keep + lax.ppermute(send, "wide", [(w, w ^ 1) for w in range(wides)])
        bits = pairs.bit_length() - 1
        total = total.reshape((2,) * bits + (rows_dev, LANES))
        for bit in range(bits):
            axis = total.ndim - 3
            mine = (pair_id >> bit) & 1
            passed = lax.dynamic_index_in_dim(total, 1 - mine, axis, keepdims=False)
            held = lax.dynamic_index_in_dim(total, mine, axis, keepdims=False)
            total = held + lax.ppermute(
                passed, "pair", [(p, p ^ (1 << bit)) for p in range(pairs)]
            )
        rounded = total.astype(jnp.bfloat16)
        return [rounded] + [
            lax.ppermute(rounded, "pair", [(p, p ^ step) for p in range(pairs)])
            for step in range(1, pairs)
        ]

    pieces = [piece for index in range(CHUNKS) for piece in reduce_rows(index)]

    blocks = vis_cells.shape[0]
    row_taps = kernel_taps(block_kernel[:, 0]).astype(jnp.bfloat16)
    col_taps = kernel_taps(block_kernel[:, 1])
    ids = jnp.arange(SUBW, dtype=jnp.int32)
    distance = ids[:, None] - ids[None, :]
    row_matrix = jnp.zeros((blocks, SUBW, SUBW), jnp.float32)
    for tap in range(SUPPORT):
        row_matrix = jnp.where(
            distance == tap, row_taps[:, tap].astype(jnp.float32)[:, None, None], row_matrix
        )
    row_matrix = row_matrix.astype(jnp.bfloat16)
    picks = jnp.stack([block_subgrid, jnp.full_like(block_subgrid, pair_id)])

    return pl.pallas_call(
        functools.partial(degrid_kernel, pairs),
        out_shape=jax.ShapeDtypeStruct((blocks, 2, NVIS), jnp.float32),
        grid=(blocks,),
        in_specs=[
            pl.BlockSpec(memory_space=pltpu.SMEM),
            pl.BlockSpec(memory_space=pltpu.SMEM),
            pl.BlockSpec((1, SUBW, SUBW), lambda b: (b, 0, 0)),
            pl.BlockSpec((1, 2, NVIS), lambda b: (b, 0, 0)),
            pl.BlockSpec((2 * SUBW, 2 * SUBW), lambda b: (0, 0)),
        ]
        + [pl.BlockSpec((rows_dev, LANES), lambda b: (0, 0))] * len(pieces),
        out_specs=pl.BlockSpec((1, 2, NVIS), lambda b: (b, 0, 0)),
        scratch_shapes=[
            pltpu.VMEM((SG_WIDE * SUBW, 2 * SUBW), jnp.bfloat16),
            pltpu.VMEM((2 * SUBW + SUPPORT, SUBW), jnp.float32),
        ],
        name="degrid",
    )(picks, col_taps, row_matrix, vis_cells, table_chunked(), *pieces)


def solution(mesh):
    placed = (
        P(("groups", "wide"), None, "pair", None),
        P("groups", None, None),
        P(("groups", "wide", "pair")),
        P(("groups", "wide", "pair"), None),
        P(("groups", "wide", "pair"), None, None),
    )
    return jax.shard_map(
        on_device,
        mesh=mesh,
        in_specs=placed,
        out_specs=P(("groups", "wide", "pair"), None, None),
        check_vma=False,
    )
```

time: 268 us -> 122 us (0.46)
  waiting for transfers between devices: 72.2 us -> 6.5 us
  other arithmetic: 69.1 us -> 21.9 us
  Pallas kernels: 0 us -> 41.1 us
  starting transfers between devices: 0.01 us -> 37.3 us
  matrix products: 35.7 us -> 0 us
  local copies, waits for them, and re-layouts: 48.5 us -> 13.8 us
  blocking collectives: 14.9 us -> 0 us
  between operations: 13.5 us -> 0.52 us
  loops' own time: 12.6 us -> 0 us
    reduce_scatter x1 -> x0, waiting for transfers between devices: 72.2 us -> none  [on_device(): lax.psum_scatter(stacked.reshape(rows_dev * lax.axis_size(('wide', 'pair'...]
    pallas_call x0 -> x7, Pallas kernels: none -> 41.1 us  [the longest x4 20.4 us: chunk_sums(): pl.pallas_call(functools.partial(chunk_kernel, hops), out_shape=[jax.Shap...]
    another operation x19 -> x4, other arithmetic: 41.8 us -> 3.3 us
    ppermute x0 -> x28, starting transfers between devices: none -> 37.3 us  [the longest x12 18 us: reduce_rows(): lax.ppermute(rounded, 'pair', [(p, p ^ step) for p in range(pairs)])]
    dot_general x18 -> x0, matrix products: 35.7 us -> none  [the longest x16 28.4 us: single(): product = jnp.dot(factor, xstack, preferred_element_type=jnp.float32)]
    dynamic_slice x32 -> x0, local copies, waits for them, and re-layouts: 33.3 us -> none  [the longest x16 22.8 us: single(): return column_ramp(product, offsets[subgrid_id, facet_id, 1])]
    all_gather x1 -> x0, blocking collectives: 14.9 us -> none  [on_device(): portion = lax.all_gather(spectrum, 'pair', axis=0, tiled=True)]
    dynamic_update_slice x32 -> x0, local copies, waits for them, and re-layouts: 13.8 us -> none  [on_device(): lax.map(single, jnp.arange(rows_dev * lax.axis_size(('wide', 'pair')) //...]
  transfers between devices with their start and end apart: 1 -> 28, of which waited for: 1 -> 6; matrix products, arithmetic and copies ran while one was open for 1% -> 25% of each run, Pallas kernels for 0% -> 28%
where the time goes in v1:
time: 122 us; the launch traced here: 121 us
  Pallas kernels  41.1 us (34%)
  starting transfers between devices  37.3 us (31%)
  other arithmetic  21.9 us (18%)
  local copies, waits for them, and re-layouts  13.8 us (11%)
  waiting for transfers between devices  6.5 us (5%)
    pallas_call x4, Pallas kernels, chunk_sums(): pl.pallas_call(functools.partial(chunk_kernel, hops), out_shape=[jax.Shap...  20.4 us
    ppermute x12, starting transfers between devices, reduce_rows(): lax.ppermute(rounded, 'pair', [(p, p ^ step) for p in range(pairs)])  18 us
    ppermute x8, starting transfers between devices, reduce_rows(): lax.ppermute(passed, 'pair', [(p, p ^ 1 << bit) for p in range(pairs)])  13.2 us
    pallas_call x1, Pallas kernels, on_device(): pl.pallas_call(factor_kernel, out_shape=jax.ShapeDtypeStruct((chips, show...  6.97 us
    pallas_call x1, Pallas kernels, on_device(): pl.pallas_call(functools.partial(degrid_kernel, pairs), out_shape=jax.Sha...  6.88 us
    pallas_call x1, Pallas kernels, on_device(): pl.pallas_call(own_kernel, out_shape=jax.ShapeDtypeStruct((shown, SUBW, 2...  6.87 us
    ppermute x8, waiting for transfers between devices, reduce_rows(): lax.ppermute(passed, 'pair', [(p, p ^ 1 << bit) for p in range(pairs)])  5.66 us
    ppermute x4, starting transfers between devices, on_device(): lax.ppermute(part, 'wide', [(w, (w + 2 * hop) % wides) for w in range(wid...  5.06 us
  transfers between devices with their start and end apart: 28, of which 6 were waited for; matrix products, arithmetic and copies ran while one was open for 25% of the time, Pallas kernels for 28%

profile of v1, /device:TPU:0, one launch (start us, length us, event | category | flops | bytes accessed | tf_op | source)
XLA Modules:
  0.0 121.2 jit_solution(7731701209881717800)
XLA Ops:
  0.0 2.0 %slice_bitcast_fusion = (bf16[1024,64]{1,0:T(8,128)(2,1)S(1)}, bf16[1024,64]{1,0:T(8,128)(2,1)S(1)}, bf16[1024,64]{1,0:T(8,128)(2,1)S(1)}, bf16[1024,64]{1,0:T(8...) fusion(bf16[1,2,1024,256]{3,2,1,0:T(8,128)(2,1)} %param.5), kind=kLoop, calls=%fused_computation.13 | loop fusion | bytes 2097152 | tf_op jit(solution)/shard_map/squeeze | solution.py:172
  2.0 0.9 pad_maximum_fusion
  2.9 3.0 %collective-permute-start = (bf16[1024,128]{1,0:T(8,128)(2,1)}, bf16[1024,128]{1,0:T(8,128)(2,1)S(1)}, u32[]{:S(2)}, u32[]{:S(2)}) collective-permute-start(bf16[1024,128]{1,0:T(8,128)(2,1)} %pad_maximum_fusion), channel_id=1, source_target_pairs={{0,8},{4,12},{8,0},{12,4},{1,9},{5,13},{9,1},{13,5},{2,10},{6,14},... | collective-permute-start | bytes 786440 | tf_op jit(solution)/shard_map/ppermute | solution.py:178
  5.9 0.8 pad_maximum_fusion.1
  6.7 0.9 pad_maximum_fusion.2
  7.6 2.0 %collective-permute-start.14 = (bf16[1024,128]{1,0:T(8,128)(2,1)}, bf16[1024,128]{1,0:T(8,128)(2,1)S(1)}, u32[]{:S(2)}, u32[]{:S(2)}) collective-permute-start(bf16[1024,128]{1,0:T(8,128)(2,1)} %pad_maximum_fusion.2), channel_id=1, source_target_pairs={{0,8},{4,12},{8,0},{12,4},{1,9},{5,13},{9,1},{13,5},{2,10},{6,14},... | collective-permute-start | bytes 786440 | tf_op jit(solution)/shard_map/ppermute | solution.py:178
  11.5 0.7 fusion.11
  12.2 0.7 fusion.9
  12.9 0.7 fusion.7
  14.6 0.8 add_reduce_fusion
  15.6 0.8 convert_reduce_fusion.7
  18.1 1.0 fusion.56
  19.6 1.3 %negate_convert_fusion = (bf16[4,1,64,256]{3,2,1,0:T(8,128)(2,1)S(1)}, bf16[4,1,64,256]{3,2,1,0:T(8,128)(2,1)S(1)}, bf16[4,1,64,256]{3,2,1,0:T(8,128)(2,1)S(1)}) fusion(s32[4,64]{1,0:T(4,128)S(1)} %multiply_add_fusion), kind=kLoop, calls=%fused_computation.21 | loop fusion | flops 1310720 | bytes 394240 | tf_op jit(solution)/shard_map/convert.13
  20.9 1.3 %fusion.68 = (f32[2,4,1,512]{3,2,1,0:T(1,128)S(1)}, f32[2,4,1,512]{3,2,1,0:T(1,128)S(1)}) fusion(s32[512]{0:T(512)} %fusion.49, s32[2,4]{1,0:T(2,128)} %bitcast.77, pred[512]{0:T(512)(128)(4,1)} %fusion.50), kind=kLoop, calls=%fused_computation.162 | loop fusion | flops 65536 | bytes 35360 | tf_op jit(solution)/shard_map/cos | solution.py:25
  22.2 1.4 %maximum_multiply_fusion.turn_ref = f32[2,4,2,1024]{3,2,1,0:T(2,128)} fusion(f32[2,4,1,1024]{3,2,1,0:T(1,128)S(1)} %get-tuple-element.40, f32[2,4,1,1024]{3,2,1,0:T(1,128)S(1)} %get-tuple-element.39, f32[1024]{0:T(1024)} %fusion.47), kind=kLoop, calls=%fused_computation.63 | loop fusion | flops 32768 | bytes 135168 | tf_op jit(solution)/shard_map/mul | solution.py:195
  23.6 2.2 %select_convert_fusion.rowmat_ref = bf16[2,256,256]{2,1,0:T(8,128)(2,1)} fusion(bf16[2]{0:T(256)(128)(2,1)} %get-tuple-element.24, bf16[2]{0:T(256)(128)(2,1)} %get-tuple-element.25, bf16[2]{0:T(256)(128)(2,1)} %get-tuple-element.26, bf16[2]{0:T(256)(128)(2,1)} %get-tuple-element.27, bf16[2]{0:T(256)(128)(2,1)} %get-tuple-element.28, ...), kind=kLoop, calls=%fused_computation.2 | loop fusion | flops 1048576 | bytes 786464 | tf_op jit(solution)/shard_map/convert_element_type | solution.py:283
  25.8 0.7 pad_maximum_fusion.4
  27.2 2.1 %concatenate.44.data_ref = bf16[1024,512]{1,0:T(8,128)(2,1)} concatenate(bf16[1024,64]{1,0:T(8,128)(2,1)S(1)} %get-tuple-element.37, bf16[1024,64]{1,0:T(8,128)(2,1)S(1)} %get-tuple-element.36, bf16[1024,64]{1,0:T(8,128)(2,1)S(1)} %get-tuple-element.35, bf16[1024,64]{1,0:T(8,128)(2,1)S(1)} %get-tuple-element.34, bf16[1024,64]{1,0:T(8,128)(2,1)S(1)} %get-tuple-element.33, ...), dimensions={1} | concatenate | bytes 2097152 | tf_op jit(solution)/shard_map/concatenate | solution.py:231
  29.3 7.0 %factors.1.factor_ref = bf16[2,4,256,2048]{3,2,1,0:T(8,128)(2,1)} custom-call(f32[2,4,2,1024]{3,2,1,0:T(2,128)} %maximum_multiply_fusion.turn_ref, f32[2,16,1024]{2,1,0:T(8,128)} %get-tuple-element.64.coarse_ref, f32[2,16,1024]{2,1,0:T(8,128)} %get-tuple-element.65.fine_ref), custom_call_target="tpu_custom_call" | custom-call | tf_op jit(solution)/shard_map/factors/pallas_call | solution.py:202
  36.3 4.8 %slice.91.factor_ref = bf16[1,4,256,2048]{3,2,1,0:T(8,128)(2,1)} slice(bf16[2,4,256,2048]{3,2,1,0:T(8,128)(2,1)} %factors.1.factor_ref), slice={[1:2], [0:4], [0:256], [0:2048]} | slice | bytes 8388608 | tf_op jit(solution)/shard_map/slice | solution.py:233
  41.0 6.9 %own_facet.1.own_ref = f32[4,256,512]{2,1,0:T(8,128)} custom-call(bf16[2,4,256,2048]{3,2,1,0:T(8,128)(2,1)} %factors.1.factor_ref, bf16[1024,512]{1,0:T(8,128)(2,1)} %concatenate.44.data_ref, f32[2,4,2,512]{3,2,1,0:T(2,128)} %pad_maximum_fusion.6.ramp_ref), custom_call_target="tpu_custom_call" | custom-call | tf_op jit(solution)/shard_map/own_facet/pallas_call | solution.py:220
  48.5 5.1 %chunk_sums.5 = (f32[512,128]{1,0:T(8,128)}, f32[512,128]{1,0:T(8,128)}) custom-call(bf16[1,4,256,2048]{3,2,1,0:T(8,128)(2,1)} %slice.91.factor_ref, f32[4,256,512]{2,1,0:T(8,128)} %own_facet.1.own_ref, f32[1,4,2,512]{3,2,1,0:T(2,128)} %fusion.37.ramp_ref, bf16[1024,128]{1,0:T(8,128)(2,1)} %collective-permute-done.7.refs_0_), custom_call_target="tpu_custom_call" | custom-call | tf_op jit(solution)/shard_map/chunk_sums/pallas_call | solution.py:238
  54.5 5.1 %chunk_sums.4 = (f32[512,128]{1,0:T(8,128)}, f32[512,128]{1,0:T(8,128)}) custom-call(bf16[1,4,256,2048]{3,2,1,0:T(8,128)(2,1)} %slice.91.factor_ref, f32[4,256,512]{2,1,0:T(8,128)} %own_facet.1.own_ref, f32[1,4,2,512]{3,2,1,0:T(2,128)} %fusion.37.ramp_ref, bf16[1024,128]{1,0:T(8,128)(2,1)} %copy-done.2), custom_call_target="tpu_custom_call" | custom-call | tf_op jit(solution)/shard_map/chunk_sums/pallas_call | solution.py:238
  60.2 0.7 copy-done.1
  60.9 5.1 %chunk_sums.6 = (f32[512,128]{1,0:T(8,128)}, f32[512,128]{1,0:T(8,128)}) custom-call(bf16[1,4,256,2048]{3,2,1,0:T(8,128)(2,1)} %slice.91.factor_ref, f32[4,256,512]{2,1,0:T(8,128)} %own_facet.1.own_ref, f32[1,4,2,512]{3,2,1,0:T(2,128)} %fusion.37.ramp_ref, bf16[1024,128]{1,0:T(8,128)(2,1)} %copy-done.1), custom_call_target="tpu_custom_call" | custom-call | tf_op jit(solution)/shard_map/chunk_sums/pallas_call | solution.py:238
  67.4 5.1 %chunk_sums.7 = (f32[512,128]{1,0:T(8,128)}, f32[512,128]{1,0:T(8,128)}) custom-call(bf16[1,4,256,2048]{3,2,1,0:T(8,128)(2,1)} %slice.91.factor_ref, f32[4,256,512]{2,1,0:T(8,128)} %own_facet.1.own_ref, f32[1,4,2,512]{3,2,1,0:T(2,128)} %fusion.37.ramp_ref, bf16[1024,128]{1,0:T(8,128)(2,1)} %copy-done), custom_call_target="tpu_custom_call" | custom-call | tf_op jit(solution)/shard_map/chunk_sums/pallas_call | solution.py:238
  73.0 2.1 %collective-permute-start.9 = (f32[2,128,128]{2,1,0:T(8,128)S(1)}, f32[2,128,128]{2,1,0:T(8,128)S(1)}, u32[]{:S(2)}, u32[]{:S(2)}) collective-permute-start(f32[2,128,128]{2,1,0:T(8,128)S(1)} %dynamic-slice_bitcast_fusion.2), channel_id=1, source_target_pairs={{0,1},{1,0},{2,3},{3,2},{4,5},{5,4},{6,7},{7,6},{8,9},{9,8},{10,11... | collective-permute-start | bytes 393224 | tf_op jit(solution)/shard_map/ppermute | solution.py:262
  75.4 2.1 %collective-permute-start.16 = (f32[2,128,128]{2,1,0:T(8,128)S(1)}, f32[2,128,128]{2,1,0:T(8,128)S(1)}, u32[]{:S(2)}, u32[]{:S(2)}) collective-permute-start(f32[2,128,128]{2,1,0:T(8,128)S(1)} %dynamic-slice_bitcast_fusion.1), channel_id=1, source_target_pairs={{0,1},{1,0},{2,3},{3,2},{4,5},{5,4},{6,7},{7,6},{8,9},{9,8},{10,11... | collective-permute-start | bytes 393224 | tf_op jit(solution)/shard_map/ppermute | solution.py:262
  77.4 1.0 add.327
  78.6 0.9 collective-permute-done.9
  79.5 3.1 %collective-permute-start.10 = (f32[128,128]{1,0:T(8,128)S(1)}, f32[128,128]{1,0:T(8,128)S(1)}, u32[]{:S(2)}, u32[]{:S(2)}) collective-permute-start(f32[128,128]{1,0:T(8,128)S(1)} %dynamic-slice_bitcast_fusion.6), channel_id=1, source_target_pairs={{0,2},{1,3},{2,0},{3,1},{4,6},{5,7},{6,4},{7,5},{8,10},{9,11},{10,... | collective-permute-start | bytes 196616 | tf_op jit(solution)/shard_map/ppermute | solution.py:262
  83.0 2.4 %collective-permute-start.3 = (f32[128,128]{1,0:T(8,128)S(1)}, f32[128,128]{1,0:T(8,128)S(1)}, u32[]{:S(2)}, u32[]{:S(2)}) collective-permute-start(f32[128,128]{1,0:T(8,128)S(1)} %dynamic-slice_bitcast_fusion.7), channel_id=1, source_target_pairs={{0,2},{1,3},{2,0},{3,1},{4,6},{5,7},{6,4},{7,5},{8,10},{9,11},{10,... | collective-permute-start | bytes 196616 | tf_op jit(solution)/shard_map/ppermute | solution.py:262
  85.4 1.7 %collective-permute-done.16 = f32[2,128,128]{2,1,0:T(8,128)S(1)} collective-permute-done((f32[2,128,128]{2,1,0:T(8,128)S(1)}, f32[2,128,128]{2,1,0:T(8,128)S(1)}, u32[]{:S(2)}, u32[]{:S(2)}) %collective-permute-start.16) | collective-permute-done | bytes 131104 | tf_op jit(solution)/shard_map/ppermute | solution.py:262
  87.2 2.2 %collective-permute-start.17 = (f32[128,128]{1,0:T(8,128)S(1)}, f32[128,128]{1,0:T(8,128)S(1)}, u32[]{:S(2)}, u32[]{:S(2)}) collective-permute-start(f32[128,128]{1,0:T(8,128)S(1)} %dynamic-slice_bitcast_fusion.5), channel_id=1, source_target_pairs={{0,2},{1,3},{2,0},{3,1},{4,6},{5,7},{6,4},{7,5},{8,10},{9,11},{10,... | collective-permute-start | bytes 196616 | tf_op jit(solution)/shard_map/ppermute | solution.py:262
  89.5 1.0 collective-permute-done.23
  90.5 1.0 collective-permute-start.24
  91.5 3.0 %collective-permute-start.13 = (bf16[128,128]{1,0:T(8,128)(2,1)S(1)}, bf16[128,128]{1,0:T(8,128)(2,1)S(1)}, u32[]{:S(2)}, u32[]{:S(2)}) collective-permute-start(bf16[128,128]{1,0:T(8,128)(2,1)S(1)} %fusion.23.refs_4_), channel_id=1, source_target_pairs={{0,3},{1,2},{2,1},{3,0},{4,7},{5,6},{6,5},{7,4},{8,11},{9,10},{10,... | collective-permute-start | bytes 98312 | tf_op jit(solution)/shard_map/ppermute | solution.py:267
  94.5 1.0 collective-permute-start.12
  96.0 1.7 %collective-permute-done.17 = f32[128,128]{1,0:T(8,128)S(1)} collective-permute-done((f32[128,128]{1,0:T(8,128)S(1)}, f32[128,128]{1,0:T(8,128)S(1)}, u32[]{:S(2)}, u32[]{:S(2)}) %collective-permute-start.17) | collective-permute-done | bytes 65568 | tf_op jit(solution)/shard_map/ppermute | solution.py:262
  97.7 2.1 %collective-permute-start.6 = (bf16[128,128]{1,0:T(8,128)(2,1)S(1)}, bf16[128,128]{1,0:T(8,128)(2,1)S(1)}, u32[]{:S(2)}, u32[]{:S(2)}) collective-permute-start(bf16[128,128]{1,0:T(8,128)(2,1)S(1)} %fusion.24.refs_0_), channel_id=1, source_target_pairs={{0,3},{1,2},{2,1},{3,0},{4,7},{5,6},{6,5},{7,4},{8,11},{9,10},{10,... | collective-permute-start | bytes 98312 | tf_op jit(solution)/shard_map/ppermute | solution.py:267
  100.0 2.6 %collective-permute-start.4 = (bf16[128,128]{1,0:T(8,128)(2,1)S(1)}, bf16[128,128]{1,0:T(8,128)(2,1)S(1)}, u32[]{:S(2)}, u32[]{:S(2)}) collective-permute-start(bf16[128,128]{1,0:T(8,128)(2,1)S(1)} %fusion.24.refs_0_), channel_id=1, source_target_pairs={{0,1},{1,0},{2,3},{3,2},{4,5},{5,4},{6,7},{7,6},{8,9},{9,8},{10,11... | collective-permute-start | bytes 98312 | tf_op jit(solution)/shard_map/ppermute | solution.py:267
  102.5 1.8 %collective-permute-start.20 = (bf16[128,128]{1,0:T(8,128)(2,1)S(1)}, bf16[128,128]{1,0:T(8,128)(2,1)S(1)}, u32[]{:S(2)}, u32[]{:S(2)}) collective-permute-start(bf16[128,128]{1,0:T(8,128)(2,1)S(1)} %fusion.22.refs_8_), channel_id=1, source_target_pairs={{0,3},{1,2},{2,1},{3,0},{4,7},{5,6},{6,5},{7,4},{8,11},{9,10},{10,... | collective-permute-start | bytes 98312 | tf_op jit(solution)/shard_map/ppermute | solution.py:267
  104.5 2.6 %collective-permute-start.18 = (bf16[128,128]{1,0:T(8,128)(2,1)S(1)}, bf16[128,128]{1,0:T(8,128)(2,1)S(1)}, u32[]{:S(2)}, u32[]{:S(2)}) collective-permute-start(bf16[128,128]{1,0:T(8,128)(2,1)S(1)} %fusion.22.refs_8_), channel_id=1, source_target_pairs={{0,1},{1,0},{2,3},{3,2},{4,5},{5,4},{6,7},{7,6},{8,9},{9,8},{10,11... | collective-permute-start | bytes 98312 | tf_op jit(solution)/shard_map/ppermute | solution.py:267
  107.0 1.8 %collective-permute-start.27 = (bf16[128,128]{1,0:T(8,128)(2,1)S(1)}, bf16[128,128]{1,0:T(8,128)(2,1)S(1)}, u32[]{:S(2)}, u32[]{:S(2)}) collective-permute-start(bf16[128,128]{1,0:T(8,128)(2,1)S(1)} %fusion.21.refs_12_), channel_id=1, source_target_pairs={{0,3},{1,2},{2,1},{3,0},{4,7},{5,6},{6,5},{7,4},{8,11},{9,10},{10,... | collective-permute-start | bytes 98312 | tf_op jit(solution)/shard_map/ppermute | solution.py:267
  108.9 2.6 %collective-permute-start.25 = (bf16[128,128]{1,0:T(8,128)(2,1)S(1)}, bf16[128,128]{1,0:T(8,128)(2,1)S(1)}, u32[]{:S(2)}, u32[]{:S(2)}) collective-permute-start(bf16[128,128]{1,0:T(8,128)(2,1)S(1)} %fusion.21.refs_12_), channel_id=1, source_target_pairs={{0,1},{1,0},{2,3},{3,2},{4,5},{5,4},{6,7},{7,6},{8,9},{9,8},{10,11... | collective-permute-start | bytes 98312 | tf_op jit(solution)/shard_map/ppermute | solution.py:267
  111.4 0.8 maximum_maximum_fusion
  112.9 0.8 collective-permute-done.26.refs_14_
  114.3 6.9 %degrid.1 = f32[2,2,2048]{2,1,0:T(2,128)} custom-call(s32[2,2]{1,0:T(2,128)} %stack.13.pick_ref, f32[2,8]{1,0:T(2,128)} %broadcast_divide_fusion.coltap_ref, bf16[2,256,256]{2,1,0:T(8,128)(2,1)} %select_convert_fusion.rowmat_ref, s32[2,2,2048]{2,1,0:T(2,128)} %cells_ref.1, bf16[512,512]{1,0:T(8,128)(2,1)} %bitcast.67, bf16[128,128]{1,0:T(8,128)(2,1)} %copy-done.9, ...), custom_call_target="tpu_custom_call" | custom-call | tf_op jit(solution)/shard_map/degrid/pallas_call | solution.py:286
  (136 shorter events, 12.5 us)
Async XLA Ops:
  0.0 14.6 %copy-start.25 = (s32[2,2]{1,0:T(2,128)S(1)}, s32[2,2]{1,0:T(2,128)}, u32[]{:S(2)}) copy-start(s32[2,2]{1,0:T(2,128)} %param.8) | copy-start | bytes 52
  0.0 16.5 %copy-start.24 = (s32[8,4,2]{0,2,1:T(2,128)S(1)}, s32[8,4,2]{0,2,1:T(2,128)}, u32[]{:S(2)}) copy-start(s32[8,4,2]{0,2,1:T(2,128)} %param.6) | copy-start | bytes 772
  2.9 51.0 %collective-permute-start = (bf16[1024,128]{1,0:T(8,128)(2,1)}, bf16[1024,128]{1,0:T(8,128)(2,1)S(1)}, u32[]{:S(2)}, u32[]{:S(2)}) collective-permute-start(bf16[1024,128]{1,0:T(8,128)(2,1)} %pad_maximum_fusion), channel_id=1, source_target_pairs={{0,8},{4,12},{8,0},{12,4},{1,9},{5,13},{9,1},{13,5},{2,10},{6,14},... | collective-permute-start | bytes 786440 | tf_op jit(solution)/shard_map/ppermute | solution.py:178
  6.7 41.8 %collective-permute-start.7 = (bf16[1024,128]{1,0:T(8,128)(2,1)}, bf16[1024,128]{1,0:T(8,128)(2,1)}, u32[]{:S(2)}, u32[]{:S(2)}) collective-permute-start(bf16[1024,128]{1,0:T(8,128)(2,1)} %pad_maximum_fusion.1), channel_id=1, source_target_pairs={{0,8},{4,12},{8,0},{12,4},{1,9},{5,13},{9,1},{13,5},{2,10},{6,14},... | collective-permute-start | bytes 786440 | tf_op jit(solution)/shard_map/ppermute | solution.py:178
  7.6 52.6 %collective-permute-start.14 = (bf16[1024,128]{1,0:T(8,128)(2,1)}, bf16[1024,128]{1,0:T(8,128)(2,1)S(1)}, u32[]{:S(2)}, u32[]{:S(2)}) collective-permute-start(bf16[1024,128]{1,0:T(8,128)(2,1)} %pad_maximum_fusion.2), channel_id=1, source_target_pairs={{0,8},{4,12},{8,0},{12,4},{1,9},{5,13},{9,1},{13,5},{2,10},{6,14},... | collective-permute-start | bytes 786440 | tf_op jit(solution)/shard_map/ppermute | solution.py:178
  9.8 56.9 %collective-permute-start.21 = (bf16[1024,128]{1,0:T(8,128)(2,1)S(1)}, bf16[1024,128]{1,0:T(8,128)(2,1)S(1)}, u32[]{:S(2)}, u32[]{:S(2)}) collective-permute-start(bf16[1024,128]{1,0:T(8,128)(2,1)S(1)} %pad_maximum_fusion.3), channel_id=1, source_target_pairs={{0,8},{4,12},{8,0},{12,4},{1,9},{5,13},{9,1},{13,5},{2,10},{6,14},... | collective-permute-start | bytes 786440 | tf_op jit(solution)/shard_map/ppermute | solution.py:178
  22.2 4.3 %copy-start.6 = (f32[2,4,1,512]{3,2,1,0:T(1,128)}, f32[2,4,1,512]{3,2,1,0:T(1,128)S(1)}, u32[]{:S(2)}) copy-start(f32[2,4,1,512]{3,2,1,0:T(1,128)S(1)} %get-tuple-element.50) | copy-start | bytes 49156
  41.0 6.9 %copy-start.7 = (f32[2,4,1,512]{3,2,1,0:T(1,128)S(1)}, f32[2,4,1,512]{3,2,1,0:T(1,128)}, u32[]{:S(2)}) copy-start(f32[2,4,1,512]{3,2,1,0:T(1,128)} %copy-done.6) | copy-start | bytes 49156
  47.9 5.7 %copy-start.26 = (f32[2]{0:T(128)S(1)}, f32[2]{0:T(128)}, u32[]{:S(2)}) copy-start(f32[2]{0:T(128)} %get-tuple-element.22) | copy-start | bytes 28
  53.6 19.3 %collective-permute-start.8 = (f32[512,128]{1,0:T(8,128)}, f32[512,128]{1,0:T(8,128)S(1)}, u32[]{:S(2)}, u32[]{:S(2)}) collective-permute-start(f32[512,128]{1,0:T(8,128)} %get-tuple-element.16), channel_id=1, source_target_pairs={{0,4},{4,0},{8,12},{12,8},{1,5},{5,1},{9,13},{13,9},{2,6},{6,2},{1... | collective-permute-start | bytes 786440 | tf_op jit(solution)/shard_map/ppermute | solution.py:254
  59.6 15.5 %collective-permute-start.1 = (f32[512,128]{1,0:T(8,128)}, f32[512,128]{1,0:T(8,128)S(1)}, u32[]{:S(2)}, u32[]{:S(2)}) collective-permute-start(f32[512,128]{1,0:T(8,128)} %get-tuple-element.14), channel_id=1, source_target_pairs={{0,4},{4,0},{8,12},{12,8},{1,5},{5,1},{9,13},{13,9},{2,6},{6,2},{1... | collective-permute-start | bytes 786440 | tf_op jit(solution)/shard_map/ppermute | solution.py:254
  66.0 7.0 %copy-start.3 = (f32[512,128]{1,0:T(8,128)S(1)}, f32[512,128]{1,0:T(8,128)}, u32[]{:S(2)}) copy-start(f32[512,128]{1,0:T(8,128)} %get-tuple-element.15) | copy-start | bytes 786436
  66.0 9.2 %copy-start.5 = (f32[512,128]{1,0:T(8,128)S(1)}, f32[512,128]{1,0:T(8,128)}, u32[]{:S(2)}) copy-start(f32[512,128]{1,0:T(8,128)} %get-tuple-element.13) | copy-start | bytes 786436
  66.0 9.4 %collective-permute-start.15 = (f32[512,128]{1,0:T(8,128)}, f32[512,128]{1,0:T(8,128)S(1)}, u32[]{:S(2)}, u32[]{:S(2)}) collective-permute-start(f32[512,128]{1,0:T(8,128)} %get-tuple-element.18), channel_id=1, source_target_pairs={{0,4},{4,0},{8,12},{12,8},{1,5},{5,1},{9,13},{13,9},{2,6},{6,2},{1... | collective-permute-start | bytes 786440 | tf_op jit(solution)/shard_map/ppermute | solution.py:254
  66.7 8.7 %copy-start.4 = (f32[512,128]{1,0:T(8,128)S(1)}, f32[512,128]{1,0:T(8,128)}, u32[]{:S(2)}) copy-start(f32[512,128]{1,0:T(8,128)} %get-tuple-element.17) | copy-start | bytes 786436
  72.5 39.8 %copy-start.27 = (s32[2]{0:T(128)S(1)}, s32[2]{0:T(128)}, u32[]{:S(2)}) copy-start(s32[2]{0:T(128)} %param.7) | copy-start | bytes 28
  72.5 5.0 %collective-permute-start.22 = (f32[512,128]{1,0:T(8,128)}, f32[512,128]{1,0:T(8,128)S(1)}, u32[]{:S(2)}, u32[]{:S(2)}) collective-permute-start(f32[512,128]{1,0:T(8,128)} %get-tuple-element.20), channel_id=1, source_target_pairs={{0,4},{4,0},{8,12},{12,8},{1,5},{5,1},{9,13},{13,9},{2,6},{6,2},{1... | collective-permute-start | bytes 786440 | tf_op jit(solution)/shard_map/ppermute | solution.py:254
  73.0 6.4 %collective-permute-start.9 = (f32[2,128,128]{2,1,0:T(8,128)S(1)}, f32[2,128,128]{2,1,0:T(8,128)S(1)}, u32[]{:S(2)}, u32[]{:S(2)}) collective-permute-start(f32[2,128,128]{2,1,0:T(8,128)S(1)} %dynamic-slice_bitcast_fusion.2), channel_id=1, source_target_pairs={{0,1},{1,0},{2,3},{3,2},{4,5},{5,4},{6,7},{7,6},{8,9},{9,8},{10,11... | collective-permute-start | bytes 393224 | tf_op jit(solution)/shard_map/ppermute | solution.py:262
  75.2 7.7 %collective-permute-start.2 = (f32[2,128,128]{2,1,0:T(8,128)S(1)}, f32[2,128,128]{2,1,0:T(8,128)S(1)}, u32[]{:S(2)}, u32[]{:S(2)}) collective-permute-start(f32[2,128,128]{2,1,0:T(8,128)S(1)} %dynamic-slice_bitcast_fusion.3), channel_id=1, source_target_pairs={{0,1},{1,0},{2,3},{3,2},{4,5},{5,4},{6,7},{7,6},{8,9},{9,8},{10,11... | collective-permute-start | bytes 393224 | tf_op jit(solution)/shard_map/ppermute | solution.py:262
  75.4 11.8 %collective-permute-start.16 = (f32[2,128,128]{2,1,0:T(8,128)S(1)}, f32[2,128,128]{2,1,0:T(8,128)S(1)}, u32[]{:S(2)}, u32[]{:S(2)}) collective-permute-start(f32[2,128,128]{2,1,0:T(8,128)S(1)} %dynamic-slice_bitcast_fusion.1), channel_id=1, source_target_pairs={{0,1},{1,0},{2,3},{3,2},{4,5},{5,4},{6,7},{7,6},{8,9},{9,8},{10,11... | collective-permute-start | bytes 393224 | tf_op jit(solution)/shard_map/ppermute | solution.py:262
  78.5 12.0 %collective-permute-start.23 = (f32[2,128,128]{2,1,0:T(8,128)S(1)}, f32[2,128,128]{2,1,0:T(8,128)S(1)}, u32[]{:S(2)}, u32[]{:S(2)}) collective-permute-start(f32[2,128,128]{2,1,0:T(8,128)S(1)} %dynamic-slice_bitcast_fusion), channel_id=1, source_target_pairs={{0,1},{1,0},{2,3},{3,2},{4,5},{5,4},{6,7},{7,6},{8,9},{9,8},{10,11... | collective-permute-start | bytes 393224 | tf_op jit(solution)/shard_map/ppermute | solution.py:262
  79.5 12.0 %collective-permute-start.10 = (f32[128,128]{1,0:T(8,128)S(1)}, f32[128,128]{1,0:T(8,128)S(1)}, u32[]{:S(2)}, u32[]{:S(2)}) collective-permute-start(f32[128,128]{1,0:T(8,128)S(1)} %dynamic-slice_bitcast_fusion.6), channel_id=1, source_target_pairs={{0,2},{1,3},{2,0},{3,1},{4,6},{5,7},{6,4},{7,5},{8,10},{9,11},{10,... | collective-permute-start | bytes 196616 | tf_op jit(solution)/shard_map/ppermute | solution.py:262
  83.0 12.5 %collective-permute-start.3 = (f32[128,128]{1,0:T(8,128)S(1)}, f32[128,128]{1,0:T(8,128)S(1)}, u32[]{:S(2)}, u32[]{:S(2)}) collective-permute-start(f32[128,128]{1,0:T(8,128)S(1)} %dynamic-slice_bitcast_fusion.7), channel_id=1, source_target_pairs={{0,2},{1,3},{2,0},{3,1},{4,6},{5,7},{6,4},{7,5},{8,10},{9,11},{10,... | collective-permute-start | bytes 196616 | tf_op jit(solution)/shard_map/ppermute | solution.py:262
  87.2 10.5 %collective-permute-start.17 = (f32[128,128]{1,0:T(8,128)S(1)}, f32[128,128]{1,0:T(8,128)S(1)}, u32[]{:S(2)}, u32[]{:S(2)}) collective-permute-start(f32[128,128]{1,0:T(8,128)S(1)} %dynamic-slice_bitcast_fusion.5), channel_id=1, source_target_pairs={{0,2},{1,3},{2,0},{3,1},{4,6},{5,7},{6,4},{7,5},{8,10},{9,11},{10,... | collective-permute-start | bytes 196616 | tf_op jit(solution)/shard_map/ppermute | solution.py:262
  90.5 9.4 %collective-permute-start.24 = (f32[128,128]{1,0:T(8,128)S(1)}, f32[128,128]{1,0:T(8,128)S(1)}, u32[]{:S(2)}, u32[]{:S(2)}) collective-permute-start(f32[128,128]{1,0:T(8,128)S(1)} %dynamic-slice_bitcast_fusion.4), channel_id=1, source_target_pairs={{0,2},{1,3},{2,0},{3,1},{4,6},{5,7},{6,4},{7,5},{8,10},{9,11},{10,... | collective-permute-start | bytes 196616 | tf_op jit(solution)/shard_map/ppermute | solution.py:262
  91.5 22.2 %copy-start.8 = (bf16[128,128]{1,0:T(8,128)(2,1)}, bf16[128,128]{1,0:T(8,128)(2,1)S(1)}, u32[]{:S(2)}) copy-start(bf16[128,128]{1,0:T(8,128)(2,1)S(1)} %fusion.23.refs_4_) | copy-start | bytes 98308
  91.5 8.4 %collective-permute-start.13 = (bf16[128,128]{1,0:T(8,128)(2,1)S(1)}, bf16[128,128]{1,0:T(8,128)(2,1)S(1)}, u32[]{:S(2)}, u32[]{:S(2)}) collective-permute-start(bf16[128,128]{1,0:T(8,128)(2,1)S(1)} %fusion.23.refs_4_), channel_id=1, source_target_pairs={{0,3},{1,2},{2,1},{3,0},{4,7},{5,6},{6,5},{7,4},{8,11},{9,10},{10,... | collective-permute-start | bytes 98312 | tf_op jit(solution)/shard_map/ppermute | solution.py:267
  94.5 8.0 %collective-permute-start.12 = (bf16[128,128]{1,0:T(8,128)(2,1)S(1)}, bf16[128,128]{1,0:T(8,128)(2,1)S(1)}, u32[]{:S(2)}, u32[]{:S(2)}) collective-permute-start(bf16[128,128]{1,0:T(8,128)(2,1)S(1)} %fusion.23.refs_4_), channel_id=1, source_target_pairs={{0,2},{1,3},{2,0},{3,1},{4,6},{5,7},{6,4},{7,5},{8,10},{9,11},{10,... | collective-permute-start | bytes 98312 | tf_op jit(solution)/shard_map/ppermute | solution.py:267
  95.5 8.8 %collective-permute-start.11 = (bf16[128,128]{1,0:T(8,128)(2,1)S(1)}, bf16[128,128]{1,0:T(8,128)(2,1)S(1)}, u32[]{:S(2)}, u32[]{:S(2)}) collective-permute-start(bf16[128,128]{1,0:T(8,128)(2,1)S(1)} %fusion.23.refs_4_), channel_id=1, source_target_pairs={{0,1},{1,0},{2,3},{3,2},{4,5},{5,4},{6,7},{7,6},{8,9},{9,8},{10,11... | collective-permute-start | bytes 98312 | tf_op jit(solution)/shard_map/ppermute | solution.py:267
  96.0 17.7 %copy-start.9 = (bf16[128,128]{1,0:T(8,128)(2,1)}, bf16[128,128]{1,0:T(8,128)(2,1)S(1)}, u32[]{:S(2)}) copy-start(bf16[128,128]{1,0:T(8,128)(2,1)S(1)} %fusion.24.refs_0_) | copy-start | bytes 98308
  97.7 6.8 %collective-permute-start.6 = (bf16[128,128]{1,0:T(8,128)(2,1)S(1)}, bf16[128,128]{1,0:T(8,128)(2,1)S(1)}, u32[]{:S(2)}, u32[]{:S(2)}) collective-permute-start(bf16[128,128]{1,0:T(8,128)(2,1)S(1)} %fusion.24.refs_0_), channel_id=1, source_target_pairs={{0,3},{1,2},{2,1},{3,0},{4,7},{5,6},{6,5},{7,4},{8,11},{9,10},{10,... | collective-permute-start | bytes 98312 | tf_op jit(solution)/shard_map/ppermute | solution.py:267
  99.8 13.9 %copy-start.10 = (bf16[128,128]{1,0:T(8,128)(2,1)}, bf16[128,128]{1,0:T(8,128)(2,1)S(1)}, u32[]{:S(2)}) copy-start(bf16[128,128]{1,0:T(8,128)(2,1)S(1)} %fusion.22.refs_8_) | copy-start | bytes 98308
  99.9 7.2 %collective-permute-start.5 = (bf16[128,128]{1,0:T(8,128)(2,1)S(1)}, bf16[128,128]{1,0:T(8,128)(2,1)S(1)}, u32[]{:S(2)}, u32[]{:S(2)}) collective-permute-start(bf16[128,128]{1,0:T(8,128)(2,1)S(1)} %fusion.24.refs_0_), channel_id=1, source_target_pairs={{0,2},{1,3},{2,0},{3,1},{4,6},{5,7},{6,4},{7,5},{8,10},{9,11},{10,... | collective-permute-start | bytes 98312 | tf_op jit(solution)/shard_map/ppermute | solution.py:267
  100.0 13.8 %copy-start.12 = (bf16[128,128]{1,0:T(8,128)(2,1)}, bf16[128,128]{1,0:T(8,128)(2,1)S(1)}, u32[]{:S(2)}) copy-start(bf16[128,128]{1,0:T(8,128)(2,1)S(1)} %collective-permute-done.13.refs_7_) | copy-start | bytes 98308
  100.0 8.9 %collective-permute-start.4 = (bf16[128,128]{1,0:T(8,128)(2,1)S(1)}, bf16[128,128]{1,0:T(8,128)(2,1)S(1)}, u32[]{:S(2)}, u32[]{:S(2)}) collective-permute-start(bf16[128,128]{1,0:T(8,128)(2,1)S(1)} %fusion.24.refs_0_), channel_id=1, source_target_pairs={{0,1},{1,0},{2,3},{3,2},{4,5},{5,4},{6,7},{7,6},{8,9},{9,8},{10,11... | collective-permute-start | bytes 98312 | tf_op jit(solution)/shard_map/ppermute | solution.py:267
  102.5 11.2 %copy-start.13 = (bf16[128,128]{1,0:T(8,128)(2,1)}, bf16[128,128]{1,0:T(8,128)(2,1)S(1)}, u32[]{:S(2)}) copy-start(bf16[128,128]{1,0:T(8,128)(2,1)S(1)} %collective-permute-done.12.refs_6_) | copy-start | bytes 98308
  102.5 6.3 %collective-permute-start.20 = (bf16[128,128]{1,0:T(8,128)(2,1)S(1)}, bf16[128,128]{1,0:T(8,128)(2,1)S(1)}, u32[]{:S(2)}, u32[]{:S(2)}) collective-permute-start(bf16[128,128]{1,0:T(8,128)(2,1)S(1)} %fusion.22.refs_8_), channel_id=1, source_target_pairs={{0,3},{1,2},{2,1},{3,0},{4,7},{5,6},{6,5},{7,4},{8,11},{9,10},{10,... | collective-permute-start | bytes 98312 | tf_op jit(solution)/shard_map/ppermute | solution.py:267
  104.3 9.4 %copy-start.11 = (bf16[128,128]{1,0:T(8,128)(2,1)}, bf16[128,128]{1,0:T(8,128)(2,1)S(1)}, u32[]{:S(2)}) copy-start(bf16[128,128]{1,0:T(8,128)(2,1)S(1)} %fusion.21.refs_12_) | copy-start | bytes 98308
  104.4 9.4 %copy-start.14 = (bf16[128,128]{1,0:T(8,128)(2,1)}, bf16[128,128]{1,0:T(8,128)(2,1)S(1)}, u32[]{:S(2)}) copy-start(bf16[128,128]{1,0:T(8,128)(2,1)S(1)} %collective-permute-done.11.refs_5_) | copy-start | bytes 98308
  104.4 8.5 %collective-permute-start.19 = (bf16[128,128]{1,0:T(8,128)(2,1)S(1)}, bf16[128,128]{1,0:T(8,128)(2,1)S(1)}, u32[]{:S(2)}, u32[]{:S(2)}) collective-permute-start(bf16[128,128]{1,0:T(8,128)(2,1)S(1)} %fusion.22.refs_8_), channel_id=1, source_target_pairs={{0,2},{1,3},{2,0},{3,1},{4,6},{5,7},{6,4},{7,5},{8,10},{9,11},{10,... | collective-permute-start | bytes 98312 | tf_op jit(solution)/shard_map/ppermute | solution.py:267
  104.5 9.3 %copy-start.15 = (bf16[128,128]{1,0:T(8,128)(2,1)}, bf16[128,128]{1,0:T(8,128)(2,1)S(1)}, u32[]{:S(2)}) copy-start(bf16[128,128]{1,0:T(8,128)(2,1)S(1)} %collective-permute-done.6.refs_3_) | copy-start | bytes 98308
  104.5 8.4 %collective-permute-start.18 = (bf16[128,128]{1,0:T(8,128)(2,1)S(1)}, bf16[128,128]{1,0:T(8,128)(2,1)S(1)}, u32[]{:S(2)}, u32[]{:S(2)}) collective-permute-start(bf16[128,128]{1,0:T(8,128)(2,1)S(1)} %fusion.22.refs_8_), channel_id=1, source_target_pairs={{0,1},{1,0},{2,3},{3,2},{4,5},{5,4},{6,7},{7,6},{8,9},{9,8},{10,11... | collective-permute-start | bytes 98312 | tf_op jit(solution)/shard_map/ppermute | solution.py:267
  107.0 6.7 %copy-start.16 = (bf16[128,128]{1,0:T(8,128)(2,1)}, bf16[128,128]{1,0:T(8,128)(2,1)S(1)}, u32[]{:S(2)}) copy-start(bf16[128,128]{1,0:T(8,128)(2,1)S(1)} %collective-permute-done.5.refs_2_) | copy-start | bytes 98308
  107.0 5.8 %collective-permute-start.27 = (bf16[128,128]{1,0:T(8,128)(2,1)S(1)}, bf16[128,128]{1,0:T(8,128)(2,1)S(1)}, u32[]{:S(2)}, u32[]{:S(2)}) collective-permute-start(bf16[128,128]{1,0:T(8,128)(2,1)S(1)} %fusion.21.refs_12_), channel_id=1, source_target_pairs={{0,3},{1,2},{2,1},{3,0},{4,7},{5,6},{6,5},{7,4},{8,11},{9,10},{10,... | collective-permute-start | bytes 98312 | tf_op jit(solution)/shard_map/ppermute | solution.py:267
  108.8 4.9 %copy-start.17 = (bf16[128,128]{1,0:T(8,128)(2,1)}, bf16[128,128]{1,0:T(8,128)(2,1)S(1)}, u32[]{:S(2)}) copy-start(bf16[128,128]{1,0:T(8,128)(2,1)S(1)} %collective-permute-done.4.refs_1_) | copy-start | bytes 98308
  108.8 4.8 %collective-permute-start.26 = (bf16[128,128]{1,0:T(8,128)(2,1)S(1)}, bf16[128,128]{1,0:T(8,128)(2,1)S(1)}, u32[]{:S(2)}, u32[]{:S(2)}) collective-permute-start(bf16[128,128]{1,0:T(8,128)(2,1)S(1)} %fusion.21.refs_12_), channel_id=1, source_target_pairs={{0,2},{1,3},{2,0},{3,1},{4,6},{5,7},{6,4},{7,5},{8,10},{9,11},{10,... | collective-permute-start | bytes 98312 | tf_op jit(solution)/shard_map/ppermute | solution.py:267
  108.9 4.9 %copy-start.18 = (bf16[128,128]{1,0:T(8,128)(2,1)}, bf16[128,128]{1,0:T(8,128)(2,1)S(1)}, u32[]{:S(2)}) copy-start(bf16[128,128]{1,0:T(8,128)(2,1)S(1)} %collective-permute-done.20.refs_11_) | copy-start | bytes 98308
  108.9 4.8 %collective-permute-start.25 = (bf16[128,128]{1,0:T(8,128)(2,1)S(1)}, bf16[128,128]{1,0:T(8,128)(2,1)S(1)}, u32[]{:S(2)}, u32[]{:S(2)}) collective-permute-start(bf16[128,128]{1,0:T(8,128)(2,1)S(1)} %fusion.21.refs_12_), channel_id=1, source_target_pairs={{0,1},{1,0},{2,3},{3,2},{4,5},{5,4},{6,7},{7,6},{8,9},{9,8},{10,11... | collective-permute-start | bytes 98312 | tf_op jit(solution)/shard_map/ppermute | solution.py:267
  (8 other events, 6.1 us)

commit v2 on v0

v2 whole, which is shorter than its diff:
```python
import functools
import math

import jax
import jax.numpy as jnp
import ml_dtypes
import numpy as np
from jax import lax
from jax.experimental import pallas as pl
from jax.experimental.pallas import tpu as pltpu
from jax.sharding import PartitionSpec as P

L = 4096
SUBW = 256
NVIS = 2048
SUPPORT = 8
OVERSAMPLE = 16
SG_WIDE = 2
SHOWN = 2 * SG_WIDE
CHUNKS = 2
CW = SUBW // CHUNKS
LANES = 2 * CW
FINE = 16
VMEM_LIMIT = 56 << 20

TURN = float(np.float32(2.0 * math.pi / L))
TURN_HIGH = float(np.float32(np.round(2.0 * math.pi / L * 2**20) / 2**20))
TURN_LOW = 2.0 * math.pi / L - TURN_HIGH


def kernel_taps(fraction):
    points = jnp.arange(SUPPORT, dtype=jnp.float32)
    centre = (SUPPORT - 1) / 2.0 + (fraction.astype(jnp.float32) + 0.5) / OVERSAMPLE - 0.5
    distance = points[None, :] - centre[:, None]
    values = jnp.exp(-distance * distance / 2.88)
    return values / jnp.sum(values, axis=-1, keepdims=True)


def table_chunked():
    grid_ids = np.arange(SUBW)
    phase = 2.0 * math.pi / SUBW * (grid_ids[:, None] * grid_ids[None, :] % SUBW)
    cosine = np.cos(phase) / math.sqrt(SUBW)
    sine = np.sin(phase) / math.sqrt(SUBW)
    upper = np.concatenate([cosine, -sine], axis=1).reshape(CHUNKS, 1, CW, 2 * SUBW)
    lower = np.concatenate([sine, cosine], axis=1).reshape(CHUNKS, 1, CW, 2 * SUBW)
    both = np.concatenate([upper, lower], axis=1).reshape(2 * SUBW, 2 * SUBW)
    return jnp.asarray(both.astype(np.float32).astype(ml_dtypes.bfloat16))


def cos_sin(number):
    quarter = lax.shift_right_logical(number + L // 8, int(math.log2(L // 4)))
    angle = (number - quarter * (L // 4)).astype(jnp.float32) * TURN
    square = angle * angle
    sine = 1.0 / 362880
    for term in (-1.0 / 5040, 1.0 / 120, -1.0 / 6, 1.0):
        sine = sine * square + term
    sine = sine * angle
    cosine = -1.0 / 3628800
    for term in (1.0 / 40320, -1.0 / 720, 1.0 / 24, -0.5, 1.0):
        cosine = cosine * square + term
    odd = (quarter & 1) == 1
    first = jnp.where(odd, sine, cosine)
    second = jnp.where(odd, cosine, sine)
    first = jnp.where(((quarter + 1) & 2) == 2, -first, first)
    second = jnp.where((quarter & 2) == 2, -second, second)
    return first, second


def ramp_of(shift):
    lane = lax.broadcasted_iota(jnp.int32, (1, 2 * SUBW), 1)
    column = lane // LANES * CW + lane % CW
    cosine, sine = cos_sin((shift * column) % SUBW * (L // SUBW))
    return cosine, jnp.where(lane % LANES < CW, sine, -sine)


def swap_halves(value):
    return jnp.concatenate([value[:, CW:], value[:, :CW]], axis=1)


def ramped(direct, crossed, cosine, sine):
    part = direct + jnp.concatenate([crossed[:, CW:], -crossed[:, :CW]], axis=1)
    return part * cosine + swap_halves(part) * sine


def prep_kernel(chips, shift_ref, place_ref, strips_ref, rest_ref, own_ref, fine, fine_at, base, base_at, held):
    length = strips_ref.shape[1]
    row_ids = place_ref[0] + lax.broadcasted_iota(jnp.int32, (FINE, length), 1)
    group = lax.broadcasted_iota(jnp.int32, (FINE, length), 0)
    centred = (2 * row_ids + 1).astype(jnp.float32) / L - 1.0
    taper = (1.0 - 0.5 * centred * centred) / math.sqrt(L)
    number = (group * row_ids) & (L - 1)
    fine_at[...] = number
    cosine, sine = cos_sin(number)
    fine[0] = cosine
    fine[1] = sine

    def make_factor(facet, shown, store):
        shift = shift_ref[facet, shown, 0] + (L - SUBW // 2)
        number = ((shift + FINE * group) * row_ids) & (L - 1)
        base_at[...] = number
        cosine, sine = cos_sin(number)
        base[0] = cosine * taper
        base[1] = sine * taper

        def one_group(high, carry):
            at = (base_at[pl.ds(high, 1), :] + fine_at[...]) & (L - 1)
            count = at.astype(jnp.float32)
            turned = count * TURN
            slip = (turned - count * TURN_HIGH) - count * TURN_LOW
            base_c = base[0, pl.ds(high, 1), :]
            base_s = base[1, pl.ds(high, 1), :]
            cosine = base_c * fine[0] - base_s * fine[1]
            sine = base_s * fine[0] + base_c * fine[1]
            rows = pl.ds(pl.multiple_of(high * FINE, FINE), FINE)
            store(
                rows,
                (cosine - slip * sine).astype(jnp.bfloat16),
                (sine + slip * cosine).astype(jnp.bfloat16),
            )
            return carry

        lax.fori_loop(0, SUBW // FINE, one_group, 0, unroll=2)

    def own_step(shown, carry):
        def store(rows, cosine, sine):
            held[rows, :length] = cosine
            held[rows, length:] = sine

        make_factor(0, shown, store)
        ramp_c, ramp_s = ramp_of(shift_ref[0, shown, 1])
        for chunk in range(CHUNKS):
            columns = slice(chunk * CW, (chunk + 1) * CW)
            lanes = slice(chunk * LANES, (chunk + 1) * LANES)
            data = jnp.concatenate([strips_ref[0, :, columns], strips_ref[1, :, columns]], axis=1)
            direct = jnp.dot(held[:, :length], data, preferred_element_type=jnp.float32)
            crossed = jnp.dot(held[:, length:], data, preferred_element_type=jnp.float32)
            own_ref[chunk, shown] = ramped(direct, crossed, ramp_c[:, lanes], ramp_s[:, lanes])
        return carry

    lax.fori_loop(0, SHOWN, own_step, 0)

    def rest_step(step, carry):
        facet = step // SHOWN
        shown = step % SHOWN

        def store(rows, cosine, sine):
            rest_ref[facet, shown, rows, :length] = cosine
            rest_ref[facet, shown, rows, length:] = sine

        make_factor(facet + 1, shown, store)
        return carry

    lax.fori_loop(0, (chips - 1) * SHOWN, rest_step, 0)


def chunk_kernel(chunk, shift_ref, rest_ref, own_ref, *refs):
    hops = len(refs) - 2
    keep_ref, send_ref = refs[hops:]
    lanes = slice(chunk * LANES, (chunk + 1) * LANES)
    length = refs[0].shape[1]
    for shown in range(SHOWN):
        total = own_ref[chunk, shown]
        for hop in range(hops):
            data = jnp.concatenate([refs[hop][0], refs[hop][1]], axis=1)
            ramp_c, ramp_s = ramp_of(shift_ref[hop + 1, shown, 1])
            direct = jnp.dot(
                rest_ref[hop, shown, :, :length], data, preferred_element_type=jnp.float32
            )
            crossed = jnp.dot(
                rest_ref[hop, shown, :, length:], data, preferred_element_type=jnp.float32
            )
            total = total + ramped(direct, crossed, ramp_c[:, lanes], ramp_s[:, lanes])
        target = keep_ref if shown < SG_WIDE else send_ref
        first = shown % SG_WIDE * SUBW
        target[first : first + SUBW, :] = total


def degrid_kernel(pairs, pick_ref, rowtap_ref, coltap_ref, cells_ref, table_ref, *refs):
    count = CHUNKS * pairs
    pieces = refs[:count]
    out_ref, held, tall = refs[count:]
    blocks = cells_ref.shape[0]
    rows_dev = pieces[0].shape[0]
    place = pick_ref[1, 0]
    for chunk in range(CHUNKS):
        for step in range(pairs):
            at = pl.multiple_of((place ^ step) * rows_dev, rows_dev)
            held[pl.ds(at, rows_dev), chunk * LANES : (chunk + 1) * LANES] = pieces[
                chunk * pairs + step
            ][...]
    tall[2 * SUBW :, :] = jnp.zeros((SUPPORT, SUBW), jnp.float32)
    ids = lax.broadcasted_iota(jnp.int32, (SUBW, SUBW), 0)
    distance = ids - lax.broadcasted_iota(jnp.int32, (SUBW, SUBW), 1)
    width = 512

    for block in range(blocks):
        row_matrix = jnp.zeros((SUBW, SUBW), jnp.float32)
        for tap in range(SUPPORT):
            row_matrix = jnp.where(distance == tap, rowtap_ref[block, tap], row_matrix)
        first = pl.multiple_of(pick_ref[0, block] * SUBW, SUBW)
        subgrid = held[pl.ds(first, SUBW), :]
        spectrum = jnp.dot(subgrid, table_ref[...], preferred_element_type=jnp.float32).astype(
            jnp.bfloat16
        )
        tall[0 : 2 * SUBW, :] = lax.dot_general(
            spectrum,
            row_matrix.astype(jnp.bfloat16),
            (((0,), (0,)), ((), ())),
            preferred_element_type=jnp.float32,
        )
        smooth = coltap_ref[block, 0] * tall[0 : 2 * SUBW, :]
        for tap in range(1, SUPPORT):
            smooth = smooth + coltap_ref[block, tap] * tall[tap : tap + 2 * SUBW, :]
        high = smooth.astype(jnp.bfloat16)
        low = (smooth - high.astype(jnp.float32)).astype(jnp.bfloat16)
        for start in range(0, NVIS, width):
            row_at = cells_ref[block, 0:1, start : start + width]
            col_at = cells_ref[block, 1:2, start : start + width]
            wide_ids = lax.broadcasted_iota(jnp.int32, (SUBW, width), 0)
            chosen = jnp.where(wide_ids == row_at, 1.0, 0.0).astype(jnp.bfloat16)
            picked = jnp.dot(high, chosen, preferred_element_type=jnp.float32) + jnp.dot(
                low, chosen, preferred_element_type=jnp.float32
            )
            hit = wide_ids == col_at
            out_ref[block, 0:1, start : start + width] = jnp.sum(
                jnp.where(hit, picked[:SUBW], 0.0), axis=0, keepdims=True
            )
            out_ref[block, 1:2, start : start + width] = jnp.sum(
                jnp.where(hit, picked[SUBW:], 0.0), axis=0, keepdims=True
            )


def on_device(strips, offsets, block_subgrid, block_kernel, vis_cells):
    pairs = lax.axis_size("pair")
    wides = lax.axis_size("wide")
    chips = wides // 2
    wide_id = lax.axis_index("wide")
    pair_id = lax.axis_index("pair")
    length = strips.shape[2]
    rows_dev = SG_WIDE * SUBW // pairs
    in_smem = pl.BlockSpec(memory_space=pltpu.SMEM)
    in_vmem = pl.BlockSpec(memory_space=pltpu.VMEM)
    params = pltpu.CompilerParams(vmem_limit_bytes=VMEM_LIMIT)

    strips = strips[0]
    arrived = [
        [
            lax.ppermute(
                strips[:, :, i * CW : (i + 1) * CW],
                "wide",
                [(w, (w + 2 * hop) % wides) for w in range(wides)],
            )
            for hop in range(1, chips)
        ]
        for i in range(CHUNKS)
    ]

    facets = (wide_id - 2 * jnp.arange(chips, dtype=jnp.int32)) % wides
    lead = jnp.arange(SG_WIDE, dtype=jnp.int32)
    subgrids = jnp.concatenate([SG_WIDE * wide_id + lead, SG_WIDE * (wide_id ^ 1) + lead])
    shifts = offsets[subgrids[None, :], facets[:, None]]
    place = (pair_id * length).reshape(1)

    rest, own = pl.pallas_call(
        functools.partial(prep_kernel, chips),
        out_shape=[
            jax.ShapeDtypeStruct((chips - 1, SHOWN, SUBW, 2 * length), jnp.bfloat16),
            jax.ShapeDtypeStruct((CHUNKS, SHOWN, SUBW, LANES), jnp.float32),
        ],
        in_specs=[in_smem, in_smem, in_vmem],
        out_specs=[in_vmem, in_vmem],
        scratch_shapes=[
            pltpu.VMEM((2, FINE, length), jnp.float32),
            pltpu.VMEM((FINE, length), jnp.int32),
            pltpu.VMEM((2, FINE, length), jnp.float32),
            pltpu.VMEM((FINE, length), jnp.int32),
            pltpu.VMEM((SUBW, 2 * length), jnp.bfloat16),
        ],
        compiler_params=params,
        name="prepare",
    )(shifts, place, strips)

    def chunk_sums(index):
        return pl.pallas_call(
            functools.partial(chunk_kernel, index),
            out_shape=[jax.ShapeDtypeStruct((SG_WIDE * SUBW, LANES), jnp.float32)] * 2,
            in_specs=[in_smem, in_vmem, in_vmem] + [in_vmem] * (chips - 1),
            out_specs=[in_vmem] * 2,
            compiler_params=params,
            name="chunk_sums",
        )(shifts, rest, own, *arrived[index])

    def reduce_rows(index):
        keep, send = chunk_sums(index)
        total = keep + lax.ppermute(send, "wide", [(w, w ^ 1) for w in range(wides)])
        bits = pairs.bit_length() - 1
        total = total.reshape((2,) * bits + (rows_dev, LANES))
        for bit in range(bits):
            axis = total.ndim - 3
            mine = (pair_id >> bit) & 1
            passed = lax.dynamic_index_in_dim(total, 1 - mine, axis, keepdims=False)
            held = lax.dynamic_index_in_dim(total, mine, axis, keepdims=False)
            total = held + lax.ppermute(
                passed, "pair", [(p, p ^ (1 << bit)) for p in range(pairs)]
            )
        rounded = total.astype(jnp.bfloat16)
        return [rounded] + [
            lax.ppermute(rounded, "pair", [(p, p ^ step) for p in range(pairs)])
            for step in range(1, pairs)
        ]

    pieces = [piece for index in range(CHUNKS) for piece in reduce_rows(index)]

    blocks = vis_cells.shape[0]
    row_taps = kernel_taps(block_kernel[:, 0]).astype(jnp.bfloat16).astype(jnp.float32)
    col_taps = kernel_taps(block_kernel[:, 1])
    picks = jnp.stack([block_subgrid, jnp.full_like(block_subgrid, pair_id)])

    return pl.pallas_call(
        functools.partial(degrid_kernel, pairs),
        out_shape=jax.ShapeDtypeStruct((blocks, 2, NVIS), jnp.float32),
        in_specs=[in_smem] * 3 + [in_vmem] * (2 + len(pieces)),
        out_specs=in_vmem,
        scratch_shapes=[
            pltpu.VMEM((SG_WIDE * SUBW, 2 * SUBW), jnp.bfloat16),
            pltpu.VMEM((2 * SUBW + SUPPORT, SUBW), jnp.float32),
        ],
        compiler_params=params,
        name="degrid",
    )(picks, row_taps, col_taps, vis_cells, table_chunked(), *pieces)


def solution(mesh):
    placed = (
        P(("groups", "wide"), None, "pair", None),
        P("groups", None, None),
        P(("groups", "wide", "pair")),
        P(("groups", "wide", "pair"), None),
        P(("groups", "wide", "pair"), None, None),
    )
    return jax.shard_map(
        on_device,
        mesh=mesh,
        in_specs=placed,
        out_specs=P(("groups", "wide", "pair"), None, None),
        check_vma=False,
    )
```

time: 268 us -> 78.7 us (0.29)
  other arithmetic: 69.1 us -> 2.69 us
  waiting for transfers between devices: 72.2 us -> 18.7 us
  local copies, waits for them, and re-layouts: 48.5 us -> 6.24 us
  matrix products: 35.7 us -> 0 us
  Pallas kernels: 0 us -> 30.8 us
  starting transfers between devices: 0.01 us -> 19.8 us
  blocking collectives: 14.9 us -> 0 us
  between operations: 13.5 us -> 0.21 us
  loops' own time: 12.6 us -> 0 us
    reduce_scatter x1 -> x0, waiting for transfers between devices: 72.2 us -> none  [on_device(): lax.psum_scatter(stacked.reshape(rows_dev * lax.axis_size(('wide', 'pair'...]
    another operation x19 -> x0, other arithmetic: 41.8 us -> none
    dot_general x18 -> x0, matrix products: 35.7 us -> none  [the longest x16 28.4 us: single(): product = jnp.dot(factor, xstack, preferred_element_type=jnp.float32)]
    dynamic_slice x32 -> x0, local copies, waits for them, and re-layouts: 33.3 us -> none  [the longest x16 22.8 us: single(): return column_ramp(product, offsets[subgrid_id, facet_id, 1])]
    pallas_call x0 -> x4, Pallas kernels: none -> 30.8 us  [the longest x1 14.4 us: on_device(): pl.pallas_call(functools.partial(prep_kernel, chips), out_shape=[jax.Shap...]
    ppermute x0 -> x14, starting transfers between devices: none -> 19.8 us  [the longest x6 9.43 us: reduce_rows(): lax.ppermute(rounded, 'pair', [(p, p ^ step) for p in range(pairs)])]
    ppermute x0 -> x14, waiting for transfers between devices: none -> 18.7 us  [the longest x4 15.4 us: reduce_rows(): lax.ppermute(passed, 'pair', [(p, p ^ 1 << bit) for p in range(pairs)])]
    all_gather x1 -> x0, blocking collectives: 14.9 us -> none  [on_device(): portion = lax.all_gather(spectrum, 'pair', axis=0, tiled=True)]
  transfers between devices with their start and end apart: 1 -> 14, of which waited for: 1 -> 6; matrix products, arithmetic and copies ran while one was open for 1% -> 7% of each run, Pallas kernels for 0% -> 31%
where the time goes in v2:
time: 78.7 us; the launch traced here: 78.4 us
  Pallas kernels  30.8 us (39%)
  starting transfers between devices  19.8 us (25%)
  waiting for transfers between devices  18.7 us (24%)
  local copies, waits for them, and re-layouts  6.24 us (8%)
  other arithmetic  2.69 us (3%)
    ppermute x4, waiting for transfers between devices, reduce_rows(): lax.ppermute(passed, 'pair', [(p, p ^ 1 << bit) for p in range(pairs)])  15.4 us
    pallas_call x1, Pallas kernels, on_device(): pl.pallas_call(functools.partial(prep_kernel, chips), out_shape=[jax.Shap...  14.4 us
    pallas_call x2, Pallas kernels, chunk_sums(): pl.pallas_call(functools.partial(chunk_kernel, index), out_shape=[jax.Sha...  10 us
    ppermute x6, starting transfers between devices, reduce_rows(): lax.ppermute(rounded, 'pair', [(p, p ^ step) for p in range(pairs)])  9.43 us
    ppermute x4, starting transfers between devices, reduce_rows(): lax.ppermute(passed, 'pair', [(p, p ^ 1 << bit) for p in range(pairs)])  7.21 us
    pallas_call x1, Pallas kernels, on_device(): pl.pallas_call(functools.partial(degrid_kernel, pairs), out_shape=jax.Sha...  6.4 us
    ppermute x2, starting transfers between devices, on_device(): lax.ppermute(strips[:, :, i * CW:(i + 1) * CW], 'wide', [(w, (w + 2 * hop...  3.11 us
    unnamed x27, local copies, waits for them, and re-layouts  3.04 us
  transfers between devices with their start and end apart: 14, of which 6 were waited for; matrix products, arithmetic and copies ran while one was open for 7% of the time, Pallas kernels for 31%

profile of v2, /device:TPU:0, one launch (start us, length us, event | category | flops | bytes accessed | tf_op | source)
XLA Modules:
  0.0 78.4 jit_solution(9747477947902378475)
XLA Ops:
  0.0 1.3 %fusion.14 = (bf16[2,1024,128]{2,1,0:T(8,128)(2,1)S(1)}, bf16[2,1024,128]{2,1,0:T(8,128)(2,1)S(1)}) fusion(bf16[2,1024,256]{2,1,0:T(8,128)(2,1)} %bitcast.28), kind=kLoop, calls=%fused_computation.37 | loop fusion | bytes 2097152 | tf_op jit(solution)/shard_map/slice | solution.py:249
  1.3 3.0 %collective-permute-start.7 = (bf16[2,1024,128]{2,1,0:T(8,128)(2,1)S(1)}, bf16[2,1024,128]{2,1,0:T(8,128)(2,1)S(1)}, u32[]{:S(2)}, u32[]{:S(2)}) collective-permute-start(bf16[2,1024,128]{2,1,0:T(8,128)(2,1)S(1)} %get-tuple-element.19), channel_id=1, source_target_pairs={{0,8},{4,12},{8,0},{12,4},{1,9},{5,13},{9,1},{13,5},{2,10},{6,14},... | collective-permute-start | bytes 1572872 | tf_op jit(solution)/shard_map/ppermute | solution.py:248
  4.3 0.1 collective-permute-start
  4.4 0.1 fusion.9
  4.5 0.1 broadcast_or_fusion
  4.6 0.1 reshape.55
  4.7 0.8 %copy.7 = s32[8,4,2]{2,1,0:T(4,128)S(1)} copy(s32[8,4,2]{0,2,1:T(2,128)} %param.7) | data formatting | bytes 512 | tf_op args[1]
  5.4 1.2 %gather_fusion = s32[8,2]{1,0:T(8,128)} fusion(s32[8,4,2]{2,1,0:T(4,128)S(1)} %copy.7, s32[8]{0:T(128)S(1)} %reshape.55), kind=kCustom, calls=%fused_computation | custom fusion | bytes 192 | tf_op jit(solution)/shard_map/gather | solution.py:261
  6.6 14.4 %prepare.1 = (bf16[1,4,256,2048]{3,2,1,0:T(8,128)(2,1)}, f32[2,4,256,256]{3,2,1,0:T(8,128)}) custom-call(s32[2,4,2]{2,1,0:T(4,128)} %bitcast.34, s32[1]{0:T(128)} %bitcast.2.place_ref, bf16[2,1024,256]{2,1,0:T(8,128)(2,1)} %bitcast.29), custom_call_target="tpu_custom_call" | custom-call | tf_op jit(solution)/shard_map/prepare/pallas_call | solution.py:264
  21.0 0.0 collective-permute-done.7.refs_0_
  21.0 0.8 %copy-done.1 = bf16[2,1024,128]{2,1,0:T(8,128)(2,1)} copy-done((bf16[2,1024,128]{2,1,0:T(8,128)(2,1)}, bf16[2,1024,128]{2,1,0:T(8,128)(2,1)S(1)}, u32[]{:S(2)}) %copy-start.1) | copy-done | bytes 524312
  21.8 5.0 %chunk_sums.3 = (f32[512,256]{1,0:T(8,128)}, f32[512,256]{1,0:T(8,128)}) custom-call(s32[2,4,2]{2,1,0:T(4,128)} %bitcast.35, bf16[1,4,256,2048]{3,2,1,0:T(8,128)(2,1)} %get-tuple-element.11.rest_ref, f32[2,4,256,256]{3,2,1,0:T(8,128)} %get-tuple-element.12.own_ref, bf16[2,1024,128]{2,1,0:T(8,128)(2,1)} %copy-done.1), custom_call_target="tpu_custom_call" | custom-call | tf_op jit(solution)/shard_map/chunk_sums/pallas_call | solution.py:284
  26.8 0.0 collective-permute-start.8
  26.8 0.7 collective-permute-done.refs_0_
  27.5 0.9 %copy-done = bf16[2,1024,128]{2,1,0:T(8,128)(2,1)} copy-done((bf16[2,1024,128]{2,1,0:T(8,128)(2,1)}, bf16[2,1024,128]{2,1,0:T(8,128)(2,1)S(1)}, u32[]{:S(2)}) %copy-start) | copy-done | bytes 524312
  28.3 5.0 %chunk_sums.2 = (f32[512,256]{1,0:T(8,128)}, f32[512,256]{1,0:T(8,128)}) custom-call(s32[2,4,2]{2,1,0:T(4,128)} %bitcast.36, bf16[1,4,256,2048]{3,2,1,0:T(8,128)(2,1)} %get-tuple-element.11.rest_ref, f32[2,4,256,256]{3,2,1,0:T(8,128)} %get-tuple-element.12.own_ref, bf16[2,1024,128]{2,1,0:T(8,128)(2,1)} %copy-done), custom_call_target="tpu_custom_call" | custom-call | tf_op jit(solution)/shard_map/chunk_sums/pallas_call | solution.py:284
  33.4 0.0 collective-permute-start.1
  33.4 0.2 add_reduce_fusion
  33.6 0.0 collective-permute-done.8
  33.6 0.1 add.113
  33.7 1.9 %collective-permute-start.9 = (f32[2,128,256]{2,1,0:T(8,128)S(1)}, f32[2,128,256]{2,1,0:T(8,128)S(1)}, u32[]{:S(2)}, u32[]{:S(2)}) collective-permute-start(f32[2,128,256]{2,1,0:T(8,128)S(1)} %dynamic-slice_bitcast_fusion), channel_id=1, source_target_pairs={{0,1},{1,0},{2,3},{3,2},{4,5},{5,4},{6,7},{7,6},{8,9},{9,8},{10,11... | collective-permute-start | bytes 786440 | tf_op jit(solution)/shard_map/ppermute | solution.py:303
  35.6 0.2 fusion.12
  35.8 0.2 fusion.13
  36.0 0.0 collective-permute-done.1
  36.0 1.1 %add.106 = f32[512,256]{1,0:T(8,128)S(1)} add(f32[512,256]{1,0:T(8,128)} %get-tuple-element.13, f32[512,256]{1,0:T(8,128)S(1)} %collective-permute-done.1) | non-fusion elementwise | flops 131072 | bytes 1572864 | tf_op jit(solution)/shard_map/add | solution.py:295
  37.1 1.4 %collective-permute-start.2 = (f32[2,128,256]{2,1,0:T(8,128)S(1)}, f32[2,128,256]{2,1,0:T(8,128)S(1)}, u32[]{:S(2)}, u32[]{:S(2)}) collective-permute-start(f32[2,128,256]{2,1,0:T(8,128)S(1)} %dynamic-slice_bitcast_fusion.1), channel_id=1, source_target_pairs={{0,1},{1,0},{2,3},{3,2},{4,5},{5,4},{6,7},{7,6},{8,9},{9,8},{10,11... | collective-permute-start | bytes 786440 | tf_op jit(solution)/shard_map/ppermute | solution.py:303
  38.5 4.4 %collective-permute-done.9 = f32[2,128,256]{2,1,0:T(8,128)S(1)} collective-permute-done((f32[2,128,256]{2,1,0:T(8,128)S(1)}, f32[2,128,256]{2,1,0:T(8,128)S(1)}, u32[]{:S(2)}, u32[]{:S(2)}) %collective-permute-start.9) | collective-permute-done | bytes 262176 | tf_op jit(solution)/shard_map/ppermute | solution.py:303
  42.9 2.9 %collective-permute-start.10 = (f32[128,256]{1,0:T(8,128)S(1)}, f32[128,256]{1,0:T(8,128)S(1)}, u32[]{:S(2)}, u32[]{:S(2)}) collective-permute-start(f32[128,256]{1,0:T(8,128)S(1)} %dynamic-slice_bitcast_fusion.2), channel_id=1, source_target_pairs={{0,2},{1,3},{2,0},{3,1},{4,6},{5,7},{6,4},{7,5},{8,10},{9,11},{10,... | collective-permute-start | bytes 393224 | tf_op jit(solution)/shard_map/ppermute | solution.py:303
  45.8 5.1 %collective-permute-done.2 = f32[2,128,256]{2,1,0:T(8,128)S(1)} collective-permute-done((f32[2,128,256]{2,1,0:T(8,128)S(1)}, f32[2,128,256]{2,1,0:T(8,128)S(1)}, u32[]{:S(2)}, u32[]{:S(2)}) %collective-permute-start.2) | collective-permute-done | bytes 262176 | tf_op jit(solution)/shard_map/ppermute | solution.py:303
  51.0 1.0 %collective-permute-start.3 = (f32[128,256]{1,0:T(8,128)S(1)}, f32[128,256]{1,0:T(8,128)S(1)}, u32[]{:S(2)}, u32[]{:S(2)}) collective-permute-start(f32[128,256]{1,0:T(8,128)S(1)} %dynamic-slice_bitcast_fusion.3), channel_id=1, source_target_pairs={{0,2},{1,3},{2,0},{3,1},{4,6},{5,7},{6,4},{7,5},{8,10},{9,11},{10,... | collective-permute-start | bytes 393224 | tf_op jit(solution)/shard_map/ppermute | solution.py:303
  52.0 0.0 collective-permute-done.10
  52.1 2.5 %collective-permute-start.11 = (bf16[128,256]{1,0:T(8,128)(2,1)S(1)}, bf16[128,256]{1,0:T(8,128)(2,1)S(1)}, u32[]{:S(2)}, u32[]{:S(2)}) collective-permute-start(bf16[128,256]{1,0:T(8,128)(2,1)S(1)} %fusion.refs_4_), channel_id=1, source_target_pairs={{0,1},{1,0},{2,3},{3,2},{4,5},{5,4},{6,7},{7,6},{8,9},{9,8},{10,11... | collective-permute-start | bytes 196616 | tf_op jit(solution)/shard_map/ppermute | solution.py:308
  54.6 1.5 %collective-permute-start.12 = (bf16[128,256]{1,0:T(8,128)(2,1)S(1)}, bf16[128,256]{1,0:T(8,128)(2,1)S(1)}, u32[]{:S(2)}, u32[]{:S(2)}) collective-permute-start(bf16[128,256]{1,0:T(8,128)(2,1)S(1)} %fusion.refs_4_), channel_id=1, source_target_pairs={{0,2},{1,3},{2,0},{3,1},{4,6},{5,7},{6,4},{7,5},{8,10},{9,11},{10,... | collective-permute-start | bytes 196616 | tf_op jit(solution)/shard_map/ppermute | solution.py:308
  56.2 0.9 %collective-permute-start.13 = (bf16[128,256]{1,0:T(8,128)(2,1)S(1)}, bf16[128,256]{1,0:T(8,128)(2,1)S(1)}, u32[]{:S(2)}, u32[]{:S(2)}) collective-permute-start(bf16[128,256]{1,0:T(8,128)(2,1)S(1)} %fusion.refs_4_), channel_id=1, source_target_pairs={{0,3},{1,2},{2,1},{3,0},{4,7},{5,6},{6,5},{7,4},{8,11},{9,10},{10,... | collective-permute-start | bytes 196616 | tf_op jit(solution)/shard_map/ppermute | solution.py:308
  57.0 6.0 %collective-permute-done.3 = f32[128,256]{1,0:T(8,128)S(1)} collective-permute-done((f32[128,256]{1,0:T(8,128)S(1)}, f32[128,256]{1,0:T(8,128)S(1)}, u32[]{:S(2)}, u32[]{:S(2)}) %collective-permute-start.3) | collective-permute-done | bytes 131104 | tf_op jit(solution)/shard_map/ppermute | solution.py:303
  63.0 0.1 collective-permute-start.4
  63.1 2.2 %collective-permute-start.5 = (bf16[128,256]{1,0:T(8,128)(2,1)S(1)}, bf16[128,256]{1,0:T(8,128)(2,1)S(1)}, u32[]{:S(2)}, u32[]{:S(2)}) collective-permute-start(bf16[128,256]{1,0:T(8,128)(2,1)S(1)} %fusion.1.refs_0_), channel_id=1, source_target_pairs={{0,2},{1,3},{2,0},{3,1},{4,6},{5,7},{6,4},{7,5},{8,10},{9,11},{10,... | collective-permute-start | bytes 196616 | tf_op jit(solution)/shard_map/ppermute | solution.py:308
  65.3 0.0 collective-permute-done.11.refs_5_
  65.3 2.2 %collective-permute-start.6 = (bf16[128,256]{1,0:T(8,128)(2,1)S(1)}, bf16[128,256]{1,0:T(8,128)(2,1)S(1)}, u32[]{:S(2)}, u32[]{:S(2)}) collective-permute-start(bf16[128,256]{1,0:T(8,128)(2,1)S(1)} %fusion.1.refs_0_), channel_id=1, source_target_pairs={{0,3},{1,2},{2,1},{3,0},{4,7},{5,6},{6,5},{7,4},{8,11},{9,10},{10,... | collective-permute-start | bytes 196616 | tf_op jit(solution)/shard_map/ppermute | solution.py:308
  67.5 0.7 fusion.6
  68.2 0.6 stack.7.pick_ref
  68.7 0.0 collective-permute-done.12.refs_6_
  68.7 0.0 collective-permute-done.13.refs_7_
  68.8 0.0 collective-permute-done.4.refs_1_
  68.8 1.8 %collective-permute-done.5.refs_2_ = bf16[128,256]{1,0:T(8,128)(2,1)S(1)} collective-permute-done((bf16[128,256]{1,0:T(8,128)(2,1)S(1)}, bf16[128,256]{1,0:T(8,128)(2,1)S(1)}, u32[]{:S(2)}, u32[]{:S(2)}) %collective-permute-start.5) | collective-permute-done | bytes 65568 | tf_op jit(solution)/shard_map/ppermute | solution.py:308
  70.6 0.8 %collective-permute-done.6.refs_3_ = bf16[128,256]{1,0:T(8,128)(2,1)S(1)} collective-permute-done((bf16[128,256]{1,0:T(8,128)(2,1)S(1)}, bf16[128,256]{1,0:T(8,128)(2,1)S(1)}, u32[]{:S(2)}, u32[]{:S(2)}) %collective-permute-start.6) | collective-permute-done | bytes 65568 | tf_op jit(solution)/shard_map/ppermute | solution.py:308
  71.5 0.6 copy-done.10
  72.0 6.4 %degrid.1 = f32[2,2,2048]{2,1,0:T(2,128)} custom-call(s32[2,2]{1,0:T(2,128)} %stack.7.pick_ref, f32[2,8]{1,0:T(2,128)} %get-tuple-element.21.rowtap_ref, f32[2,8]{1,0:T(2,128)} %get-tuple-element.22.coltap_ref, s32[2,2,2048]{2,1,0:T(2,128)} %cells_ref.1, bf16[512,512]{1,0:T(8,128)(2,1)} %constant.77.clone.table_ref, bf16[128,256]{1,0:T(8,128)(2,1)} %copy-done.4, ...), custom_call_target="tpu_custom_call" | custom-call | tf_op jit(solution)/shard_map/degrid/pallas_call | solution.py:319
  (33 shorter events, 0.3 us)
Async XLA Ops:
  1.3 19.7 %collective-permute-start.7 = (bf16[2,1024,128]{2,1,0:T(8,128)(2,1)S(1)}, bf16[2,1024,128]{2,1,0:T(8,128)(2,1)S(1)}, u32[]{:S(2)}, u32[]{:S(2)}) collective-permute-start(bf16[2,1024,128]{2,1,0:T(8,128)(2,1)S(1)} %get-tuple-element.19), channel_id=1, source_target_pairs={{0,8},{4,12},{8,0},{12,4},{1,9},{5,13},{9,1},{13,5},{2,10},{6,14},... | collective-permute-start | bytes 1572872 | tf_op jit(solution)/shard_map/ppermute | solution.py:248
  4.3 23.2 %collective-permute-start = (bf16[2,1024,128]{2,1,0:T(8,128)(2,1)S(1)}, bf16[2,1024,128]{2,1,0:T(8,128)(2,1)S(1)}, u32[]{:S(2)}, u32[]{:S(2)}) collective-permute-start(bf16[2,1024,128]{2,1,0:T(8,128)(2,1)S(1)} %get-tuple-element.20), channel_id=1, source_target_pairs={{0,8},{4,12},{8,0},{12,4},{1,9},{5,13},{9,1},{13,5},{2,10},{6,14},... | collective-permute-start | bytes 1572872 | tf_op jit(solution)/shard_map/ppermute | solution.py:248
  21.0 0.8 %copy-start.1 = (bf16[2,1024,128]{2,1,0:T(8,128)(2,1)}, bf16[2,1024,128]{2,1,0:T(8,128)(2,1)S(1)}, u32[]{:S(2)}) copy-start(bf16[2,1024,128]{2,1,0:T(8,128)(2,1)S(1)} %collective-permute-done.7.refs_0_) | copy-start | bytes 1572868
  26.8 6.6 %copy-start.11 = (s32[2,2]{1,0:T(2,128)S(1)}, s32[2,2]{1,0:T(2,128)}, u32[]{:S(2)}) copy-start(s32[2,2]{1,0:T(2,128)} %param.9) | copy-start | bytes 52
  26.8 6.8 %copy-start.2 = (f32[512,256]{1,0:T(8,128)S(1)}, f32[512,256]{1,0:T(8,128)}, u32[]{:S(2)}) copy-start(f32[512,256]{1,0:T(8,128)} %get-tuple-element.15) | copy-start | bytes 1572868
  26.8 6.8 %collective-permute-start.8 = (f32[512,256]{1,0:T(8,128)}, f32[512,256]{1,0:T(8,128)S(1)}, u32[]{:S(2)}, u32[]{:S(2)}) collective-permute-start(f32[512,256]{1,0:T(8,128)} %get-tuple-element.16), channel_id=1, source_target_pairs={{0,4},{4,0},{8,12},{12,8},{1,5},{5,1},{9,13},{13,9},{2,6},{6,2},{1... | collective-permute-start | bytes 1572872 | tf_op jit(solution)/shard_map/ppermute | solution.py:295
  27.5 0.9 %copy-start = (bf16[2,1024,128]{2,1,0:T(8,128)(2,1)}, bf16[2,1024,128]{2,1,0:T(8,128)(2,1)S(1)}, u32[]{:S(2)}) copy-start(bf16[2,1024,128]{2,1,0:T(8,128)(2,1)S(1)} %collective-permute-done.refs_0_) | copy-start | bytes 1572868
  33.4 34.8 %copy-start.12 = (s32[2]{0:T(128)S(1)}, s32[2]{0:T(128)}, u32[]{:S(2)}) copy-start(s32[2]{0:T(128)} %param.8) | copy-start | bytes 28
  33.4 2.6 %collective-permute-start.1 = (f32[512,256]{1,0:T(8,128)}, f32[512,256]{1,0:T(8,128)S(1)}, u32[]{:S(2)}, u32[]{:S(2)}) collective-permute-start(f32[512,256]{1,0:T(8,128)} %get-tuple-element.14), channel_id=1, source_target_pairs={{0,4},{4,0},{8,12},{12,8},{1,5},{5,1},{9,13},{13,9},{2,6},{6,2},{1... | collective-permute-start | bytes 1572872 | tf_op jit(solution)/shard_map/ppermute | solution.py:295
  33.7 9.2 %collective-permute-start.9 = (f32[2,128,256]{2,1,0:T(8,128)S(1)}, f32[2,128,256]{2,1,0:T(8,128)S(1)}, u32[]{:S(2)}, u32[]{:S(2)}) collective-permute-start(f32[2,128,256]{2,1,0:T(8,128)S(1)} %dynamic-slice_bitcast_fusion), channel_id=1, source_target_pairs={{0,1},{1,0},{2,3},{3,2},{4,5},{5,4},{6,7},{7,6},{8,9},{9,8},{10,11... | collective-permute-start | bytes 786440 | tf_op jit(solution)/shard_map/ppermute | solution.py:303
  37.1 13.8 %collective-permute-start.2 = (f32[2,128,256]{2,1,0:T(8,128)S(1)}, f32[2,128,256]{2,1,0:T(8,128)S(1)}, u32[]{:S(2)}, u32[]{:S(2)}) collective-permute-start(f32[2,128,256]{2,1,0:T(8,128)S(1)} %dynamic-slice_bitcast_fusion.1), channel_id=1, source_target_pairs={{0,1},{1,0},{2,3},{3,2},{4,5},{5,4},{6,7},{7,6},{8,9},{9,8},{10,11... | collective-permute-start | bytes 786440 | tf_op jit(solution)/shard_map/ppermute | solution.py:303
  42.9 9.1 %collective-permute-start.10 = (f32[128,256]{1,0:T(8,128)S(1)}, f32[128,256]{1,0:T(8,128)S(1)}, u32[]{:S(2)}, u32[]{:S(2)}) collective-permute-start(f32[128,256]{1,0:T(8,128)S(1)} %dynamic-slice_bitcast_fusion.2), channel_id=1, source_target_pairs={{0,2},{1,3},{2,0},{3,1},{4,6},{5,7},{6,4},{7,5},{8,10},{9,11},{10,... | collective-permute-start | bytes 393224 | tf_op jit(solution)/shard_map/ppermute | solution.py:303
  51.0 12.0 %collective-permute-start.3 = (f32[128,256]{1,0:T(8,128)S(1)}, f32[128,256]{1,0:T(8,128)S(1)}, u32[]{:S(2)}, u32[]{:S(2)}) collective-permute-start(f32[128,256]{1,0:T(8,128)S(1)} %dynamic-slice_bitcast_fusion.3), channel_id=1, source_target_pairs={{0,2},{1,3},{2,0},{3,1},{4,6},{5,7},{6,4},{7,5},{8,10},{9,11},{10,... | collective-permute-start | bytes 393224 | tf_op jit(solution)/shard_map/ppermute | solution.py:303
  52.1 19.4 %copy-start.3 = (bf16[128,256]{1,0:T(8,128)(2,1)}, bf16[128,256]{1,0:T(8,128)(2,1)S(1)}, u32[]{:S(2)}) copy-start(bf16[128,256]{1,0:T(8,128)(2,1)S(1)} %fusion.refs_4_) | copy-start | bytes 196612
  52.1 13.2 %collective-permute-start.11 = (bf16[128,256]{1,0:T(8,128)(2,1)S(1)}, bf16[128,256]{1,0:T(8,128)(2,1)S(1)}, u32[]{:S(2)}, u32[]{:S(2)}) collective-permute-start(bf16[128,256]{1,0:T(8,128)(2,1)S(1)} %fusion.refs_4_), channel_id=1, source_target_pairs={{0,1},{1,0},{2,3},{3,2},{4,5},{5,4},{6,7},{7,6},{8,9},{9,8},{10,11... | collective-permute-start | bytes 196616 | tf_op jit(solution)/shard_map/ppermute | solution.py:308
  54.6 14.1 %collective-permute-start.12 = (bf16[128,256]{1,0:T(8,128)(2,1)S(1)}, bf16[128,256]{1,0:T(8,128)(2,1)S(1)}, u32[]{:S(2)}, u32[]{:S(2)}) collective-permute-start(bf16[128,256]{1,0:T(8,128)(2,1)S(1)} %fusion.refs_4_), channel_id=1, source_target_pairs={{0,2},{1,3},{2,0},{3,1},{4,6},{5,7},{6,4},{7,5},{8,10},{9,11},{10,... | collective-permute-start | bytes 196616 | tf_op jit(solution)/shard_map/ppermute | solution.py:308
  56.2 12.6 %collective-permute-start.13 = (bf16[128,256]{1,0:T(8,128)(2,1)S(1)}, bf16[128,256]{1,0:T(8,128)(2,1)S(1)}, u32[]{:S(2)}, u32[]{:S(2)}) collective-permute-start(bf16[128,256]{1,0:T(8,128)(2,1)S(1)} %fusion.refs_4_), channel_id=1, source_target_pairs={{0,3},{1,2},{2,1},{3,0},{4,7},{5,6},{6,5},{7,4},{8,11},{9,10},{10,... | collective-permute-start | bytes 196616 | tf_op jit(solution)/shard_map/ppermute | solution.py:308
  63.0 8.4 %copy-start.4 = (bf16[128,256]{1,0:T(8,128)(2,1)}, bf16[128,256]{1,0:T(8,128)(2,1)S(1)}, u32[]{:S(2)}) copy-start(bf16[128,256]{1,0:T(8,128)(2,1)S(1)} %fusion.1.refs_0_) | copy-start | bytes 196612
  63.0 5.7 %collective-permute-start.4 = (bf16[128,256]{1,0:T(8,128)(2,1)S(1)}, bf16[128,256]{1,0:T(8,128)(2,1)S(1)}, u32[]{:S(2)}, u32[]{:S(2)}) collective-permute-start(bf16[128,256]{1,0:T(8,128)(2,1)S(1)} %fusion.1.refs_0_), channel_id=1, source_target_pairs={{0,1},{1,0},{2,3},{3,2},{4,5},{5,4},{6,7},{7,6},{8,9},{9,8},{10,11... | collective-permute-start | bytes 196616 | tf_op jit(solution)/shard_map/ppermute | solution.py:308
  63.1 7.5 %collective-permute-start.5 = (bf16[128,256]{1,0:T(8,128)(2,1)S(1)}, bf16[128,256]{1,0:T(8,128)(2,1)S(1)}, u32[]{:S(2)}, u32[]{:S(2)}) collective-permute-start(bf16[128,256]{1,0:T(8,128)(2,1)S(1)} %fusion.1.refs_0_), channel_id=1, source_target_pairs={{0,2},{1,3},{2,0},{3,1},{4,6},{5,7},{6,4},{7,5},{8,10},{9,11},{10,... | collective-permute-start | bytes 196616 | tf_op jit(solution)/shard_map/ppermute | solution.py:308
  65.3 6.1 %copy-start.5 = (bf16[128,256]{1,0:T(8,128)(2,1)}, bf16[128,256]{1,0:T(8,128)(2,1)S(1)}, u32[]{:S(2)}) copy-start(bf16[128,256]{1,0:T(8,128)(2,1)S(1)} %collective-permute-done.11.refs_5_) | copy-start | bytes 196612
  65.3 6.1 %collective-permute-start.6 = (bf16[128,256]{1,0:T(8,128)(2,1)S(1)}, bf16[128,256]{1,0:T(8,128)(2,1)S(1)}, u32[]{:S(2)}, u32[]{:S(2)}) collective-permute-start(bf16[128,256]{1,0:T(8,128)(2,1)S(1)} %fusion.1.refs_0_), channel_id=1, source_target_pairs={{0,3},{1,2},{2,1},{3,0},{4,7},{5,6},{6,5},{7,4},{8,11},{9,10},{10,... | collective-permute-start | bytes 196616 | tf_op jit(solution)/shard_map/ppermute | solution.py:308
  68.7 2.7 %copy-start.6 = (bf16[128,256]{1,0:T(8,128)(2,1)}, bf16[128,256]{1,0:T(8,128)(2,1)S(1)}, u32[]{:S(2)}) copy-start(bf16[128,256]{1,0:T(8,128)(2,1)S(1)} %collective-permute-done.12.refs_6_) | copy-start | bytes 196612
  68.8 2.7 %copy-start.7 = (bf16[128,256]{1,0:T(8,128)(2,1)}, bf16[128,256]{1,0:T(8,128)(2,1)S(1)}, u32[]{:S(2)}) copy-start(bf16[128,256]{1,0:T(8,128)(2,1)S(1)} %collective-permute-done.13.refs_7_) | copy-start | bytes 196612
  68.8 2.7 %copy-start.8 = (bf16[128,256]{1,0:T(8,128)(2,1)}, bf16[128,256]{1,0:T(8,128)(2,1)S(1)}, u32[]{:S(2)}) copy-start(bf16[128,256]{1,0:T(8,128)(2,1)S(1)} %collective-permute-done.4.refs_1_) | copy-start | bytes 196612
  70.6 0.9 %copy-start.9 = (bf16[128,256]{1,0:T(8,128)(2,1)}, bf16[128,256]{1,0:T(8,128)(2,1)S(1)}, u32[]{:S(2)}) copy-start(bf16[128,256]{1,0:T(8,128)(2,1)S(1)} %collective-permute-done.5.refs_2_) | copy-start | bytes 196612
  71.4 0.6 copy-start.10

commit v3 on v2

v3 whole, which is shorter than its diff:
```python
import functools
import math

import jax
import jax.numpy as jnp
import ml_dtypes
import numpy as np
from jax import lax
from jax.experimental import pallas as pl
from jax.experimental.pallas import tpu as pltpu
from jax.sharding import PartitionSpec as P

L = 4096
SUBW = 256
NVIS = 2048
SUPPORT = 8
OVERSAMPLE = 16
SG_WIDE = 2
SHOWN = 2 * SG_WIDE
CHUNKS = 2
CW = SUBW // CHUNKS
LANES = 2 * CW
FINE = 16
VMEM_LIMIT = 20 << 20

TURN = float(np.float32(2.0 * math.pi / L))
TURN_HIGH = float(np.float32(np.round(2.0 * math.pi / L * 2**20) / 2**20))
TURN_LOW = 2.0 * math.pi / L - TURN_HIGH


def tap_shape(fraction):
    centre = (SUPPORT - 1) / 2.0 + (fraction.astype(jnp.float32) + 0.5) / OVERSAMPLE - 0.5
    point = lax.broadcasted_iota(jnp.int32, (SUPPORT, 128), 0).astype(jnp.float32)
    distance = point - centre
    total = jnp.sum(jnp.exp(-distance * distance / 2.88), axis=0, keepdims=True)
    return centre, -jnp.log2(total)[:, 0:1]


def table_chunked():
    grid_ids = np.arange(SUBW)
    phase = 2.0 * math.pi / SUBW * (grid_ids[:, None] * grid_ids[None, :] % SUBW)
    cosine = np.cos(phase) / math.sqrt(SUBW)
    sine = np.sin(phase) / math.sqrt(SUBW)
    upper = np.concatenate([cosine, -sine], axis=1).reshape(CHUNKS, 1, CW, 2 * SUBW)
    lower = np.concatenate([sine, cosine], axis=1).reshape(CHUNKS, 1, CW, 2 * SUBW)
    both = np.concatenate([upper, lower], axis=1).reshape(2 * SUBW, 2 * SUBW)
    return jnp.asarray(both.T.astype(np.float32).astype(ml_dtypes.bfloat16))


def cos_sin(number):
    quarter = lax.shift_right_logical(number + L // 8, int(math.log2(L // 4)))
    angle = (number - quarter * (L // 4)).astype(jnp.float32) * TURN
    square = angle * angle
    sine = 1.0 / 362880
    for term in (-1.0 / 5040, 1.0 / 120, -1.0 / 6, 1.0):
        sine = sine * square + term
    sine = sine * angle
    cosine = -1.0 / 3628800
    for term in (1.0 / 40320, -1.0 / 720, 1.0 / 24, -0.5, 1.0):
        cosine = cosine * square + term
    odd = (quarter & 1) == 1
    first = jnp.where(odd, sine, cosine)
    second = jnp.where(odd, cosine, sine)
    first = jnp.where(((quarter + 1) & 2) == 2, -first, first)
    second = jnp.where((quarter & 2) == 2, -second, second)
    return first, second


def ramp_of(shift):
    lane = lax.broadcasted_iota(jnp.int32, (1, 2 * SUBW), 1)
    column = lane // LANES * CW + lane % CW
    cosine, sine = cos_sin((shift * column) % SUBW * (L // SUBW))
    return cosine, jnp.where(lane % LANES < CW, sine, -sine)


def cost(flops):
    return pl.CostEstimate(flops=flops, bytes_accessed=1 << 20, transcendentals=0)


def swap_halves(value):
    return jnp.concatenate([value[:, CW:], value[:, :CW]], axis=1)


def ramped(direct, crossed, cosine, sine):
    part = direct + jnp.concatenate([crossed[:, CW:], -crossed[:, :CW]], axis=1)
    return part * cosine + swap_halves(part) * sine


def shift_of(offset_ref, place_ref, wides, hop, shown, part):
    wide_id = place_ref[1]
    owner = wide_id ^ (shown // SG_WIDE)
    facet = lax.rem(wide_id - 2 * hop + wides, wides)
    return offset_ref[SG_WIDE * owner + shown % SG_WIDE, facet, part]


def prep_kernel(wides, offset_ref, place_ref, strips_hbm, rest_ref, own_ref, fine, fine_at, base, base_at, held, strips_ref, arrival):
    chips = wides // 2
    shift_at = functools.partial(shift_of, offset_ref, place_ref, wides)
    length = strips_ref.shape[1]
    copy = pltpu.make_async_copy(strips_hbm, strips_ref, arrival)
    copy.start()
    row_ids = place_ref[0] + lax.broadcasted_iota(jnp.int32, (FINE, length), 1)
    group = lax.broadcasted_iota(jnp.int32, (FINE, length), 0)
    centred = (2 * row_ids + 1).astype(jnp.float32) / L - 1.0
    taper = (1.0 - 0.5 * centred * centred) / math.sqrt(L)
    number = (group * row_ids) & (L - 1)
    fine_at[...] = number
    cosine, sine = cos_sin(number)
    fine[0] = cosine
    fine[1] = sine

    def make_factor(facet, shown, store):
        shift = shift_at(facet, shown, 0) + (L - SUBW // 2)
        number = ((shift + FINE * group) * row_ids) & (L - 1)
        base_at[...] = number
        cosine, sine = cos_sin(number)
        base[0] = cosine * taper
        base[1] = sine * taper

        def one_group(high, carry):
            at = (base_at[pl.ds(high, 1), :] + fine_at[...]) & (L - 1)
            count = at.astype(jnp.float32)
            turned = count * TURN
            slip = (turned - count * TURN_HIGH) - count * TURN_LOW
            base_c = base[0, pl.ds(high, 1), :]
            base_s = base[1, pl.ds(high, 1), :]
            cosine = base_c * fine[0] - base_s * fine[1]
            sine = base_s * fine[0] + base_c * fine[1]
            rows = pl.ds(pl.multiple_of(high * FINE, FINE), FINE)
            store(
                rows,
                (cosine - slip * sine).astype(jnp.bfloat16),
                (sine + slip * cosine).astype(jnp.bfloat16),
            )
            return carry

        lax.fori_loop(0, SUBW // FINE, one_group, 0, unroll=2)

    def rest_step(step, carry):
        facet = step // SHOWN
        shown = step % SHOWN

        def store(rows, cosine, sine):
            rest_ref[facet, shown, rows, :length] = cosine
            rest_ref[facet, shown, rows, length:] = sine

        make_factor(facet + 1, shown, store)
        return carry

    lax.fori_loop(0, (chips - 1) * SHOWN, rest_step, 0)
    copy.wait()

    def own_step(shown, carry):
        def store(rows, cosine, sine):
            held[rows, :length] = cosine
            held[rows, length:] = sine

        make_factor(0, shown, store)
        ramp_c, ramp_s = ramp_of(shift_at(0, shown, 1))
        for chunk in range(CHUNKS):
            columns = slice(chunk * CW, (chunk + 1) * CW)
            lanes = slice(chunk * LANES, (chunk + 1) * LANES)
            data = jnp.concatenate([strips_ref[0, :, columns], strips_ref[1, :, columns]], axis=1)
            direct = jnp.dot(held[:, :length], data, preferred_element_type=jnp.float32)
            crossed = jnp.dot(held[:, length:], data, preferred_element_type=jnp.float32)
            own_ref[chunk, shown] = ramped(direct, crossed, ramp_c[:, lanes], ramp_s[:, lanes])
        return carry

    lax.fori_loop(0, SHOWN, own_step, 0)


def chunk_kernel(chunk, wides, offset_ref, place_ref, rest_ref, own_ref, *refs):
    hops = wides // 2 - 1
    keep_ref, send_ref = refs[-2:]
    lanes = slice(chunk * LANES, (chunk + 1) * LANES)
    length = refs[0].shape[1]
    for shown in range(SHOWN):
        total = own_ref[chunk, shown]
        for hop in range(hops):
            data = jnp.concatenate([refs[hop][0], refs[hop][1]], axis=1)
            ramp_c, ramp_s = ramp_of(shift_of(offset_ref, place_ref, wides, hop + 1, shown, 1))
            direct = jnp.dot(
                rest_ref[hop, shown, :, :length], data, preferred_element_type=jnp.float32
            )
            crossed = jnp.dot(
                rest_ref[hop, shown, :, length:], data, preferred_element_type=jnp.float32
            )
            total = total + ramped(direct, crossed, ramp_c[:, lanes], ramp_s[:, lanes])
        target = keep_ref if shown < SG_WIDE else send_ref
        first = shown % SG_WIDE * SUBW
        target[first : first + SUBW, :] = total


def weight_kernel(fraction_ref, cells_ref, row_ref, col_ref):
    width = 512
    scale = -1.0 / (2.88 * math.log(2.0))
    ids = lax.broadcasted_iota(jnp.int32, (SUBW, width), 0).astype(jnp.float32)
    for block in range(cells_ref.shape[0]):
        for part, target in ((0, row_ref), (1, col_ref)):
            centre, norm = tap_shape(fraction_ref[block, part])

            def one_part(step, carry):
                lanes = pl.ds(pl.multiple_of(step * width, width), width)
                distance = ids - cells_ref[block, part : part + 1, lanes].astype(jnp.float32)
                offset = distance - centre
                values = jnp.exp2(offset * offset * scale + norm)
                inside = jnp.abs(distance - (SUPPORT - 1) / 2.0) < SUPPORT / 2.0
                target[block, :, lanes] = jnp.where(inside, values, 0.0).astype(target.dtype)
                return carry

            lax.fori_loop(0, NVIS // width, one_part, 0)


def degrid_kernel(pairs, place_ref, pick_ref, row_ref, col_ref, table_ref, *refs):
    count = CHUNKS * pairs
    pieces = refs[:count]
    out_ref, held = refs[count:]
    rows_dev = pieces[0].shape[0]
    place = place_ref[2]
    for chunk in range(CHUNKS):
        for step in range(pairs):
            at = pl.multiple_of((place ^ step) * rows_dev, rows_dev)
            held[pl.ds(at, rows_dev), chunk * LANES : (chunk + 1) * LANES] = pieces[
                chunk * pairs + step
            ][...]
    width = 512
    for block in range(row_ref.shape[0]):
        first = pl.multiple_of(pick_ref[block] * SUBW, SUBW)
        spectrum = lax.dot_general(
            table_ref[...],
            held[pl.ds(first, SUBW), :],
            (((1,), (1,)), ((), ())),
            preferred_element_type=jnp.float32,
        ).astype(jnp.bfloat16)
        for start in range(0, NVIS, width):
            lanes = slice(start, start + width)
            spread = jnp.dot(
                spectrum, row_ref[block, :, lanes], preferred_element_type=jnp.float32
            )
            weights = col_ref[block, :, lanes]
            out_ref[block, 0:1, lanes] = jnp.sum(weights * spread[:SUBW], axis=0, keepdims=True)
            out_ref[block, 1:2, lanes] = jnp.sum(weights * spread[SUBW:], axis=0, keepdims=True)


def on_device(strips, offsets, block_subgrid, block_kernel, vis_cells):
    pairs = lax.axis_size("pair")
    wides = lax.axis_size("wide")
    chips = wides // 2
    wide_id = lax.axis_index("wide")
    pair_id = lax.axis_index("pair")
    length = strips.shape[2]
    rows_dev = SG_WIDE * SUBW // pairs
    in_smem = pl.BlockSpec(memory_space=pltpu.SMEM)
    in_vmem = pl.BlockSpec(memory_space=pltpu.VMEM)
    anywhere = pl.BlockSpec(memory_space=pl.ANY)
    params = pltpu.CompilerParams(vmem_limit_bytes=VMEM_LIMIT)

    strips = strips[0]
    arrived = []
    whole = strips
    for index in range(CHUNKS):
        part = whole[:, :, index * CW : (index + 1) * CW]
        whole, part = lax.optimization_barrier((whole, part))
        arrived.append(
            [
                lax.ppermute(part, "wide", [(w, (w + 2 * hop) % wides) for w in range(wides)])
                for hop in range(1, chips)
            ]
        )

    place = jnp.stack([pair_id * length, wide_id, pair_id])

    rest, own = pl.pallas_call(
        functools.partial(prep_kernel, wides),
        out_shape=[
            jax.ShapeDtypeStruct((chips - 1, SHOWN, SUBW, 2 * length), jnp.bfloat16),
            jax.ShapeDtypeStruct((CHUNKS, SHOWN, SUBW, LANES), jnp.float32),
        ],
        in_specs=[in_smem, in_smem, anywhere],
        out_specs=[in_vmem, in_vmem],
        scratch_shapes=[
            pltpu.VMEM((2, FINE, length), jnp.float32),
            pltpu.VMEM((FINE, length), jnp.int32),
            pltpu.VMEM((2, FINE, length), jnp.float32),
            pltpu.VMEM((FINE, length), jnp.int32),
            pltpu.VMEM((SUBW, 2 * length), jnp.bfloat16),
            pltpu.VMEM((2, length, SUBW), jnp.bfloat16),
            pltpu.SemaphoreType.DMA,
        ],
        compiler_params=params,
        cost_estimate=cost(12100000000),
        name="prepare",
    )(offsets, place, strips)

    bits = pairs.bit_length() - 1

    def start_chunk(index):
        keep, send = pl.pallas_call(
            functools.partial(chunk_kernel, index, wides),
            out_shape=[jax.ShapeDtypeStruct((SG_WIDE * SUBW, LANES), jnp.float32)] * 2,
            in_specs=[in_smem, in_smem] + [in_vmem] * (chips + 1),
            out_specs=[in_vmem] * 2,
            compiler_params=params,
            cost_estimate=cost(2420000000),
        name="chunk_sums",
        )(offsets, place, rest, own, *arrived[index])
        other = lax.ppermute(send, "wide", [(w, w ^ 1) for w in range(wides)])
        shape = (2,) * bits + (rows_dev, LANES)
        return halved(keep.reshape(shape), other.reshape(shape), 0)

    def halved(first, second, bit):
        axis = first.ndim - 3
        mine = (pair_id >> bit) & 1
        passed, held = [
            lax.dynamic_index_in_dim(first, side, axis, keepdims=False)
            + lax.dynamic_index_in_dim(second, side, axis, keepdims=False)
            for side in (1 - mine, mine)
        ]
        return passed, held

    def exchange(passed, bit):
        return lax.ppermute(passed, "pair", [(p, p ^ (1 << bit)) for p in range(pairs)])

    blocks = vis_cells.shape[0]
    halves = []
    for index in range(CHUNKS):
        passed, held = start_chunk(index)
        halves.append((exchange(passed, 0), held))

    row_weights, col_weights = pl.pallas_call(
        weight_kernel,
        out_shape=[
            jax.ShapeDtypeStruct((blocks, SUBW, NVIS), jnp.bfloat16),
            jax.ShapeDtypeStruct((blocks, SUBW, NVIS), jnp.float32),
        ],
        in_specs=[in_smem, in_vmem],
        out_specs=[in_vmem] * 2,
        compiler_params=params,
        cost_estimate=cost(5500000000),
        name="weights",
    )(block_kernel, vis_cells)

    for bit in range(1, bits):
        for index in range(CHUNKS):
            passed, held = halved(*halves[index], bit)
            halves[index] = (exchange(passed, bit), held)

    pieces = []
    for index in range(CHUNKS):
        first, second = halves[index]
        parts = {0: (first + second).astype(jnp.bfloat16)}
        for step in range(1, pairs):
            parts[step] = lax.ppermute(parts[0], "pair", [(p, p ^ step) for p in range(pairs)])
        pieces += [parts[step] for step in range(pairs)]

    return pl.pallas_call(
        functools.partial(degrid_kernel, pairs),
        out_shape=jax.ShapeDtypeStruct((blocks, 2, NVIS), jnp.float32),
        in_specs=[in_smem] * 2 + [in_vmem] * (3 + len(pieces)),
        out_specs=in_vmem,
        scratch_shapes=[pltpu.VMEM((SG_WIDE * SUBW, 2 * SUBW), jnp.bfloat16)],
        compiler_params=params,
        cost_estimate=cost(3300000000),
        name="degrid",
    )(place, block_subgrid, row_weights, col_weights, table_chunked(), *pieces)


def solution(mesh):
    placed = (
        P(("groups", "wide"), None, "pair", None),
        P("groups", None, None),
        P(("groups", "wide", "pair")),
        P(("groups", "wide", "pair"), None),
        P(("groups", "wide", "pair"), None, None),
    )
    return jax.shard_map(
        on_device,
        mesh=mesh,
        in_specs=placed,
        out_specs=P(("groups", "wide", "pair"), None, None),
        check_vma=False,
    )
```

time: 78.7 us -> 72.1 us (0.916)
  Pallas kernels: 30.8 us -> 22.8 us
  waiting for transfers between devices: 18.7 us -> 22 us
  local copies, waits for them, and re-layouts: 6.24 us -> 4.19 us
    pallas_call x3 -> x4, Pallas kernels: 24.4 us -> 19.5 us  [the longest x1 11.6 us: on_device(): pl.pallas_call(functools.partial(prep_kernel, wides), out_shape=[jax.Shap...]
    ppermute x14, waiting for transfers between devices: 18.7 us -> 22 us  [the longest x4 14.5 us: exchange(): lax.ppermute(passed, 'pair', [(p, p ^ 1 << bit) for p in range(pairs)])]
    pallas_call x1, Pallas kernels: 6.4 us -> 3.33 us  [on_device(): pl.pallas_call(functools.partial(degrid_kernel, pairs), out_shape=jax.Sha...]
    gather x1 -> x0, local copies, waits for them, and re-layouts: 1.17 us -> none  [on_device(): shifts = offsets[subgrids[None, :], facets[:, None]]]
    unnamed x27 -> x11, local copies, waits for them, and re-layouts: 3.04 us -> 2.04 us
    slice x1 -> x2, local copies, waits for them, and re-layouts: 1.27 us -> 2.16 us  [on_device(): part = whole[:, :, index * CW:(index + 1) * CW]]
    add x5 -> x6, other arithmetic: 1.26 us -> 2.08 us  [halved(): lax.dynamic_index_in_dim(first, side, axis, keepdims=False)]
  transfers between devices with their start and end apart: 14 -> 14, of which waited for: 6 -> 6; matrix products, arithmetic and copies ran while one was open for 7% -> 4% of each run, Pallas kernels for 31% -> 27%
where the time goes in v3:
time: 72.1 us; the launch traced here: 71.7 us
  Pallas kernels  22.8 us (32%)
  waiting for transfers between devices  22 us (31%)
  starting transfers between devices  20.3 us (28%)
  local copies, waits for them, and re-layouts  4.19 us (6%)
  other arithmetic  2.21 us (3%)
    ppermute x4, waiting for transfers between devices, exchange(): lax.ppermute(passed, 'pair', [(p, p ^ 1 << bit) for p in range(pairs)])  14.5 us
    pallas_call x1, Pallas kernels, on_device(): pl.pallas_call(functools.partial(prep_kernel, wides), out_shape=[jax.Shap...  11.6 us
    ppermute x6, starting transfers between devices, on_device(): lax.ppermute(parts[0], 'pair', [(p, p ^ step) for p in range(pairs)])  9.43 us
    ppermute x4, starting transfers between devices, exchange(): lax.ppermute(passed, 'pair', [(p, p ^ 1 << bit) for p in range(pairs)])  7.64 us
    ppermute x2, waiting for transfers between devices, on_device(): lax.ppermute(part, 'wide', [(w, (w + 2 * hop) % wides) for w in range(wid...  7.09 us
    pallas_call x2, Pallas kernels, start_chunk(): pl.pallas_call(functools.partial(chunk_kernel, index, wides), out_shape=[...  4.34 us
    pallas_call x1, Pallas kernels, on_device(): pl.pallas_call(weight_kernel, out_shape=[jax.ShapeDtypeStruct((blocks, SU...  3.55 us
    pallas_call x1, Pallas kernels, on_device(): pl.pallas_call(functools.partial(degrid_kernel, pairs), out_shape=jax.Sha...  3.33 us
  transfers between devices with their start and end apart: 14, of which 6 were waited for; matrix products, arithmetic and copies ran while one was open for 4% of the time, Pallas kernels for 27%

profile of v3, /device:TPU:0, one launch (start us, length us, event | category | flops | bytes accessed | tf_op | source)
XLA Modules:
  0.0 71.7 jit_solution(13157459527287095140)
XLA Ops:
  0.0 1.1 %slice.8 = bf16[2,1024,128]{2,1,0:T(8,128)(2,1)S(1)} slice(bf16[2,1024,256]{2,1,0:T(8,128)(2,1)} %bitcast.52), slice={[0:2], [0:1024], [0:128]} | slice | bytes 1048576 | tf_op jit(solution)/shard_map/slice | solution.py:262
  1.1 1.1 %slice.7 = bf16[2,1024,128]{2,1,0:T(8,128)(2,1)S(1)} slice(bf16[2,1024,256]{2,1,0:T(8,128)(2,1)} %bitcast.53), slice={[0:2], [0:1024], [128:256]} | slice | bytes 1048576 | tf_op jit(solution)/shard_map/slice | solution.py:262
  2.2 3.0 %collective-permute-start.7 = (bf16[2,1024,128]{2,1,0:T(8,128)(2,1)S(1)}, bf16[2,1024,128]{2,1,0:T(8,128)(2,1)S(1)}, u32[]{:S(2)}, u32[]{:S(2)}) collective-permute-start(bf16[2,1024,128]{2,1,0:T(8,128)(2,1)S(1)} %slice.7), channel_id=1, source_target_pairs={{0,8},{4,12},{8,0},{12,4},{1,9},{5,13},{9,1},{13,5},{2,10},{6,14},... | collective-permute-start | bytes 1572872 | tf_op jit(solution)/shard_map/ppermute | solution.py:266
  5.2 0.1 collective-permute-start
  5.3 0.8 %copy.11.offset_ref = s32[8,4,2]{2,1,0:T(4,128)S(1)} copy(s32[8,4,2]{0,2,1:T(2,128)} %param.7) | data formatting | bytes 512 | tf_op args[1]
  6.1 0.1 pad_add_fusion.place_ref
  6.1 1.2 %copy-done = bf16[1,2,1024,256]{3,2,1,0:T(8,128)(2,1)S(1)} copy-done((bf16[1,2,1024,256]{3,2,1,0:T(8,128)(2,1)S(1)}, bf16[1,2,1024,256]{3,2,1,0:T(8,128)(2,1)}, u32[]{:S(2)}) %copy-start) | copy-done | bytes 1048600
  7.4 11.6 %prepare.1 = (bf16[1,4,256,2048]{3,2,1,0:T(8,128)(2,1)S(1)}, f32[2,4,256,256]{3,2,1,0:T(8,128)S(1)}) custom-call(s32[8,4,2]{2,1,0:T(4,128)S(1)} %copy.11.offset_ref, s32[3]{0:T(128)S(1)} %pad_add_fusion.place_ref, bf16[2,1024,256]{2,1,0:T(8,128)(2,1)S(1)} %bitcast.54), custom_call_target="tpu_custom_call" | custom-call | flops 12099999744 | bytes 1048576 | tf_op jit(solution)/shard_map/prepare/pallas_call | solution.py:273
  19.0 0.0 collective-permute-done.7.refs_0_
  19.0 2.2 %chunk_sums.3 = (f32[512,256]{1,0:T(8,128)S(1)}, f32[512,256]{1,0:T(8,128)S(1)}) custom-call(s32[8,4,2]{2,1,0:T(4,128)S(1)} %copy.11.offset_ref, s32[3]{0:T(128)S(1)} %pad_add_fusion.place_ref, bf16[1,4,256,2048]{3,2,1,0:T(8,128)(2,1)S(1)} %get-tuple-element.18.rest_ref, f32[2,4,256,256]{3,2,1,0:T(8,128)S(1)} %get-tuple-element.19.own_ref, ...), custom_call_target="tpu_custom_call" | custom-call | flops 2420000000 | bytes 1048576 | tf_op jit(solution)/shard_map/chunk_sums/pallas_call | solution.py:298
  21.2 0.1 collective-permute-start.8
  21.3 7.1 %collective-permute-done.refs_0_ = bf16[2,1024,128]{2,1,0:T(8,128)(2,1)S(1)} collective-permute-done((bf16[2,1024,128]{2,1,0:T(8,128)(2,1)S(1)}, bf16[2,1024,128]{2,1,0:T(8,128)(2,1)S(1)}, u32[]{:S(2)}, u32[]{:S(2)}) %collective-permute-start) | collective-permute-done | bytes 524320 | tf_op jit(solution)/shard_map/ppermute | solution.py:266
  28.4 2.2 %chunk_sums.2 = (f32[512,256]{1,0:T(8,128)S(1)}, f32[512,256]{1,0:T(8,128)S(1)}) custom-call(s32[8,4,2]{2,1,0:T(4,128)S(1)} %copy.11.offset_ref, s32[3]{0:T(128)S(1)} %pad_add_fusion.place_ref, bf16[1,4,256,2048]{3,2,1,0:T(8,128)(2,1)S(1)} %get-tuple-element.18.rest_ref, f32[2,4,256,256]{3,2,1,0:T(8,128)S(1)} %get-tuple-element.19.own_ref, ...), custom_call_target="tpu_custom_call" | custom-call | flops 2420000000 | bytes 1048576 | tf_op jit(solution)/shard_map/chunk_sums/pallas_call | solution.py:298
  30.5 0.0 copy-start.1
  30.5 0.0 copy-start.2
  30.6 0.1 collective-permute-start.1
  30.6 0.0 collective-permute-done.8
  30.7 1.9 %collective-permute-start.9 = (f32[2,128,256]{2,1,0:T(8,128)S(1)}, f32[2,128,256]{2,1,0:T(8,128)S(1)}, u32[]{:S(2)}, u32[]{:S(2)}) collective-permute-start(f32[2,128,256]{2,1,0:T(8,128)S(1)} %fusion), channel_id=1, source_target_pairs={{0,1},{1,0},{2,3},{3,2},{4,5},{5,4},{6,7},{7,6},{8,9},{9,8},{10,11... | collective-permute-start | bytes 786440 | tf_op jit(solution)/shard_map/ppermute | solution.py:322
  32.6 0.1 collective-permute-done.1
  32.7 1.0 %fusion.1 = f32[2,128,256]{2,1,0:T(8,128)S(1)} fusion(f32[2,2,128,256]{3,2,1,0:T(8,128)} %bitcast.5, s32[]{:T(128)S(6)} %select_n.26, f32[2,2,128,256]{3,2,1,0:T(8,128)S(1)} %bitcast.57), kind=kLoop, calls=%fused_computation.3 | loop fusion | flops 65536 | bytes 786436 | tf_op jit(solution)/shard_map/add | solution.py:315
  33.6 1.9 %collective-permute-start.2 = (f32[2,128,256]{2,1,0:T(8,128)S(1)}, f32[2,128,256]{2,1,0:T(8,128)S(1)}, u32[]{:S(2)}, u32[]{:S(2)}) collective-permute-start(f32[2,128,256]{2,1,0:T(8,128)S(1)} %fusion.1), channel_id=1, source_target_pairs={{0,1},{1,0},{2,3},{3,2},{4,5},{5,4},{6,7},{7,6},{8,9},{9,8},{10,11... | collective-permute-start | bytes 786440 | tf_op jit(solution)/shard_map/ppermute | solution.py:322
  35.5 4.3 %collective-permute-done.9 = f32[2,128,256]{2,1,0:T(8,128)S(1)} collective-permute-done((f32[2,128,256]{2,1,0:T(8,128)S(1)}, f32[2,128,256]{2,1,0:T(8,128)S(1)}, u32[]{:S(2)}, u32[]{:S(2)}) %collective-permute-start.9) | collective-permute-done | bytes 262176 | tf_op jit(solution)/shard_map/ppermute | solution.py:322
  39.9 2.9 %collective-permute-start.10 = (f32[128,256]{1,0:T(8,128)S(1)}, f32[128,256]{1,0:T(8,128)S(1)}, u32[]{:S(2)}, u32[]{:S(2)}) collective-permute-start(f32[128,256]{1,0:T(8,128)S(1)} %fusion.3), channel_id=1, source_target_pairs={{0,2},{1,3},{2,0},{3,1},{4,6},{5,7},{6,4},{7,5},{8,10},{9,11},{10,... | collective-permute-start | bytes 393224 | tf_op jit(solution)/shard_map/ppermute | solution.py:322
  42.8 1.0 %dynamic-slice_add_fusion.1 = f32[2,1,128,256]{3,2,1,0:T(8,128)S(1)} fusion(f32[2,2,128,256]{3,2,1,0:T(8,128)} %bitcast.5, s32[]{:T(128)S(6)} %select_n.28, f32[2,2,128,256]{3,2,1,0:T(8,128)S(1)} %bitcast.58), kind=kLoop, calls=%fused_computation.5 | loop fusion | flops 65536 | bytes 786436 | tf_op jit(solution)/shard_map/add | solution.py:315
  43.7 4.2 %collective-permute-done.2 = f32[2,128,256]{2,1,0:T(8,128)S(1)} collective-permute-done((f32[2,128,256]{2,1,0:T(8,128)S(1)}, f32[2,128,256]{2,1,0:T(8,128)S(1)}, u32[]{:S(2)}, u32[]{:S(2)}) %collective-permute-start.2) | collective-permute-done | bytes 262176 | tf_op jit(solution)/shard_map/ppermute | solution.py:322
  47.9 1.0 %collective-permute-start.3 = (f32[128,256]{1,0:T(8,128)S(1)}, f32[128,256]{1,0:T(8,128)S(1)}, u32[]{:S(2)}, u32[]{:S(2)}) collective-permute-start(f32[128,256]{1,0:T(8,128)S(1)} %fusion.5), channel_id=1, source_target_pairs={{0,2},{1,3},{2,0},{3,1},{4,6},{5,7},{6,4},{7,5},{8,10},{9,11},{10,... | collective-permute-start | bytes 393224 | tf_op jit(solution)/shard_map/ppermute | solution.py:322
  49.0 0.0 collective-permute-done.10
  49.0 2.5 %collective-permute-start.11 = (bf16[128,256]{1,0:T(8,128)(2,1)S(1)}, bf16[128,256]{1,0:T(8,128)(2,1)S(1)}, u32[]{:S(2)}, u32[]{:S(2)}) collective-permute-start(bf16[128,256]{1,0:T(8,128)(2,1)S(1)} %fusion.2.refs_4_), channel_id=1, source_target_pairs={{0,1},{1,0},{2,3},{3,2},{4,5},{5,4},{6,7},{7,6},{8,9},{9,8},{10,11... | collective-permute-start | bytes 196616 | tf_op jit(solution)/shard_map/ppermute | solution.py:353
  51.6 1.5 %collective-permute-start.12 = (bf16[128,256]{1,0:T(8,128)(2,1)S(1)}, bf16[128,256]{1,0:T(8,128)(2,1)S(1)}, u32[]{:S(2)}, u32[]{:S(2)}) collective-permute-start(bf16[128,256]{1,0:T(8,128)(2,1)S(1)} %fusion.2.refs_4_), channel_id=1, source_target_pairs={{0,2},{1,3},{2,0},{3,1},{4,6},{5,7},{6,4},{7,5},{8,10},{9,11},{10,... | collective-permute-start | bytes 196616 | tf_op jit(solution)/shard_map/ppermute | solution.py:353
  53.1 0.9 %collective-permute-start.13 = (bf16[128,256]{1,0:T(8,128)(2,1)S(1)}, bf16[128,256]{1,0:T(8,128)(2,1)S(1)}, u32[]{:S(2)}, u32[]{:S(2)}) collective-permute-start(bf16[128,256]{1,0:T(8,128)(2,1)S(1)} %fusion.2.refs_4_), channel_id=1, source_target_pairs={{0,3},{1,2},{2,1},{3,0},{4,7},{5,6},{6,5},{7,4},{8,11},{9,10},{10,... | collective-permute-start | bytes 196616 | tf_op jit(solution)/shard_map/ppermute | solution.py:353
  54.0 6.0 %collective-permute-done.3 = f32[128,256]{1,0:T(8,128)S(1)} collective-permute-done((f32[128,256]{1,0:T(8,128)S(1)}, f32[128,256]{1,0:T(8,128)S(1)}, u32[]{:S(2)}, u32[]{:S(2)}) %collective-permute-start.3) | collective-permute-done | bytes 131104 | tf_op jit(solution)/shard_map/ppermute | solution.py:322
  60.0 0.0 copy-start.3
  60.0 0.0 copy-start.4
  60.0 0.1 collective-permute-start.4
  60.1 2.2 %collective-permute-start.5 = (bf16[128,256]{1,0:T(8,128)(2,1)S(1)}, bf16[128,256]{1,0:T(8,128)(2,1)S(1)}, u32[]{:S(2)}, u32[]{:S(2)}) collective-permute-start(bf16[128,256]{1,0:T(8,128)(2,1)S(1)} %fusion.4.refs_0_), channel_id=1, source_target_pairs={{0,2},{1,3},{2,0},{3,1},{4,6},{5,7},{6,4},{7,5},{8,10},{9,11},{10,... | collective-permute-start | bytes 196616 | tf_op jit(solution)/shard_map/ppermute | solution.py:353
  62.3 0.0 collective-permute-done.11.refs_5_
  62.3 2.2 %collective-permute-start.6 = (bf16[128,256]{1,0:T(8,128)(2,1)S(1)}, bf16[128,256]{1,0:T(8,128)(2,1)S(1)}, u32[]{:S(2)}, u32[]{:S(2)}) collective-permute-start(bf16[128,256]{1,0:T(8,128)(2,1)S(1)} %fusion.4.refs_0_), channel_id=1, source_target_pairs={{0,3},{1,2},{2,1},{3,0},{4,7},{5,6},{6,5},{7,4},{8,11},{9,10},{10,... | collective-permute-start | bytes 196616 | tf_op jit(solution)/shard_map/ppermute | solution.py:353
  64.5 0.0 copy-done.1
  64.5 0.0 copy-done.2
  64.5 3.5 %weights.1 = (bf16[2,256,2048]{2,1,0:T(8,128)(2,1)S(1)}, f32[2,256,2048]{2,1,0:T(8,128)S(1)}) custom-call(s32[2,2]{1,0:T(2,128)S(1)} %copy-done.2, s32[2,2,2048]{2,1,0:T(2,128)S(1)} %copy-done.1), custom_call_target="tpu_custom_call" | custom-call | flops 5500000256 | bytes 1048576 | tf_op jit(solution)/shard_map/weights/pallas_call | solution.py:330
  68.0 0.0 collective-permute-done.12.refs_6_
  68.1 0.0 collective-permute-done.13.refs_7_
  68.1 0.0 collective-permute-done.4.refs_1_
  68.1 0.0 collective-permute-done.5.refs_2_
  68.1 0.3 collective-permute-done.6.refs_3_
  68.4 0.0 copy-done.3
  68.4 0.0 copy-done.4
  68.4 3.3 %degrid.1 = f32[2,2,2048]{2,1,0:T(2,128)} custom-call(s32[3]{0:T(128)S(1)} %pad_add_fusion.place_ref, s32[2]{0:T(128)S(1)} %copy-done.3, bf16[2,256,2048]{2,1,0:T(8,128)(2,1)S(1)} %get-tuple-element.16.row_ref, f32[2,256,2048]{2,1,0:T(8,128)S(1)} %get-tuple-element.17.col_ref, bf16[512,512]{1,0:T(8,128)(2,1)S(1)} %copy-done.4, ...), custom_call_target="tpu_custom_call" | custom-call | flops 3300000000 | bytes 1048576 | tf_op jit(solution)/shard_map/degrid/pallas_call | solution.py:356
  (7 shorter events, 0.2 us)
Async XLA Ops:
  2.2 16.8 %collective-permute-start.7 = (bf16[2,1024,128]{2,1,0:T(8,128)(2,1)S(1)}, bf16[2,1024,128]{2,1,0:T(8,128)(2,1)S(1)}, u32[]{:S(2)}, u32[]{:S(2)}) collective-permute-start(bf16[2,1024,128]{2,1,0:T(8,128)(2,1)S(1)} %slice.7), channel_id=1, source_target_pairs={{0,8},{4,12},{8,0},{12,4},{1,9},{5,13},{9,1},{13,5},{2,10},{6,14},... | collective-permute-start | bytes 1572872 | tf_op jit(solution)/shard_map/ppermute | solution.py:266
  5.2 23.2 %collective-permute-start = (bf16[2,1024,128]{2,1,0:T(8,128)(2,1)S(1)}, bf16[2,1024,128]{2,1,0:T(8,128)(2,1)S(1)}, u32[]{:S(2)}, u32[]{:S(2)}) collective-permute-start(bf16[2,1024,128]{2,1,0:T(8,128)(2,1)S(1)} %slice.8), channel_id=1, source_target_pairs={{0,8},{4,12},{8,0},{12,4},{1,9},{5,13},{9,1},{13,5},{2,10},{6,14},... | collective-permute-start | bytes 1572872 | tf_op jit(solution)/shard_map/ppermute | solution.py:266
  6.1 1.2 %copy-start = (bf16[1,2,1024,256]{3,2,1,0:T(8,128)(2,1)S(1)}, bf16[1,2,1024,256]{3,2,1,0:T(8,128)(2,1)}, u32[]{:S(2)}) copy-start(bf16[1,2,1024,256]{3,2,1,0:T(8,128)(2,1)} %param.6) | copy-start | bytes 3145732
  21.2 9.4 %collective-permute-start.8 = (f32[512,256]{1,0:T(8,128)S(1)}, f32[512,256]{1,0:T(8,128)S(1)}, u32[]{:S(2)}, u32[]{:S(2)}) collective-permute-start(f32[512,256]{1,0:T(8,128)S(1)} %get-tuple-element.26), channel_id=1, source_target_pairs={{0,4},{4,0},{8,12},{12,8},{1,5},{5,1},{9,13},{13,9},{2,6},{6,2},{1... | collective-permute-start | bytes 1572872 | tf_op jit(solution)/shard_map/ppermute | solution.py:307
  30.5 34.0 %copy-start.1 = (s32[2,2,2048]{2,1,0:T(2,128)S(1)}, s32[2,2,2048]{2,1,0:T(2,128)}, u32[]{:S(2)}) copy-start(s32[2,2,2048]{2,1,0:T(2,128)} %cells_ref.1) | copy-start | bytes 98308
  30.5 34.0 %copy-start.2 = (s32[2,2]{1,0:T(2,128)S(1)}, s32[2,2]{1,0:T(2,128)}, u32[]{:S(2)}) copy-start(s32[2,2]{1,0:T(2,128)} %fraction_ref.1) | copy-start | bytes 52
  30.6 2.1 %collective-permute-start.1 = (f32[512,256]{1,0:T(8,128)S(1)}, f32[512,256]{1,0:T(8,128)}, u32[]{:S(2)}, u32[]{:S(2)}) collective-permute-start(f32[512,256]{1,0:T(8,128)S(1)} %get-tuple-element.22), channel_id=1, source_target_pairs={{0,4},{4,0},{8,12},{12,8},{1,5},{5,1},{9,13},{13,9},{2,6},{6,2},{1... | collective-permute-start | bytes 1572872 | tf_op jit(solution)/shard_map/ppermute | solution.py:307
  30.7 9.2 %collective-permute-start.9 = (f32[2,128,256]{2,1,0:T(8,128)S(1)}, f32[2,128,256]{2,1,0:T(8,128)S(1)}, u32[]{:S(2)}, u32[]{:S(2)}) collective-permute-start(f32[2,128,256]{2,1,0:T(8,128)S(1)} %fusion), channel_id=1, source_target_pairs={{0,1},{1,0},{2,3},{3,2},{4,5},{5,4},{6,7},{7,6},{8,9},{9,8},{10,11... | collective-permute-start | bytes 786440 | tf_op jit(solution)/shard_map/ppermute | solution.py:322
  33.6 14.3 %collective-permute-start.2 = (f32[2,128,256]{2,1,0:T(8,128)S(1)}, f32[2,128,256]{2,1,0:T(8,128)S(1)}, u32[]{:S(2)}, u32[]{:S(2)}) collective-permute-start(f32[2,128,256]{2,1,0:T(8,128)S(1)} %fusion.1), channel_id=1, source_target_pairs={{0,1},{1,0},{2,3},{3,2},{4,5},{5,4},{6,7},{7,6},{8,9},{9,8},{10,11... | collective-permute-start | bytes 786440 | tf_op jit(solution)/shard_map/ppermute | solution.py:322
  39.9 9.1 %collective-permute-start.10 = (f32[128,256]{1,0:T(8,128)S(1)}, f32[128,256]{1,0:T(8,128)S(1)}, u32[]{:S(2)}, u32[]{:S(2)}) collective-permute-start(f32[128,256]{1,0:T(8,128)S(1)} %fusion.3), channel_id=1, source_target_pairs={{0,2},{1,3},{2,0},{3,1},{4,6},{5,7},{6,4},{7,5},{8,10},{9,11},{10,... | collective-permute-start | bytes 393224 | tf_op jit(solution)/shard_map/ppermute | solution.py:322
  47.9 12.0 %collective-permute-start.3 = (f32[128,256]{1,0:T(8,128)S(1)}, f32[128,256]{1,0:T(8,128)S(1)}, u32[]{:S(2)}, u32[]{:S(2)}) collective-permute-start(f32[128,256]{1,0:T(8,128)S(1)} %fusion.5), channel_id=1, source_target_pairs={{0,2},{1,3},{2,0},{3,1},{4,6},{5,7},{6,4},{7,5},{8,10},{9,11},{10,... | collective-permute-start | bytes 393224 | tf_op jit(solution)/shard_map/ppermute | solution.py:322
  49.0 13.3 %collective-permute-start.11 = (bf16[128,256]{1,0:T(8,128)(2,1)S(1)}, bf16[128,256]{1,0:T(8,128)(2,1)S(1)}, u32[]{:S(2)}, u32[]{:S(2)}) collective-permute-start(bf16[128,256]{1,0:T(8,128)(2,1)S(1)} %fusion.2.refs_4_), channel_id=1, source_target_pairs={{0,1},{1,0},{2,3},{3,2},{4,5},{5,4},{6,7},{7,6},{8,9},{9,8},{10,11... | collective-permute-start | bytes 196616 | tf_op jit(solution)/shard_map/ppermute | solution.py:353
  51.6 16.5 %collective-permute-start.12 = (bf16[128,256]{1,0:T(8,128)(2,1)S(1)}, bf16[128,256]{1,0:T(8,128)(2,1)S(1)}, u32[]{:S(2)}, u32[]{:S(2)}) collective-permute-start(bf16[128,256]{1,0:T(8,128)(2,1)S(1)} %fusion.2.refs_4_), channel_id=1, source_target_pairs={{0,2},{1,3},{2,0},{3,1},{4,6},{5,7},{6,4},{7,5},{8,10},{9,11},{10,... | collective-permute-start | bytes 196616 | tf_op jit(solution)/shard_map/ppermute | solution.py:353
  53.1 14.9 %collective-permute-start.13 = (bf16[128,256]{1,0:T(8,128)(2,1)S(1)}, bf16[128,256]{1,0:T(8,128)(2,1)S(1)}, u32[]{:S(2)}, u32[]{:S(2)}) collective-permute-start(bf16[128,256]{1,0:T(8,128)(2,1)S(1)} %fusion.2.refs_4_), channel_id=1, source_target_pairs={{0,3},{1,2},{2,1},{3,0},{4,7},{5,6},{6,5},{7,4},{8,11},{9,10},{10,... | collective-permute-start | bytes 196616 | tf_op jit(solution)/shard_map/ppermute | solution.py:353
  60.0 8.4 %copy-start.3 = (s32[2]{0:T(128)S(1)}, s32[2]{0:T(128)}, u32[]{:S(2)}) copy-start(s32[2]{0:T(128)} %pick_ref.1) | copy-start | bytes 28
  60.0 8.4 %copy-start.4 = (bf16[512,512]{1,0:T(8,128)(2,1)S(1)}, bf16[512,512]{1,0:T(8,128)(2,1)}, u32[]{:S(2)}) copy-start(bf16[512,512]{1,0:T(8,128)(2,1)} %constant.59.clone.table_ref) | copy-start | bytes 1572868
  60.0 8.0 %collective-permute-start.4 = (bf16[128,256]{1,0:T(8,128)(2,1)S(1)}, bf16[128,256]{1,0:T(8,128)(2,1)S(1)}, u32[]{:S(2)}, u32[]{:S(2)}) collective-permute-start(bf16[128,256]{1,0:T(8,128)(2,1)S(1)} %fusion.4.refs_0_), channel_id=1, source_target_pairs={{0,1},{1,0},{2,3},{3,2},{4,5},{5,4},{6,7},{7,6},{8,9},{9,8},{10,11... | collective-permute-start | bytes 196616 | tf_op jit(solution)/shard_map/ppermute | solution.py:353
  60.1 8.0 %collective-permute-start.5 = (bf16[128,256]{1,0:T(8,128)(2,1)S(1)}, bf16[128,256]{1,0:T(8,128)(2,1)S(1)}, u32[]{:S(2)}, u32[]{:S(2)}) collective-permute-start(bf16[128,256]{1,0:T(8,128)(2,1)S(1)} %fusion.4.refs_0_), channel_id=1, source_target_pairs={{0,2},{1,3},{2,0},{3,1},{4,6},{5,7},{6,4},{7,5},{8,10},{9,11},{10,... | collective-permute-start | bytes 196616 | tf_op jit(solution)/shard_map/ppermute | solution.py:353
  62.3 6.1 %collective-permute-start.6 = (bf16[128,256]{1,0:T(8,128)(2,1)S(1)}, bf16[128,256]{1,0:T(8,128)(2,1)S(1)}, u32[]{:S(2)}, u32[]{:S(2)}) collective-permute-start(bf16[128,256]{1,0:T(8,128)(2,1)S(1)} %fusion.4.refs_0_), channel_id=1, source_target_pairs={{0,3},{1,2},{2,1},{3,0},{4,7},{5,6},{6,5},{7,4},{8,11},{9,10},{10,... | collective-permute-start | bytes 196616 | tf_op jit(solution)/shard_map/ppermute | solution.py:353

commit v4 on v3

--- a/solution.py
+++ b/solution.py
@@ -21,6 +21,9 @@
 CW = SUBW // CHUNKS
 LANES = 2 * CW
 FINE = 16
+WIDTH = 256
+PARTS = 2
+PART = LANES // PARTS
 VMEM_LIMIT = 20 << 20
 
 TURN = float(np.float32(2.0 * math.pi / L))
@@ -93,7 +96,9 @@
     return offset_ref[SG_WIDE * owner + shown % SG_WIDE, facet, part]
 
 
-def prep_kernel(wides, offset_ref, place_ref, strips_hbm, rest_ref, own_ref, fine, fine_at, base, base_at, held, strips_ref, arrival):
+def prep_kernel(wides, offset_ref, place_ref, strips_hbm, rest_ref, *refs):
+    own_refs = refs[:CHUNKS]
+    fine, fine_at, base, base_at, held, strips_ref, arrival = refs[CHUNKS:]
     chips = wides // 2
     shift_at = functools.partial(shift_of, offset_ref, place_ref, wides)
     length = strips_ref.shape[1]
@@ -117,32 +122,37 @@
         base[0] = cosine * taper
         base[1] = sine * taper
 
-        def one_group(high, carry):
-            at = (base_at[pl.ds(high, 1), :] + fine_at[...]) & (L - 1)
-            count = at.astype(jnp.float32)
-            turned = count * TURN
-            slip = (turned - count * TURN_HIGH) - count * TURN_LOW
-            base_c = base[0, pl.ds(high, 1), :]
-            base_s = base[1, pl.ds(high, 1), :]
-            cosine = base_c * fine[0] - base_s * fine[1]
-            sine = base_s * fine[0] + base_c * fine[1]
-            rows = pl.ds(pl.multiple_of(high * FINE, FINE), FINE)
-            store(
-                rows,
-                (cosine - slip * sine).astype(jnp.bfloat16),
-                (sine + slip * cosine).astype(jnp.bfloat16),
-            )
+        def one_strip(step, carry):
+            lanes = pl.ds(pl.multiple_of(step * WIDTH, WIDTH), WIDTH)
+            fine_n = fine_at[:, lanes]
+            fine_c = fine[0, :, lanes]
+            fine_s = fine[1, :, lanes]
+            for high in range(SUBW // FINE):
+                at = (base_at[high : high + 1, lanes] + fine_n) & (L - 1)
+                count = at.astype(jnp.float32)
+                turned = count * TURN
+                slip = (turned - count * TURN_HIGH) - count * TURN_LOW
+                base_c = base[0, high : high + 1, lanes]
+                base_s = base[1, high : high + 1, lanes]
+                cosine = base_c * fine_c - base_s * fine_s
+                sine = base_s * fine_c + base_c * fine_s
+                store(
+                    slice(high * FINE, (high + 1) * FINE),
+                    step * WIDTH,
+                    (cosine - slip * sine).astype(jnp.bfloat16),
+                    (sine + slip * cosine).astype(jnp.bfloat16),
+                )
             return carry
 
-        lax.fori_loop(0, SUBW // FINE, one_group, 0, unroll=2)
+        lax.fori_loop(0, length // WIDTH, one_strip, 0)
 
     def rest_step(step, carry):
         facet = step // SHOWN
         shown = step % SHOWN
 
-        def store(rows, cosine, sine):
-            rest_ref[facet, shown, rows, :length] = cosine
-            rest_ref[facet, shown, rows, length:] = sine
+        def store(rows, start, cosine, sine):
+            rest_ref[facet, shown, rows, pl.ds(pl.multiple_of(start, WIDTH), WIDTH)] = cosine
+            rest_ref[facet, shown, rows, pl.ds(pl.multiple_of(start + length, WIDTH), WIDTH)] = sine
 
         make_factor(facet + 1, shown, store)
         return carry
@@ -151,9 +161,9 @@
     copy.wait()
 
     def own_step(shown, carry):
-        def store(rows, cosine, sine):
-            held[rows, :length] = cosine
-            held[rows, length:] = sine
+        def store(rows, start, cosine, sine):
+            held[rows, pl.ds(pl.multiple_of(start, WIDTH), WIDTH)] = cosine
+            held[rows, pl.ds(pl.multiple_of(start + length, WIDTH), WIDTH)] = sine
 
         make_factor(0, shown, store)
         ramp_c, ramp_s = ramp_of(shift_at(0, shown, 1))
@@ -163,7 +173,7 @@
             data = jnp.concatenate([strips_ref[0, :, columns], strips_ref[1, :, columns]], axis=1)
             direct = jnp.dot(held[:, :length], data, preferred_element_type=jnp.float32)
             crossed = jnp.dot(held[:, length:], data, preferred_element_type=jnp.float32)
-            own_ref[chunk, shown] = ramped(direct, crossed, ramp_c[:, lanes], ramp_s[:, lanes])
+            own_refs[chunk][shown] = ramped(direct, crossed, ramp_c[:, lanes], ramp_s[:, lanes])
         return carry
 
     lax.fori_loop(0, SHOWN, own_step, 0)
@@ -171,11 +181,14 @@
 
 def chunk_kernel(chunk, wides, offset_ref, place_ref, rest_ref, own_ref, *refs):
     hops = wides // 2 - 1
-    keep_ref, send_ref = refs[-2:]
+    targets, whole = refs[-5:-1], refs[-1]
+    rows_dev = targets[0].shape[-2]
+    groups = SUBW // (2 * rows_dev)
+    mine = place_ref[2] & 1
     lanes = slice(chunk * LANES, (chunk + 1) * LANES)
     length = refs[0].shape[1]
     for shown in range(SHOWN):
-        total = own_ref[chunk, shown]
+        total = own_ref[shown]
         for hop in range(hops):
             data = jnp.concatenate([refs[hop][0], refs[hop][1]], axis=1)
             ramp_c, ramp_s = ramp_of(shift_of(offset_ref, place_ref, wides, hop + 1, shown, 1))
@@ -186,9 +199,16 @@
                 rest_ref[hop, shown, :, length:], data, preferred_element_type=jnp.float32
             )
             total = total + ramped(direct, crossed, ramp_c[:, lanes], ramp_s[:, lanes])
-        target = keep_ref if shown < SG_WIDE else send_ref
-        first = shown % SG_WIDE * SUBW
-        target[first : first + SUBW, :] = total
+        whole[...] = total
+        for group in range(groups):
+            index = shown % SG_WIDE * groups + group
+            for half in range(2):
+                side = mine ^ (1 - half)
+                at = pl.multiple_of((2 * group + side) * rows_dev, rows_dev)
+                for part in range(PARTS):
+                    targets[shown // SG_WIDE * 2 + half][part, index] = whole[
+                        pl.ds(at, rows_dev), part * PART : (part + 1) * PART
+                    ]
 
 
 def weight_kernel(fraction_ref, cells_ref, row_ref, col_ref):
@@ -215,14 +235,14 @@
     count = CHUNKS * pairs
     pieces = refs[:count]
     out_ref, held = refs[count:]
-    rows_dev = pieces[0].shape[0]
+    rows_dev = pieces[0].shape[1]
     place = place_ref[2]
     for chunk in range(CHUNKS):
         for step in range(pairs):
             at = pl.multiple_of((place ^ step) * rows_dev, rows_dev)
-            held[pl.ds(at, rows_dev), chunk * LANES : (chunk + 1) * LANES] = pieces[
-                chunk * pairs + step
-            ][...]
+            for part in range(PARTS):
+                lane = chunk * LANES + part * PART
+                held[pl.ds(at, rows_dev), lane : lane + PART] = pieces[chunk * pairs + step][part]
     width = 512
     for block in range(row_ref.shape[0]):
         first = pl.multiple_of(pick_ref[block] * SUBW, SUBW)
@@ -257,10 +277,8 @@
 
     strips = strips[0]
     arrived = []
-    whole = strips
     for index in range(CHUNKS):
-        part = whole[:, :, index * CW : (index + 1) * CW]
-        whole, part = lax.optimization_barrier((whole, part))
+        part = strips[:, :, index * CW : (index + 1) * CW]
         arrived.append(
             [
                 lax.ppermute(part, "wide", [(w, (w + 2 * hop) % wides) for w in range(wides)])
@@ -270,14 +288,14 @@
 
     place = jnp.stack([pair_id * length, wide_id, pair_id])
 
-    rest, own = pl.pallas_call(
+    rest, *own = pl.pallas_call(
         functools.partial(prep_kernel, wides),
         out_shape=[
             jax.ShapeDtypeStruct((chips - 1, SHOWN, SUBW, 2 * length), jnp.bfloat16),
-            jax.ShapeDtypeStruct((CHUNKS, SHOWN, SUBW, LANES), jnp.float32),
-        ],
+        ]
+        + [jax.ShapeDtypeStruct((SHOWN, SUBW, LANES), jnp.float32)] * CHUNKS,
         in_specs=[in_smem, in_smem, anywhere],
-        out_specs=[in_vmem, in_vmem],
+        out_specs=[in_vmem] * (1 + CHUNKS),
         scratch_shapes=[
             pltpu.VMEM((2, FINE, length), jnp.float32),
             pltpu.VMEM((FINE, length), jnp.int32),
@@ -295,18 +313,28 @@
     bits = pairs.bit_length() - 1
 
     def start_chunk(index):
-        keep, send = pl.pallas_call(
+        sums = pl.pallas_call(
             functools.partial(chunk_kernel, index, wides),
-            out_shape=[jax.ShapeDtypeStruct((SG_WIDE * SUBW, LANES), jnp.float32)] * 2,
+            out_shape=[jax.ShapeDtypeStruct((PARTS, pairs // 2, rows_dev, PART), jnp.float32)] * 4,
             in_specs=[in_smem, in_smem] + [in_vmem] * (chips + 1),
-            out_specs=[in_vmem] * 2,
+            out_specs=[in_vmem] * 4,
+            scratch_shapes=[pltpu.VMEM((SUBW, LANES), jnp.float32)],
             compiler_params=params,
             cost_estimate=cost(2420000000),
-        name="chunk_sums",
-        )(offsets, place, rest, own, *arrived[index])
-        other = lax.ppermute(send, "wide", [(w, w ^ 1) for w in range(wides)])
-        shape = (2,) * bits + (rows_dev, LANES)
-        return halved(keep.reshape(shape), other.reshape(shape), 0)
+            name="chunk_sums",
+        )(offsets, place, rest, own[index], *arrived[index])
+        shape = (2,) * (bits - 1) + (rows_dev, PART)
+        cores = [(w, w ^ 1) for w in range(wides)]
+        keep_pass, keep_hold, send_pass, send_hold = sums
+        other_pass = lax.ppermute(send_pass, "wide", cores)
+        other_hold = lax.ppermute(send_hold, "wide", cores)
+        return [
+            (
+                (keep_pass[part] + other_pass[part]).reshape(shape),
+                (keep_hold[part] + other_hold[part]).reshape(shape),
+            )
+            for part in range(PARTS)
+        ]
 
     def halved(first, second, bit):
         axis = first.ndim - 3
@@ -324,8 +352,8 @@
     blocks = vis_cells.shape[0]
     halves = []
     for index in range(CHUNKS):
-        passed, held = start_chunk(index)
-        halves.append((exchange(passed, 0), held))
+        for passed, held in start_chunk(index):
+            halves.append((exchange(passed, 0), held))
 
     row_weights, col_weights = pl.pallas_call(
         weight_kernel,
@@ -341,14 +369,14 @@
     )(block_kernel, vis_cells)
 
     for bit in range(1, bits):
-        for index in range(CHUNKS):
+        for index in range(CHUNKS * PARTS):
             passed, held = halved(*halves[index], bit)
             halves[index] = (exchange(passed, bit), held)
 
     pieces = []
     for index in range(CHUNKS):
-        first, second = halves[index]
-        parts = {0: (first + second).astype(jnp.bfloat16)}
+        both = halves[index * PARTS : (index + 1) * PARTS]
+        parts = {0: jnp.stack([first + second for first, second in both]).astype(jnp.bfloat16)}
         for step in range(1, pairs):
             parts[step] = lax.ppermute(parts[0], "pair", [(p, p ^ step) for p in range(pairs)])
         pieces += [parts[step] for step in range(pairs)]

time: 72.1 us -> 69.8 us (0.968)
  starting transfers between devices: 20.3 us -> 25.9 us
  waiting for transfers between devices: 22 us -> 17.9 us
  other arithmetic: 2.21 us -> 0.38 us
  Pallas kernels: 22.8 us -> 21.9 us
  local copies, waits for them, and re-layouts: 4.19 us -> 3.3 us
    ppermute x4 -> x8, waiting for transfers between devices: 14.5 us -> 9.28 us  [exchange(): lax.ppermute(passed, 'pair', [(p, p ^ 1 << bit) for p in range(pairs)])]
    ppermute x4 -> x8, starting transfers between devices: 7.64 us -> 12.6 us  [exchange(): lax.ppermute(passed, 'pair', [(p, p ^ 1 << bit) for p in range(pairs)])]
    add x6 -> x4, other arithmetic: 2.08 us -> 0.04 us  [halved(): lax.dynamic_index_in_dim(first, side, axis, keepdims=False)]
    pallas_call x1, Pallas kernels: 11.6 us -> 10.4 us  [on_device(): pl.pallas_call(functools.partial(prep_kernel, wides), out_shape=[jax.Shap...]
    ppermute x2, waiting for transfers between devices: 7.09 us -> 8.21 us  [on_device(): lax.ppermute(part, 'wide', [(w, (w + 2 * hop) % wides) for w in range(wid...]
    slice x2 -> x1, local copies, waits for them, and re-layouts: 2.16 us -> 1.27 us  [on_device(): part = strips[:, :, index * CW:(index + 1) * CW]]
  transfers between devices with their start and end apart: 14 -> 20, of which waited for: 6 -> 7; matrix products, arithmetic and copies ran while one was open for 4% -> 2% of each run, Pallas kernels for 27% -> 27%
where the time goes in v4:
time: 69.8 us; the launch traced here: 69.6 us
  starting transfers between devices  25.9 us (37%)
  Pallas kernels  21.9 us (31%)
  waiting for transfers between devices  17.9 us (26%)
  local copies, waits for them, and re-layouts  3.3 us (5%)
    ppermute x8, starting transfers between devices, exchange(): lax.ppermute(passed, 'pair', [(p, p ^ 1 << bit) for p in range(pairs)])  12.6 us
    pallas_call x1, Pallas kernels, on_device(): pl.pallas_call(functools.partial(prep_kernel, wides), out_shape=[jax.Shap...  10.4 us
    ppermute x6, starting transfers between devices, on_device(): lax.ppermute(parts[0], 'pair', [(p, p ^ step) for p in range(pairs)])  9.43 us
    ppermute x8, waiting for transfers between devices, exchange(): lax.ppermute(passed, 'pair', [(p, p ^ 1 << bit) for p in range(pairs)])  9.28 us
    ppermute x2, waiting for transfers between devices, on_device(): lax.ppermute(part, 'wide', [(w, (w + 2 * hop) % wides) for w in range(wid...  8.21 us
    pallas_call x2, Pallas kernels, start_chunk(): pl.pallas_call(functools.partial(chunk_kernel, index, wides), out_shape=[...  4.64 us
    pallas_call x1, Pallas kernels, on_device(): pl.pallas_call(weight_kernel, out_shape=[jax.ShapeDtypeStruct((blocks, SU...  3.55 us
    pallas_call x1, Pallas kernels, on_device(): pl.pallas_call(functools.partial(degrid_kernel, pairs), out_shape=jax.Sha...  3.38 us
  transfers between devices with their start and end apart: 20, of which 7 were waited for; matrix products, arithmetic and copies ran while one was open for 2% of the time, Pallas kernels for 27%

profile of v4, /device:TPU:0, one launch (start us, length us, event | category | flops | bytes accessed | tf_op | source)
XLA Modules:
  0.0 69.6 jit_solution(6192347328858744706)
XLA Ops:
  0.0 1.3 %fusion.16 = (bf16[2,1024,128]{2,1,0:T(8,128)(2,1)S(1)}, bf16[2,1024,128]{2,1,0:T(8,128)(2,1)S(1)}) fusion(bf16[2,1024,256]{2,1,0:T(8,128)(2,1)} %bitcast.92), kind=kLoop, calls=%fused_computation.39 | loop fusion | bytes 2097152 | tf_op jit(solution)/shard_map/slice | solution.py:281
  1.3 3.0 %collective-permute-start.10 = (bf16[2,1024,128]{2,1,0:T(8,128)(2,1)S(1)}, bf16[2,1024,128]{2,1,0:T(8,128)(2,1)S(1)}, u32[]{:S(2)}, u32[]{:S(2)}) collective-permute-start(bf16[2,1024,128]{2,1,0:T(8,128)(2,1)S(1)} %get-tuple-element.31), channel_id=1, source_target_pairs={{0,8},{4,12},{8,0},{12,4},{1,9},{5,13},{9,1},{13,5},{2,10},{6,14},... | collective-permute-start | bytes 1572872 | tf_op jit(solution)/shard_map/ppermute | solution.py:284
  4.3 0.1 collective-permute-start
  4.4 0.8 %copy.8.offset_ref = s32[8,4,2]{2,1,0:T(4,128)S(1)} copy(s32[8,4,2]{0,2,1:T(2,128)} %param.7) | data formatting | bytes 512 | tf_op args[1]
  5.2 0.1 pad_add_fusion.place_ref
  5.2 1.2 %copy-done = bf16[1,2,1024,256]{3,2,1,0:T(8,128)(2,1)S(1)} copy-done((bf16[1,2,1024,256]{3,2,1,0:T(8,128)(2,1)S(1)}, bf16[1,2,1024,256]{3,2,1,0:T(8,128)(2,1)}, u32[]{:S(2)}) %copy-start) | copy-done | bytes 1048600
  6.5 10.4 %prepare.1 = (bf16[1,4,256,2048]{3,2,1,0:T(8,128)(2,1)S(1)}, f32[4,256,256]{2,1,0:T(8,128)S(1)}, f32[4,256,256]{2,1,0:T(8,128)S(1)}) custom-call(s32[8,4,2]{2,1,0:T(4,128)S(1)} %copy.8.offset_ref, s32[3]{0:T(128)S(1)} %pad_add_fusion.place_ref, bf16[2,1024,256]{2,1,0:T(8,128)(2,1)S(1)} %bitcast.93), custom_call_target="tpu_custom_call" | custom-call | flops 12099999744 | bytes 1048576 | tf_op jit(solution)/shard_map/prepare/pallas_call | solution.py:291
  16.9 0.2 collective-permute-done.10.refs_0_
  17.1 2.3 %chunk_sums.3 = (f32[2,2,128,128]{3,2,1,0:T(8,128)S(1)}, f32[2,2,128,128]{3,2,1,0:T(8,128)S(1)}, f32[2,2,128,128]{3,2,1,0:T(8,128)S(1)}, f32[2,2,128,128]{3,2,1,0:T(8,128)S(1)}) custom-call(s32[8,4,2]{2,1,0:T(4,128)S(1)} %copy.8.offset_ref, s32[3]{0:T(128)S(1)} %pad_add_fusion.place_ref, bf16[1,4,256,2048]{3,2,1,0:T(8,128)(2,1)S(1)} %get-tuple-element.20.rest_ref, ...), custom_call_target="tpu_custom_call" | custom-call | flops 2420000000 | bytes 1048576 | tf_op jit(solution)/shard_map/chunk_sums/pallas_call | solution.py:316
  19.4 0.1 collective-permute-start.11
  19.5 8.0 %collective-permute-done.refs_0_ = bf16[2,1024,128]{2,1,0:T(8,128)(2,1)S(1)} collective-permute-done((bf16[2,1024,128]{2,1,0:T(8,128)(2,1)S(1)}, bf16[2,1024,128]{2,1,0:T(8,128)(2,1)S(1)}, u32[]{:S(2)}, u32[]{:S(2)}) %collective-permute-start) | collective-permute-done | bytes 524320 | tf_op jit(solution)/shard_map/ppermute | solution.py:284
  27.5 2.3 %chunk_sums.2 = (f32[2,2,128,128]{3,2,1,0:T(8,128)S(1)}, f32[2,2,128,128]{3,2,1,0:T(8,128)S(1)}, f32[2,2,128,128]{3,2,1,0:T(8,128)S(1)}, f32[2,2,128,128]{3,2,1,0:T(8,128)S(1)}) custom-call(s32[8,4,2]{2,1,0:T(4,128)S(1)} %copy.8.offset_ref, s32[3]{0:T(128)S(1)} %pad_add_fusion.place_ref, bf16[1,4,256,2048]{3,2,1,0:T(8,128)(2,1)S(1)} %get-tuple-element.20.rest_ref, ...), custom_call_target="tpu_custom_call" | custom-call | flops 2420000000 | bytes 1048576 | tf_op jit(solution)/shard_map/chunk_sums/pallas_call | solution.py:316
  29.8 0.0 copy-start.1
  29.8 0.0 copy-start.2
  29.8 0.1 collective-permute-start.1
  29.9 0.5 collective-permute-start.13
  30.4 0.1 collective-permute-start.3
  30.5 0.0 collective-permute-done.11
  30.5 1.9 %collective-permute-start.12 = (f32[2,128,128]{2,1,0:T(8,128)S(1)}, f32[2,128,128]{2,1,0:T(8,128)S(1)}, u32[]{:S(2)}, u32[]{:S(2)}) collective-permute-start(f32[2,128,128]{2,1,0:T(8,128)S(1)} %get-tuple-element.33), channel_id=1, source_target_pairs={{0,1},{1,0},{2,3},{3,2},{4,5},{5,4},{6,7},{7,6},{8,9},{9,8},{10,11... | collective-permute-start | bytes 393224 | tf_op jit(solution)/shard_map/ppermute | solution.py:350
  32.4 0.2 collective-permute-start.15
  32.6 0.0 collective-permute-done.1
  32.7 1.9 %collective-permute-start.2 = (f32[2,128,128]{2,1,0:T(8,128)S(1)}, f32[2,128,128]{2,1,0:T(8,128)S(1)}, u32[]{:S(2)}, u32[]{:S(2)}) collective-permute-start(f32[2,128,128]{2,1,0:T(8,128)S(1)} %get-tuple-element.37), channel_id=1, source_target_pairs={{0,1},{1,0},{2,3},{3,2},{4,5},{5,4},{6,7},{7,6},{8,9},{9,8},{10,11... | collective-permute-start | bytes 393224 | tf_op jit(solution)/shard_map/ppermute | solution.py:350
  34.5 0.0 collective-permute-done.13
  34.5 0.2 collective-permute-start.5
  34.9 2.0 %collective-permute-done.12 = f32[2,128,128]{2,1,0:T(8,128)S(1)} collective-permute-done((f32[2,128,128]{2,1,0:T(8,128)S(1)}, f32[2,128,128]{2,1,0:T(8,128)S(1)}, u32[]{:S(2)}, u32[]{:S(2)}) %collective-permute-start.12) | collective-permute-done | bytes 131104 | tf_op jit(solution)/shard_map/ppermute | solution.py:350
  36.9 2.9 %collective-permute-start.14 = (f32[128,128]{1,0:T(8,128)S(1)}, f32[128,128]{1,0:T(8,128)S(1)}, u32[]{:S(2)}, u32[]{:S(2)}) collective-permute-start(f32[128,128]{1,0:T(8,128)S(1)} %fusion.7), channel_id=1, source_target_pairs={{0,2},{1,3},{2,0},{3,1},{4,6},{5,7},{6,4},{7,5},{8,10},{9,11},{10,... | collective-permute-start | bytes 196616 | tf_op jit(solution)/shard_map/ppermute | solution.py:350
  39.8 2.8 %collective-permute-start.16 = (f32[128,128]{1,0:T(8,128)S(1)}, f32[128,128]{1,0:T(8,128)S(1)}, u32[]{:S(2)}, u32[]{:S(2)}) collective-permute-start(f32[128,128]{1,0:T(8,128)S(1)} %fusion.5), channel_id=1, source_target_pairs={{0,2},{1,3},{2,0},{3,1},{4,6},{5,7},{6,4},{7,5},{8,10},{9,11},{10,... | collective-permute-start | bytes 196616 | tf_op jit(solution)/shard_map/ppermute | solution.py:350
  42.6 2.7 %collective-permute-done.2 = f32[2,128,128]{2,1,0:T(8,128)S(1)} collective-permute-done((f32[2,128,128]{2,1,0:T(8,128)S(1)}, f32[2,128,128]{2,1,0:T(8,128)S(1)}, u32[]{:S(2)}, u32[]{:S(2)}) %collective-permute-start.2) | collective-permute-done | bytes 131104 | tf_op jit(solution)/shard_map/ppermute | solution.py:350
  45.3 1.2 %collective-permute-start.4 = (f32[128,128]{1,0:T(8,128)S(1)}, f32[128,128]{1,0:T(8,128)S(1)}, u32[]{:S(2)}, u32[]{:S(2)}) collective-permute-start(f32[128,128]{1,0:T(8,128)S(1)} %fusion.11), channel_id=1, source_target_pairs={{0,2},{1,3},{2,0},{3,1},{4,6},{5,7},{6,4},{7,5},{8,10},{9,11},{10,... | collective-permute-start | bytes 196616 | tf_op jit(solution)/shard_map/ppermute | solution.py:350
  46.5 1.4 %collective-permute-done.5 = f32[2,128,128]{2,1,0:T(8,128)S(1)} collective-permute-done((f32[2,128,128]{2,1,0:T(8,128)S(1)}, f32[2,128,128]{2,1,0:T(8,128)S(1)}, u32[]{:S(2)}, u32[]{:S(2)}) %collective-permute-start.5) | collective-permute-done | bytes 131104 | tf_op jit(solution)/shard_map/ppermute | solution.py:350
  47.9 1.6 %collective-permute-start.6 = (f32[128,128]{1,0:T(8,128)S(1)}, f32[128,128]{1,0:T(8,128)S(1)}, u32[]{:S(2)}, u32[]{:S(2)}) collective-permute-start(f32[128,128]{1,0:T(8,128)S(1)} %fusion.9), channel_id=1, source_target_pairs={{0,2},{1,3},{2,0},{3,1},{4,6},{5,7},{6,4},{7,5},{8,10},{9,11},{10,... | collective-permute-start | bytes 196616 | tf_op jit(solution)/shard_map/ppermute | solution.py:350
  49.5 0.0 collective-permute-done.16
  49.6 2.5 %collective-permute-start.17 = (bf16[2,128,128]{2,1,0:T(8,128)(2,1)S(1)}, bf16[2,128,128]{2,1,0:T(8,128)(2,1)S(1)}, u32[]{:S(2)}, u32[]{:S(2)}) collective-permute-start(bf16[2,128,128]{2,1,0:T(8,128)(2,1)S(1)} %pad_maximum_fusion.1.refs_4_), channel_id=1, source_target_pairs={{0,1},{1,0},{2,3},{3,2},{4,5},{5,4},{6,7},{7,6},{8,9},{9,8},{10,11... | collective-permute-start | bytes 196616 | tf_op jit(solution)/shard_map/ppermute | solution.py:381
  52.1 1.6 %collective-permute-start.18 = (bf16[2,128,128]{2,1,0:T(8,128)(2,1)S(1)}, bf16[2,128,128]{2,1,0:T(8,128)(2,1)S(1)}, u32[]{:S(2)}, u32[]{:S(2)}) collective-permute-start(bf16[2,128,128]{2,1,0:T(8,128)(2,1)S(1)} %pad_maximum_fusion.1.refs_4_), channel_id=1, source_target_pairs={{0,2},{1,3},{2,0},{3,1},{4,6},{5,7},{6,4},{7,5},{8,10},{9,11},{10,... | collective-permute-start | bytes 196616 | tf_op jit(solution)/shard_map/ppermute | solution.py:381
  53.7 0.8 %collective-permute-start.19 = (bf16[2,128,128]{2,1,0:T(8,128)(2,1)S(1)}, bf16[2,128,128]{2,1,0:T(8,128)(2,1)S(1)}, u32[]{:S(2)}, u32[]{:S(2)}) collective-permute-start(bf16[2,128,128]{2,1,0:T(8,128)(2,1)S(1)} %pad_maximum_fusion.1.refs_4_), channel_id=1, source_target_pairs={{0,3},{1,2},{2,1},{3,0},{4,7},{5,6},{6,5},{7,4},{8,11},{9,10},{10,... | collective-permute-start | bytes 196616 | tf_op jit(solution)/shard_map/ppermute | solution.py:381
  54.6 0.0 collective-permute-done.4
  54.6 3.2 %collective-permute-done.6 = f32[128,128]{1,0:T(8,128)S(1)} collective-permute-done((f32[128,128]{1,0:T(8,128)S(1)}, f32[128,128]{1,0:T(8,128)S(1)}, u32[]{:S(2)}, u32[]{:S(2)}) %collective-permute-start.6) | collective-permute-done | bytes 65568 | tf_op jit(solution)/shard_map/ppermute | solution.py:350
  57.8 0.0 copy-start.3
  57.8 0.0 copy-start.4
  57.8 0.1 collective-permute-start.7
  57.9 1.9 %collective-permute-start.8 = (bf16[2,128,128]{2,1,0:T(8,128)(2,1)S(1)}, bf16[2,128,128]{2,1,0:T(8,128)(2,1)S(1)}, u32[]{:S(2)}, u32[]{:S(2)}) collective-permute-start(bf16[2,128,128]{2,1,0:T(8,128)(2,1)S(1)} %pad_maximum_fusion.refs_0_), channel_id=1, source_target_pairs={{0,2},{1,3},{2,0},{3,1},{4,6},{5,7},{6,4},{7,5},{8,10},{9,11},{10,... | collective-permute-start | bytes 196616 | tf_op jit(solution)/shard_map/ppermute | solution.py:381
  59.8 0.0 collective-permute-done.17.refs_5_
  59.8 2.4 %collective-permute-start.9 = (bf16[2,128,128]{2,1,0:T(8,128)(2,1)S(1)}, bf16[2,128,128]{2,1,0:T(8,128)(2,1)S(1)}, u32[]{:S(2)}, u32[]{:S(2)}) collective-permute-start(bf16[2,128,128]{2,1,0:T(8,128)(2,1)S(1)} %pad_maximum_fusion.refs_0_), channel_id=1, source_target_pairs={{0,3},{1,2},{2,1},{3,0},{4,7},{5,6},{6,5},{7,4},{8,11},{9,10},{10,... | collective-permute-start | bytes 196616 | tf_op jit(solution)/shard_map/ppermute | solution.py:381
  62.3 3.5 %weights.1 = (bf16[2,256,2048]{2,1,0:T(8,128)(2,1)S(1)}, f32[2,256,2048]{2,1,0:T(8,128)S(1)}) custom-call(s32[2,2]{1,0:T(2,128)S(1)} %copy-done.2, s32[2,2,2048]{2,1,0:T(2,128)S(1)} %copy-done.1), custom_call_target="tpu_custom_call" | custom-call | flops 5500000256 | bytes 1048576 | tf_op jit(solution)/shard_map/weights/pallas_call | solution.py:358
  65.8 0.0 collective-permute-done.19.refs_7_
  65.8 0.0 collective-permute-done.7.refs_1_
  65.8 0.4 collective-permute-done.8.refs_2_
  66.2 3.4 %degrid.1 = f32[2,2,2048]{2,1,0:T(2,128)} custom-call(s32[3]{0:T(128)S(1)} %pad_add_fusion.place_ref, s32[2]{0:T(128)S(1)} %copy-done.3, bf16[2,256,2048]{2,1,0:T(8,128)(2,1)S(1)} %get-tuple-element.18.row_ref, f32[2,256,2048]{2,1,0:T(8,128)S(1)} %get-tuple-element.19.col_ref, bf16[512,512]{1,0:T(8,128)(2,1)S(1)} %copy-done.4, ...), custom_call_target="tpu_custom_call" | custom-call | flops 3300000000 | bytes 1048576 | tf_op jit(solution)/shard_map/degrid/pallas_call | solution.py:384
  (24 shorter events, 0.3 us)
Async XLA Ops:
  1.3 15.8 %collective-permute-start.10 = (bf16[2,1024,128]{2,1,0:T(8,128)(2,1)S(1)}, bf16[2,1024,128]{2,1,0:T(8,128)(2,1)S(1)}, u32[]{:S(2)}, u32[]{:S(2)}) collective-permute-start(bf16[2,1024,128]{2,1,0:T(8,128)(2,1)S(1)} %get-tuple-element.31), channel_id=1, source_target_pairs={{0,8},{4,12},{8,0},{12,4},{1,9},{5,13},{9,1},{13,5},{2,10},{6,14},... | collective-permute-start | bytes 1572872 | tf_op jit(solution)/shard_map/ppermute | solution.py:284
  4.3 23.2 %collective-permute-start = (bf16[2,1024,128]{2,1,0:T(8,128)(2,1)S(1)}, bf16[2,1024,128]{2,1,0:T(8,128)(2,1)S(1)}, u32[]{:S(2)}, u32[]{:S(2)}) collective-permute-start(bf16[2,1024,128]{2,1,0:T(8,128)(2,1)S(1)} %get-tuple-element.32), channel_id=1, source_target_pairs={{0,8},{4,12},{8,0},{12,4},{1,9},{5,13},{9,1},{13,5},{2,10},{6,14},... | collective-permute-start | bytes 1572872 | tf_op jit(solution)/shard_map/ppermute | solution.py:284
  5.2 1.2 %copy-start = (bf16[1,2,1024,256]{3,2,1,0:T(8,128)(2,1)S(1)}, bf16[1,2,1024,256]{3,2,1,0:T(8,128)(2,1)}, u32[]{:S(2)}) copy-start(bf16[1,2,1024,256]{3,2,1,0:T(8,128)(2,1)} %param.6) | copy-start | bytes 3145732
  19.4 11.1 %collective-permute-start.11 = (f32[2,2,128,128]{3,2,1,0:T(8,128)S(1)}, f32[2,2,128,128]{3,2,1,0:T(8,128)S(1)}, u32[]{:S(2)}, u32[]{:S(2)}) collective-permute-start(f32[2,2,128,128]{3,2,1,0:T(8,128)S(1)} %get-tuple-element.28), channel_id=1, source_target_pairs={{0,4},{4,0},{8,12},{12,8},{1,5},{5,1},{9,13},{13,9},{2,6},{6,2},{1... | collective-permute-start | bytes 786440 | tf_op jit(solution)/shard_map/ppermute | solution.py:329
  29.8 32.5 %copy-start.1 = (s32[2,2,2048]{2,1,0:T(2,128)S(1)}, s32[2,2,2048]{2,1,0:T(2,128)}, u32[]{:S(2)}) copy-start(s32[2,2,2048]{2,1,0:T(2,128)} %cells_ref.1) | copy-start | bytes 98308
  29.8 32.5 %copy-start.2 = (s32[2,2]{1,0:T(2,128)S(1)}, s32[2,2]{1,0:T(2,128)}, u32[]{:S(2)}) copy-start(s32[2,2]{1,0:T(2,128)} %fraction_ref.1) | copy-start | bytes 52
  29.8 2.8 %collective-permute-start.1 = (f32[2,2,128,128]{3,2,1,0:T(8,128)S(1)}, f32[2,2,128,128]{3,2,1,0:T(8,128)S(1)}, u32[]{:S(2)}, u32[]{:S(2)}) collective-permute-start(f32[2,2,128,128]{3,2,1,0:T(8,128)S(1)} %get-tuple-element.23), channel_id=1, source_target_pairs={{0,4},{4,0},{8,12},{12,8},{1,5},{5,1},{9,13},{13,9},{2,6},{6,2},{1... | collective-permute-start | bytes 786440 | tf_op jit(solution)/shard_map/ppermute | solution.py:329
  29.9 4.6 %collective-permute-start.13 = (f32[2,2,128,128]{3,2,1,0:T(8,128)S(1)}, f32[2,2,128,128]{3,2,1,0:T(8,128)S(1)}, u32[]{:S(2)}, u32[]{:S(2)}) collective-permute-start(f32[2,2,128,128]{3,2,1,0:T(8,128)S(1)} %get-tuple-element.30), channel_id=1, source_target_pairs={{0,4},{4,0},{8,12},{12,8},{1,5},{5,1},{9,13},{13,9},{2,6},{6,2},{1... | collective-permute-start | bytes 786440 | tf_op jit(solution)/shard_map/ppermute | solution.py:330
  30.4 4.4 %collective-permute-start.3 = (f32[2,2,128,128]{3,2,1,0:T(8,128)S(1)}, f32[2,2,128,128]{3,2,1,0:T(8,128)S(1)}, u32[]{:S(2)}, u32[]{:S(2)}) collective-permute-start(f32[2,2,128,128]{3,2,1,0:T(8,128)S(1)} %get-tuple-element.25), channel_id=1, source_target_pairs={{0,4},{4,0},{8,12},{12,8},{1,5},{5,1},{9,13},{13,9},{2,6},{6,2},{1... | collective-permute-start | bytes 786440 | tf_op jit(solution)/shard_map/ppermute | solution.py:330
  30.5 6.4 %collective-permute-start.12 = (f32[2,128,128]{2,1,0:T(8,128)S(1)}, f32[2,128,128]{2,1,0:T(8,128)S(1)}, u32[]{:S(2)}, u32[]{:S(2)}) collective-permute-start(f32[2,128,128]{2,1,0:T(8,128)S(1)} %get-tuple-element.33), channel_id=1, source_target_pairs={{0,1},{1,0},{2,3},{3,2},{4,5},{5,4},{6,7},{7,6},{8,9},{9,8},{10,11... | collective-permute-start | bytes 393224 | tf_op jit(solution)/shard_map/ppermute | solution.py:350
  32.4 7.4 %collective-permute-start.15 = (f32[2,128,128]{2,1,0:T(8,128)S(1)}, f32[2,128,128]{2,1,0:T(8,128)S(1)}, u32[]{:S(2)}, u32[]{:S(2)}) collective-permute-start(f32[2,128,128]{2,1,0:T(8,128)S(1)} %get-tuple-element.34), channel_id=1, source_target_pairs={{0,1},{1,0},{2,3},{3,2},{4,5},{5,4},{6,7},{7,6},{8,9},{9,8},{10,11... | collective-permute-start | bytes 393224 | tf_op jit(solution)/shard_map/ppermute | solution.py:350
  32.7 12.6 %collective-permute-start.2 = (f32[2,128,128]{2,1,0:T(8,128)S(1)}, f32[2,128,128]{2,1,0:T(8,128)S(1)}, u32[]{:S(2)}, u32[]{:S(2)}) collective-permute-start(f32[2,128,128]{2,1,0:T(8,128)S(1)} %get-tuple-element.37), channel_id=1, source_target_pairs={{0,1},{1,0},{2,3},{3,2},{4,5},{5,4},{6,7},{7,6},{8,9},{9,8},{10,11... | collective-permute-start | bytes 393224 | tf_op jit(solution)/shard_map/ppermute | solution.py:350
  34.5 13.3 %collective-permute-start.5 = (f32[2,128,128]{2,1,0:T(8,128)S(1)}, f32[2,128,128]{2,1,0:T(8,128)S(1)}, u32[]{:S(2)}, u32[]{:S(2)}) collective-permute-start(f32[2,128,128]{2,1,0:T(8,128)S(1)} %get-tuple-element.38), channel_id=1, source_target_pairs={{0,1},{1,0},{2,3},{3,2},{4,5},{5,4},{6,7},{7,6},{8,9},{9,8},{10,11... | collective-permute-start | bytes 393224 | tf_op jit(solution)/shard_map/ppermute | solution.py:350
  36.9 12.6 %collective-permute-start.14 = (f32[128,128]{1,0:T(8,128)S(1)}, f32[128,128]{1,0:T(8,128)S(1)}, u32[]{:S(2)}, u32[]{:S(2)}) collective-permute-start(f32[128,128]{1,0:T(8,128)S(1)} %fusion.7), channel_id=1, source_target_pairs={{0,2},{1,3},{2,0},{3,1},{4,6},{5,7},{6,4},{7,5},{8,10},{9,11},{10,... | collective-permute-start | bytes 196616 | tf_op jit(solution)/shard_map/ppermute | solution.py:350
  39.8 9.7 %collective-permute-start.16 = (f32[128,128]{1,0:T(8,128)S(1)}, f32[128,128]{1,0:T(8,128)S(1)}, u32[]{:S(2)}, u32[]{:S(2)}) collective-permute-start(f32[128,128]{1,0:T(8,128)S(1)} %fusion.5), channel_id=1, source_target_pairs={{0,2},{1,3},{2,0},{3,1},{4,6},{5,7},{6,4},{7,5},{8,10},{9,11},{10,... | collective-permute-start | bytes 196616 | tf_op jit(solution)/shard_map/ppermute | solution.py:350
  45.3 9.2 %collective-permute-start.4 = (f32[128,128]{1,0:T(8,128)S(1)}, f32[128,128]{1,0:T(8,128)S(1)}, u32[]{:S(2)}, u32[]{:S(2)}) collective-permute-start(f32[128,128]{1,0:T(8,128)S(1)} %fusion.11), channel_id=1, source_target_pairs={{0,2},{1,3},{2,0},{3,1},{4,6},{5,7},{6,4},{7,5},{8,10},{9,11},{10,... | collective-permute-start | bytes 196616 | tf_op jit(solution)/shard_map/ppermute | solution.py:350
  47.9 9.9 %collective-permute-start.6 = (f32[128,128]{1,0:T(8,128)S(1)}, f32[128,128]{1,0:T(8,128)S(1)}, u32[]{:S(2)}, u32[]{:S(2)}) collective-permute-start(f32[128,128]{1,0:T(8,128)S(1)} %fusion.9), channel_id=1, source_target_pairs={{0,2},{1,3},{2,0},{3,1},{4,6},{5,7},{6,4},{7,5},{8,10},{9,11},{10,... | collective-permute-start | bytes 196616 | tf_op jit(solution)/shard_map/ppermute | solution.py:350
  49.6 10.2 %collective-permute-start.17 = (bf16[2,128,128]{2,1,0:T(8,128)(2,1)S(1)}, bf16[2,128,128]{2,1,0:T(8,128)(2,1)S(1)}, u32[]{:S(2)}, u32[]{:S(2)}) collective-permute-start(bf16[2,128,128]{2,1,0:T(8,128)(2,1)S(1)} %pad_maximum_fusion.1.refs_4_), channel_id=1, source_target_pairs={{0,1},{1,0},{2,3},{3,2},{4,5},{5,4},{6,7},{7,6},{8,9},{9,8},{10,11... | collective-permute-start | bytes 196616 | tf_op jit(solution)/shard_map/ppermute | solution.py:381
  52.1 13.7 %collective-permute-start.18 = (bf16[2,128,128]{2,1,0:T(8,128)(2,1)S(1)}, bf16[2,128,128]{2,1,0:T(8,128)(2,1)S(1)}, u32[]{:S(2)}, u32[]{:S(2)}) collective-permute-start(bf16[2,128,128]{2,1,0:T(8,128)(2,1)S(1)} %pad_maximum_fusion.1.refs_4_), channel_id=1, source_target_pairs={{0,2},{1,3},{2,0},{3,1},{4,6},{5,7},{6,4},{7,5},{8,10},{9,11},{10,... | collective-permute-start | bytes 196616 | tf_op jit(solution)/shard_map/ppermute | solution.py:381
  53.7 12.1 %collective-permute-start.19 = (bf16[2,128,128]{2,1,0:T(8,128)(2,1)S(1)}, bf16[2,128,128]{2,1,0:T(8,128)(2,1)S(1)}, u32[]{:S(2)}, u32[]{:S(2)}) collective-permute-start(bf16[2,128,128]{2,1,0:T(8,128)(2,1)S(1)} %pad_maximum_fusion.1.refs_4_), channel_id=1, source_target_pairs={{0,3},{1,2},{2,1},{3,0},{4,7},{5,6},{6,5},{7,4},{8,11},{9,10},{10,... | collective-permute-start | bytes 196616 | tf_op jit(solution)/shard_map/ppermute | solution.py:381
  57.8 8.4 %copy-start.3 = (s32[2]{0:T(128)S(1)}, s32[2]{0:T(128)}, u32[]{:S(2)}) copy-start(s32[2]{0:T(128)} %pick_ref.1) | copy-start | bytes 28
  57.8 8.4 %copy-start.4 = (bf16[512,512]{1,0:T(8,128)(2,1)S(1)}, bf16[512,512]{1,0:T(8,128)(2,1)}, u32[]{:S(2)}) copy-start(bf16[512,512]{1,0:T(8,128)(2,1)} %constant.59.clone.table_ref) | copy-start | bytes 1572868
  57.8 8.0 %collective-permute-start.7 = (bf16[2,128,128]{2,1,0:T(8,128)(2,1)S(1)}, bf16[2,128,128]{2,1,0:T(8,128)(2,1)S(1)}, u32[]{:S(2)}, u32[]{:S(2)}) collective-permute-start(bf16[2,128,128]{2,1,0:T(8,128)(2,1)S(1)} %pad_maximum_fusion.refs_0_), channel_id=1, source_target_pairs={{0,1},{1,0},{2,3},{3,2},{4,5},{5,4},{6,7},{7,6},{8,9},{9,8},{10,11... | collective-permute-start | bytes 196616 | tf_op jit(solution)/shard_map/ppermute | solution.py:381
  57.9 8.3 %collective-permute-start.8 = (bf16[2,128,128]{2,1,0:T(8,128)(2,1)S(1)}, bf16[2,128,128]{2,1,0:T(8,128)(2,1)S(1)}, u32[]{:S(2)}, u32[]{:S(2)}) collective-permute-start(bf16[2,128,128]{2,1,0:T(8,128)(2,1)S(1)} %pad_maximum_fusion.refs_0_), channel_id=1, source_target_pairs={{0,2},{1,3},{2,0},{3,1},{4,6},{5,7},{6,4},{7,5},{8,10},{9,11},{10,... | collective-permute-start | bytes 196616 | tf_op jit(solution)/shard_map/ppermute | solution.py:381
  59.8 6.4 %collective-permute-start.9 = (bf16[2,128,128]{2,1,0:T(8,128)(2,1)S(1)}, bf16[2,128,128]{2,1,0:T(8,128)(2,1)S(1)}, u32[]{:S(2)}, u32[]{:S(2)}) collective-permute-start(bf16[2,128,128]{2,1,0:T(8,128)(2,1)S(1)} %pad_maximum_fusion.refs_0_), channel_id=1, source_target_pairs={{0,3},{1,2},{2,1},{3,0},{4,7},{5,6},{6,5},{7,4},{8,11},{9,10},{10,... | collective-permute-start | bytes 196616 | tf_op jit(solution)/shard_map/ppermute | solution.py:381

commit v5 on v4

--- a/solution.py
+++ b/solution.py
@@ -97,8 +97,8 @@
 
 
 def prep_kernel(wides, offset_ref, place_ref, strips_hbm, rest_ref, *refs):
-    own_refs = refs[:CHUNKS]
-    fine, fine_at, base, base_at, held, strips_ref, arrival = refs[CHUNKS:]
+    own_refs, ramp_ref = refs[:CHUNKS], refs[CHUNKS]
+    fine, fine_at, base, base_at, held, strips_ref, arrival = refs[CHUNKS + 1 :]
     chips = wides // 2
     shift_at = functools.partial(shift_of, offset_ref, place_ref, wides)
     length = strips_ref.shape[1]
@@ -154,6 +154,9 @@
             rest_ref[facet, shown, rows, pl.ds(pl.multiple_of(start, WIDTH), WIDTH)] = cosine
             rest_ref[facet, shown, rows, pl.ds(pl.multiple_of(start + length, WIDTH), WIDTH)] = sine
 
+        ramp_c, ramp_s = ramp_of(shift_at(facet + 1, shown, 1))
+        ramp_ref[facet, shown, 0:1] = ramp_c
+        ramp_ref[facet, shown, 1:2] = ramp_s
         make_factor(facet + 1, shown, store)
         return carry
 
@@ -179,26 +182,30 @@
     lax.fori_loop(0, SHOWN, own_step, 0)
 
 
-def chunk_kernel(chunk, wides, offset_ref, place_ref, rest_ref, own_ref, *refs):
+def chunk_kernel(chunk, wides, place_ref, rest_ref, ramp_ref, own_ref, *refs):
     hops = wides // 2 - 1
     targets, whole = refs[-5:-1], refs[-1]
     rows_dev = targets[0].shape[-2]
     groups = SUBW // (2 * rows_dev)
     mine = place_ref[2] & 1
     lanes = slice(chunk * LANES, (chunk + 1) * LANES)
-    length = refs[0].shape[1]
+    stacked = [
+        jnp.concatenate(
+            [
+                jnp.concatenate([refs[hop][0], refs[hop][1]], axis=1),
+                jnp.concatenate([refs[hop][1], -refs[hop][0]], axis=1),
+            ],
+            axis=0,
+        )
+        for hop in range(hops)
+    ]
     for shown in range(SHOWN):
         total = own_ref[shown]
         for hop in range(hops):
-            data = jnp.concatenate([refs[hop][0], refs[hop][1]], axis=1)
-            ramp_c, ramp_s = ramp_of(shift_of(offset_ref, place_ref, wides, hop + 1, shown, 1))
-            direct = jnp.dot(
-                rest_ref[hop, shown, :, :length], data, preferred_element_type=jnp.float32
-            )
-            crossed = jnp.dot(
-                rest_ref[hop, shown, :, length:], data, preferred_element_type=jnp.float32
-            )
-            total = total + ramped(direct, crossed, ramp_c[:, lanes], ramp_s[:, lanes])
+            ramp_c = ramp_ref[hop, shown, 0:1, lanes]
+            ramp_s = ramp_ref[hop, shown, 1:2, lanes]
+            part = jnp.dot(rest_ref[hop, shown], stacked[hop], preferred_element_type=jnp.float32)
+            total = total + part * ramp_c + swap_halves(part) * ramp_s
         whole[...] = total
         for group in range(groups):
             index = shown % SG_WIDE * groups + group
@@ -288,14 +295,15 @@
 
     place = jnp.stack([pair_id * length, wide_id, pair_id])
 
-    rest, *own = pl.pallas_call(
+    rest, *own, ramps = pl.pallas_call(
         functools.partial(prep_kernel, wides),
         out_shape=[
             jax.ShapeDtypeStruct((chips - 1, SHOWN, SUBW, 2 * length), jnp.bfloat16),
         ]
-        + [jax.ShapeDtypeStruct((SHOWN, SUBW, LANES), jnp.float32)] * CHUNKS,
+        + [jax.ShapeDtypeStruct((SHOWN, SUBW, LANES), jnp.float32)] * CHUNKS
+        + [jax.ShapeDtypeStruct((chips - 1, SHOWN, 2, 2 * SUBW), jnp.float32)],
         in_specs=[in_smem, in_smem, anywhere],
-        out_specs=[in_vmem] * (1 + CHUNKS),
+        out_specs=[in_vmem] * (2 + CHUNKS),
         scratch_shapes=[
             pltpu.VMEM((2, FINE, length), jnp.float32),
             pltpu.VMEM((FINE, length), jnp.int32),
@@ -316,13 +324,13 @@
         sums = pl.pallas_call(
             functools.partial(chunk_kernel, index, wides),
             out_shape=[jax.ShapeDtypeStruct((PARTS, pairs // 2, rows_dev, PART), jnp.float32)] * 4,
-            in_specs=[in_smem, in_smem] + [in_vmem] * (chips + 1),
+            in_specs=[in_smem] + [in_vmem] * (chips + 2),
             out_specs=[in_vmem] * 4,
             scratch_shapes=[pltpu.VMEM((SUBW, LANES), jnp.float32)],
             compiler_params=params,
             cost_estimate=cost(2420000000),
             name="chunk_sums",
-        )(offsets, place, rest, own[index], *arrived[index])
+        )(place, rest, ramps, own[index], *arrived[index])
         shape = (2,) * (bits - 1) + (rows_dev, PART)
         cores = [(w, w ^ 1) for w in range(wides)]
         keep_pass, keep_hold, send_pass, send_hold = sums

time: 69.8 us -> 69.5 us (level)
  transfers between devices with their start and end apart: 20 -> 20, of which waited for: 7 -> 7; matrix products, arithmetic and copies ran while one was open for 2% -> 2% of each run, Pallas kernels for 27% -> 26%
where the time goes in v5:
time: 69.5 us; the launch traced here: 69.3 us
  starting transfers between devices  25.9 us (37%)
  Pallas kernels  21.5 us (31%)
  waiting for transfers between devices  18 us (26%)
  local copies, waits for them, and re-layouts  3.3 us (5%)
    ppermute x8, starting transfers between devices, exchange(): lax.ppermute(passed, 'pair', [(p, p ^ 1 << bit) for p in range(pairs)])  12.6 us
    pallas_call x1, Pallas kernels, on_device(): pl.pallas_call(functools.partial(prep_kernel, wides), out_shape=[jax.Shap...  10.5 us
    ppermute x6, starting transfers between devices, on_device(): lax.ppermute(parts[0], 'pair', [(p, p ^ step) for p in range(pairs)])  9.43 us
    ppermute x8, waiting for transfers between devices, exchange(): lax.ppermute(passed, 'pair', [(p, p ^ 1 << bit) for p in range(pairs)])  9.31 us
    ppermute x2, waiting for transfers between devices, on_device(): lax.ppermute(part, 'wide', [(w, (w + 2 * hop) % wides) for w in range(wid...  8.32 us
    pallas_call x2, Pallas kernels, start_chunk(): pl.pallas_call(functools.partial(chunk_kernel, index, wides), out_shape=[...  4.1 us
    pallas_call x1, Pallas kernels, on_device(): pl.pallas_call(weight_kernel, out_shape=[jax.ShapeDtypeStruct((blocks, SU...  3.55 us
    pallas_call x1, Pallas kernels, on_device(): pl.pallas_call(functools.partial(degrid_kernel, pairs), out_shape=jax.Sha...  3.38 us
  transfers between devices with their start and end apart: 20, of which 7 were waited for; matrix products, arithmetic and copies ran while one was open for 2% of the time, Pallas kernels for 26%

profile of v5, /device:TPU:0, one launch (start us, length us, event | category | flops | bytes accessed | tf_op | source)
XLA Modules:
  0.0 69.3 jit_solution(16015185962107022422)
XLA Ops:
  0.0 1.3 %fusion.16 = (bf16[2,1024,128]{2,1,0:T(8,128)(2,1)S(1)}, bf16[2,1024,128]{2,1,0:T(8,128)(2,1)S(1)}) fusion(bf16[2,1024,256]{2,1,0:T(8,128)(2,1)} %bitcast.92), kind=kLoop, calls=%fused_computation.39 | loop fusion | bytes 2097152 | tf_op jit(solution)/shard_map/slice | solution.py:288
  1.3 3.0 %collective-permute-start.10 = (bf16[2,1024,128]{2,1,0:T(8,128)(2,1)S(1)}, bf16[2,1024,128]{2,1,0:T(8,128)(2,1)S(1)}, u32[]{:S(2)}, u32[]{:S(2)}) collective-permute-start(bf16[2,1024,128]{2,1,0:T(8,128)(2,1)S(1)} %get-tuple-element.33), channel_id=1, source_target_pairs={{0,8},{4,12},{8,0},{12,4},{1,9},{5,13},{9,1},{13,5},{2,10},{6,14},... | collective-permute-start | bytes 1572872 | tf_op jit(solution)/shard_map/ppermute | solution.py:291
  4.3 0.1 collective-permute-start
  4.4 0.8 %copy.7.offset_ref = s32[8,4,2]{2,1,0:T(4,128)S(1)} copy(s32[8,4,2]{0,2,1:T(2,128)} %param.7) | data formatting | bytes 512 | tf_op args[1]
  5.2 0.1 pad_add_fusion.place_ref
  5.3 1.2 %copy-done = bf16[1,2,1024,256]{3,2,1,0:T(8,128)(2,1)S(1)} copy-done((bf16[1,2,1024,256]{3,2,1,0:T(8,128)(2,1)S(1)}, bf16[1,2,1024,256]{3,2,1,0:T(8,128)(2,1)}, u32[]{:S(2)}) %copy-start) | copy-done | bytes 1048600
  6.5 10.5 %prepare.1 = (bf16[1,4,256,2048]{3,2,1,0:T(8,128)(2,1)S(1)}, f32[4,256,256]{2,1,0:T(8,128)S(1)}, f32[4,256,256]{2,1,0:T(8,128)S(1)}, f32[1,4,2,512]{3,2,1,0:T(2,128)S(1)}) custom-call(s32[8,4,2]{2,1,0:T(4,128)S(1)} %copy.7.offset_ref, s32[3]{0:T(128)S(1)} %pad_add_fusion.place_ref, bf16[2,1024,256]{2,1,0:T(8,128)(2,1)S(1)} %bitcast.93), custom_call_target="tpu_custom_call" | custom-call | flops 12099999744 | bytes 1048576 | tf_op jit(solution)/shard_map/prepare/pallas_call | solution.py:298
  17.0 0.1 collective-permute-done.10.refs_0_
  17.1 2.1 %chunk_sums.3 = (f32[2,2,128,128]{3,2,1,0:T(8,128)S(1)}, f32[2,2,128,128]{3,2,1,0:T(8,128)S(1)}, f32[2,2,128,128]{3,2,1,0:T(8,128)S(1)}, f32[2,2,128,128]{3,2,1,0:T(8,128)S(1)}) custom-call(s32[3]{0:T(128)S(1)} %pad_add_fusion.place_ref, bf16[1,4,256,2048]{3,2,1,0:T(8,128)(2,1)S(1)} %get-tuple-element.21.rest_ref, ...), custom_call_target="tpu_custom_call" | custom-call | flops 2420000000 | bytes 1048576 | tf_op jit(solution)/shard_map/chunk_sums/pallas_call | solution.py:324
  19.1 0.1 collective-permute-start.11
  19.2 8.3 %collective-permute-done.refs_0_ = bf16[2,1024,128]{2,1,0:T(8,128)(2,1)S(1)} collective-permute-done((bf16[2,1024,128]{2,1,0:T(8,128)(2,1)S(1)}, bf16[2,1024,128]{2,1,0:T(8,128)(2,1)S(1)}, u32[]{:S(2)}, u32[]{:S(2)}) %collective-permute-start) | collective-permute-done | bytes 524320 | tf_op jit(solution)/shard_map/ppermute | solution.py:291
  27.5 2.0 %chunk_sums.2 = (f32[2,2,128,128]{3,2,1,0:T(8,128)S(1)}, f32[2,2,128,128]{3,2,1,0:T(8,128)S(1)}, f32[2,2,128,128]{3,2,1,0:T(8,128)S(1)}, f32[2,2,128,128]{3,2,1,0:T(8,128)S(1)}) custom-call(s32[3]{0:T(128)S(1)} %pad_add_fusion.place_ref, bf16[1,4,256,2048]{3,2,1,0:T(8,128)(2,1)S(1)} %get-tuple-element.21.rest_ref, ...), custom_call_target="tpu_custom_call" | custom-call | flops 2420000000 | bytes 1048576 | tf_op jit(solution)/shard_map/chunk_sums/pallas_call | solution.py:324
  29.5 0.0 copy-start.1
  29.5 0.0 copy-start.2
  29.5 0.1 collective-permute-start.1
  29.6 0.5 collective-permute-start.13
  30.1 0.1 collective-permute-start.3
  30.2 0.0 collective-permute-done.11
  30.2 1.9 %collective-permute-start.12 = (f32[2,128,128]{2,1,0:T(8,128)S(1)}, f32[2,128,128]{2,1,0:T(8,128)S(1)}, u32[]{:S(2)}, u32[]{:S(2)}) collective-permute-start(f32[2,128,128]{2,1,0:T(8,128)S(1)} %get-tuple-element.35), channel_id=1, source_target_pairs={{0,1},{1,0},{2,3},{3,2},{4,5},{5,4},{6,7},{7,6},{8,9},{9,8},{10,11... | collective-permute-start | bytes 393224 | tf_op jit(solution)/shard_map/ppermute | solution.py:358
  32.1 0.2 collective-permute-start.15
  32.3 0.0 collective-permute-done.1
  32.4 1.9 %collective-permute-start.2 = (f32[2,128,128]{2,1,0:T(8,128)S(1)}, f32[2,128,128]{2,1,0:T(8,128)S(1)}, u32[]{:S(2)}, u32[]{:S(2)}) collective-permute-start(f32[2,128,128]{2,1,0:T(8,128)S(1)} %get-tuple-element.39), channel_id=1, source_target_pairs={{0,1},{1,0},{2,3},{3,2},{4,5},{5,4},{6,7},{7,6},{8,9},{9,8},{10,11... | collective-permute-start | bytes 393224 | tf_op jit(solution)/shard_map/ppermute | solution.py:358
  34.2 0.0 collective-permute-done.13
  34.2 0.2 collective-permute-start.5
  34.5 0.0 collective-permute-done.3
  34.6 2.0 %collective-permute-done.12 = f32[2,128,128]{2,1,0:T(8,128)S(1)} collective-permute-done((f32[2,128,128]{2,1,0:T(8,128)S(1)}, f32[2,128,128]{2,1,0:T(8,128)S(1)}, u32[]{:S(2)}, u32[]{:S(2)}) %collective-permute-start.12) | collective-permute-done | bytes 131104 | tf_op jit(solution)/shard_map/ppermute | solution.py:358
  36.6 2.9 %collective-permute-start.14 = (f32[128,128]{1,0:T(8,128)S(1)}, f32[128,128]{1,0:T(8,128)S(1)}, u32[]{:S(2)}, u32[]{:S(2)}) collective-permute-start(f32[128,128]{1,0:T(8,128)S(1)} %fusion.7), channel_id=1, source_target_pairs={{0,2},{1,3},{2,0},{3,1},{4,6},{5,7},{6,4},{7,5},{8,10},{9,11},{10,... | collective-permute-start | bytes 196616 | tf_op jit(solution)/shard_map/ppermute | solution.py:358
  39.5 2.8 %collective-permute-start.16 = (f32[128,128]{1,0:T(8,128)S(1)}, f32[128,128]{1,0:T(8,128)S(1)}, u32[]{:S(2)}, u32[]{:S(2)}) collective-permute-start(f32[128,128]{1,0:T(8,128)S(1)} %fusion.5), channel_id=1, source_target_pairs={{0,2},{1,3},{2,0},{3,1},{4,6},{5,7},{6,4},{7,5},{8,10},{9,11},{10,... | collective-permute-start | bytes 196616 | tf_op jit(solution)/shard_map/ppermute | solution.py:358
  42.3 2.7 %collective-permute-done.2 = f32[2,128,128]{2,1,0:T(8,128)S(1)} collective-permute-done((f32[2,128,128]{2,1,0:T(8,128)S(1)}, f32[2,128,128]{2,1,0:T(8,128)S(1)}, u32[]{:S(2)}, u32[]{:S(2)}) %collective-permute-start.2) | collective-permute-done | bytes 131104 | tf_op jit(solution)/shard_map/ppermute | solution.py:358
  45.0 1.2 %collective-permute-start.4 = (f32[128,128]{1,0:T(8,128)S(1)}, f32[128,128]{1,0:T(8,128)S(1)}, u32[]{:S(2)}, u32[]{:S(2)}) collective-permute-start(f32[128,128]{1,0:T(8,128)S(1)} %fusion.11), channel_id=1, source_target_pairs={{0,2},{1,3},{2,0},{3,1},{4,6},{5,7},{6,4},{7,5},{8,10},{9,11},{10,... | collective-permute-start | bytes 196616 | tf_op jit(solution)/shard_map/ppermute | solution.py:358
  46.2 1.4 %collective-permute-done.5 = f32[2,128,128]{2,1,0:T(8,128)S(1)} collective-permute-done((f32[2,128,128]{2,1,0:T(8,128)S(1)}, f32[2,128,128]{2,1,0:T(8,128)S(1)}, u32[]{:S(2)}, u32[]{:S(2)}) %collective-permute-start.5) | collective-permute-done | bytes 131104 | tf_op jit(solution)/shard_map/ppermute | solution.py:358
  47.6 1.6 %collective-permute-start.6 = (f32[128,128]{1,0:T(8,128)S(1)}, f32[128,128]{1,0:T(8,128)S(1)}, u32[]{:S(2)}, u32[]{:S(2)}) collective-permute-start(f32[128,128]{1,0:T(8,128)S(1)} %fusion.9), channel_id=1, source_target_pairs={{0,2},{1,3},{2,0},{3,1},{4,6},{5,7},{6,4},{7,5},{8,10},{9,11},{10,... | collective-permute-start | bytes 196616 | tf_op jit(solution)/shard_map/ppermute | solution.py:358
  49.2 0.0 collective-permute-done.14
  49.3 2.5 %collective-permute-start.17 = (bf16[2,128,128]{2,1,0:T(8,128)(2,1)S(1)}, bf16[2,128,128]{2,1,0:T(8,128)(2,1)S(1)}, u32[]{:S(2)}, u32[]{:S(2)}) collective-permute-start(bf16[2,128,128]{2,1,0:T(8,128)(2,1)S(1)} %pad_maximum_fusion.1.refs_4_), channel_id=1, source_target_pairs={{0,1},{1,0},{2,3},{3,2},{4,5},{5,4},{6,7},{7,6},{8,9},{9,8},{10,11... | collective-permute-start | bytes 196616 | tf_op jit(solution)/shard_map/ppermute | solution.py:389
  51.8 1.6 %collective-permute-start.18 = (bf16[2,128,128]{2,1,0:T(8,128)(2,1)S(1)}, bf16[2,128,128]{2,1,0:T(8,128)(2,1)S(1)}, u32[]{:S(2)}, u32[]{:S(2)}) collective-permute-start(bf16[2,128,128]{2,1,0:T(8,128)(2,1)S(1)} %pad_maximum_fusion.1.refs_4_), channel_id=1, source_target_pairs={{0,2},{1,3},{2,0},{3,1},{4,6},{5,7},{6,4},{7,5},{8,10},{9,11},{10,... | collective-permute-start | bytes 196616 | tf_op jit(solution)/shard_map/ppermute | solution.py:389
  53.5 0.8 %collective-permute-start.19 = (bf16[2,128,128]{2,1,0:T(8,128)(2,1)S(1)}, bf16[2,128,128]{2,1,0:T(8,128)(2,1)S(1)}, u32[]{:S(2)}, u32[]{:S(2)}) collective-permute-start(bf16[2,128,128]{2,1,0:T(8,128)(2,1)S(1)} %pad_maximum_fusion.1.refs_4_), channel_id=1, source_target_pairs={{0,3},{1,2},{2,1},{3,0},{4,7},{5,6},{6,5},{7,4},{8,11},{9,10},{10,... | collective-permute-start | bytes 196616 | tf_op jit(solution)/shard_map/ppermute | solution.py:389
  54.3 3.2 %collective-permute-done.6 = f32[128,128]{1,0:T(8,128)S(1)} collective-permute-done((f32[128,128]{1,0:T(8,128)S(1)}, f32[128,128]{1,0:T(8,128)S(1)}, u32[]{:S(2)}, u32[]{:S(2)}) %collective-permute-start.6) | collective-permute-done | bytes 65568 | tf_op jit(solution)/shard_map/ppermute | solution.py:358
  57.5 0.0 copy-start.3
  57.5 0.0 copy-start.4
  57.5 0.1 collective-permute-start.7
  57.6 1.9 %collective-permute-start.8 = (bf16[2,128,128]{2,1,0:T(8,128)(2,1)S(1)}, bf16[2,128,128]{2,1,0:T(8,128)(2,1)S(1)}, u32[]{:S(2)}, u32[]{:S(2)}) collective-permute-start(bf16[2,128,128]{2,1,0:T(8,128)(2,1)S(1)} %pad_maximum_fusion.refs_0_), channel_id=1, source_target_pairs={{0,2},{1,3},{2,0},{3,1},{4,6},{5,7},{6,4},{7,5},{8,10},{9,11},{10,... | collective-permute-start | bytes 196616 | tf_op jit(solution)/shard_map/ppermute | solution.py:389
  59.5 0.0 collective-permute-done.17.refs_5_
  59.5 2.5 %collective-permute-start.9 = (bf16[2,128,128]{2,1,0:T(8,128)(2,1)S(1)}, bf16[2,128,128]{2,1,0:T(8,128)(2,1)S(1)}, u32[]{:S(2)}, u32[]{:S(2)}) collective-permute-start(bf16[2,128,128]{2,1,0:T(8,128)(2,1)S(1)} %pad_maximum_fusion.refs_0_), channel_id=1, source_target_pairs={{0,3},{1,2},{2,1},{3,0},{4,7},{5,6},{6,5},{7,4},{8,11},{9,10},{10,... | collective-permute-start | bytes 196616 | tf_op jit(solution)/shard_map/ppermute | solution.py:389
  62.0 3.5 %weights.1 = (bf16[2,256,2048]{2,1,0:T(8,128)(2,1)S(1)}, f32[2,256,2048]{2,1,0:T(8,128)S(1)}) custom-call(s32[2,2]{1,0:T(2,128)S(1)} %copy-done.2, s32[2,2,2048]{2,1,0:T(2,128)S(1)} %copy-done.1), custom_call_target="tpu_custom_call" | custom-call | flops 5500000256 | bytes 1048576 | tf_op jit(solution)/shard_map/weights/pallas_call | solution.py:366
  65.5 0.0 collective-permute-done.19.refs_7_
  65.6 0.0 collective-permute-done.7.refs_1_
  65.6 0.3 collective-permute-done.8.refs_2_
  65.9 3.4 %degrid.1 = f32[2,2,2048]{2,1,0:T(2,128)} custom-call(s32[3]{0:T(128)S(1)} %pad_add_fusion.place_ref, s32[2]{0:T(128)S(1)} %copy-done.3, bf16[2,256,2048]{2,1,0:T(8,128)(2,1)S(1)} %get-tuple-element.19.row_ref, f32[2,256,2048]{2,1,0:T(8,128)S(1)} %get-tuple-element.20.col_ref, bf16[512,512]{1,0:T(8,128)(2,1)S(1)} %copy-done.4, ...), custom_call_target="tpu_custom_call" | custom-call | flops 3300000000 | bytes 1048576 | tf_op jit(solution)/shard_map/degrid/pallas_call | solution.py:392
  (24 shorter events, 0.3 us)
Async XLA Ops:
  1.3 15.8 %collective-permute-start.10 = (bf16[2,1024,128]{2,1,0:T(8,128)(2,1)S(1)}, bf16[2,1024,128]{2,1,0:T(8,128)(2,1)S(1)}, u32[]{:S(2)}, u32[]{:S(2)}) collective-permute-start(bf16[2,1024,128]{2,1,0:T(8,128)(2,1)S(1)} %get-tuple-element.33), channel_id=1, source_target_pairs={{0,8},{4,12},{8,0},{12,4},{1,9},{5,13},{9,1},{13,5},{2,10},{6,14},... | collective-permute-start | bytes 1572872 | tf_op jit(solution)/shard_map/ppermute | solution.py:291
  4.3 23.2 %collective-permute-start = (bf16[2,1024,128]{2,1,0:T(8,128)(2,1)S(1)}, bf16[2,1024,128]{2,1,0:T(8,128)(2,1)S(1)}, u32[]{:S(2)}, u32[]{:S(2)}) collective-permute-start(bf16[2,1024,128]{2,1,0:T(8,128)(2,1)S(1)} %get-tuple-element.34), channel_id=1, source_target_pairs={{0,8},{4,12},{8,0},{12,4},{1,9},{5,13},{9,1},{13,5},{2,10},{6,14},... | collective-permute-start | bytes 1572872 | tf_op jit(solution)/shard_map/ppermute | solution.py:291
  5.2 1.2 %copy-start = (bf16[1,2,1024,256]{3,2,1,0:T(8,128)(2,1)S(1)}, bf16[1,2,1024,256]{3,2,1,0:T(8,128)(2,1)}, u32[]{:S(2)}) copy-start(bf16[1,2,1024,256]{3,2,1,0:T(8,128)(2,1)} %param.6) | copy-start | bytes 3145732
  19.1 11.1 %collective-permute-start.11 = (f32[2,2,128,128]{3,2,1,0:T(8,128)S(1)}, f32[2,2,128,128]{3,2,1,0:T(8,128)S(1)}, u32[]{:S(2)}, u32[]{:S(2)}) collective-permute-start(f32[2,2,128,128]{3,2,1,0:T(8,128)S(1)} %get-tuple-element.30), channel_id=1, source_target_pairs={{0,4},{4,0},{8,12},{12,8},{1,5},{5,1},{9,13},{13,9},{2,6},{6,2},{1... | collective-permute-start | bytes 786440 | tf_op jit(solution)/shard_map/ppermute | solution.py:337
  29.5 32.5 %copy-start.1 = (s32[2,2,2048]{2,1,0:T(2,128)S(1)}, s32[2,2,2048]{2,1,0:T(2,128)}, u32[]{:S(2)}) copy-start(s32[2,2,2048]{2,1,0:T(2,128)} %cells_ref.1) | copy-start | bytes 98308
  29.5 32.5 %copy-start.2 = (s32[2,2]{1,0:T(2,128)S(1)}, s32[2,2]{1,0:T(2,128)}, u32[]{:S(2)}) copy-start(s32[2,2]{1,0:T(2,128)} %fraction_ref.1) | copy-start | bytes 52
  29.5 2.8 %collective-permute-start.1 = (f32[2,2,128,128]{3,2,1,0:T(8,128)S(1)}, f32[2,2,128,128]{3,2,1,0:T(8,128)S(1)}, u32[]{:S(2)}, u32[]{:S(2)}) collective-permute-start(f32[2,2,128,128]{3,2,1,0:T(8,128)S(1)} %get-tuple-element.25), channel_id=1, source_target_pairs={{0,4},{4,0},{8,12},{12,8},{1,5},{5,1},{9,13},{13,9},{2,6},{6,2},{1... | collective-permute-start | bytes 786440 | tf_op jit(solution)/shard_map/ppermute | solution.py:337
  29.6 4.6 %collective-permute-start.13 = (f32[2,2,128,128]{3,2,1,0:T(8,128)S(1)}, f32[2,2,128,128]{3,2,1,0:T(8,128)S(1)}, u32[]{:S(2)}, u32[]{:S(2)}) collective-permute-start(f32[2,2,128,128]{3,2,1,0:T(8,128)S(1)} %get-tuple-element.32), channel_id=1, source_target_pairs={{0,4},{4,0},{8,12},{12,8},{1,5},{5,1},{9,13},{13,9},{2,6},{6,2},{1... | collective-permute-start | bytes 786440 | tf_op jit(solution)/shard_map/ppermute | solution.py:338
  30.1 4.4 %collective-permute-start.3 = (f32[2,2,128,128]{3,2,1,0:T(8,128)S(1)}, f32[2,2,128,128]{3,2,1,0:T(8,128)S(1)}, u32[]{:S(2)}, u32[]{:S(2)}) collective-permute-start(f32[2,2,128,128]{3,2,1,0:T(8,128)S(1)} %get-tuple-element.27), channel_id=1, source_target_pairs={{0,4},{4,0},{8,12},{12,8},{1,5},{5,1},{9,13},{13,9},{2,6},{6,2},{1... | collective-permute-start | bytes 786440 | tf_op jit(solution)/shard_map/ppermute | solution.py:338
  30.2 6.4 %collective-permute-start.12 = (f32[2,128,128]{2,1,0:T(8,128)S(1)}, f32[2,128,128]{2,1,0:T(8,128)S(1)}, u32[]{:S(2)}, u32[]{:S(2)}) collective-permute-start(f32[2,128,128]{2,1,0:T(8,128)S(1)} %get-tuple-element.35), channel_id=1, source_target_pairs={{0,1},{1,0},{2,3},{3,2},{4,5},{5,4},{6,7},{7,6},{8,9},{9,8},{10,11... | collective-permute-start | bytes 393224 | tf_op jit(solution)/shard_map/ppermute | solution.py:358
  32.1 7.4 %collective-permute-start.15 = (f32[2,128,128]{2,1,0:T(8,128)S(1)}, f32[2,128,128]{2,1,0:T(8,128)S(1)}, u32[]{:S(2)}, u32[]{:S(2)}) collective-permute-start(f32[2,128,128]{2,1,0:T(8,128)S(1)} %get-tuple-element.36), channel_id=1, source_target_pairs={{0,1},{1,0},{2,3},{3,2},{4,5},{5,4},{6,7},{7,6},{8,9},{9,8},{10,11... | collective-permute-start | bytes 393224 | tf_op jit(solution)/shard_map/ppermute | solution.py:358
  32.4 12.7 %collective-permute-start.2 = (f32[2,128,128]{2,1,0:T(8,128)S(1)}, f32[2,128,128]{2,1,0:T(8,128)S(1)}, u32[]{:S(2)}, u32[]{:S(2)}) collective-permute-start(f32[2,128,128]{2,1,0:T(8,128)S(1)} %get-tuple-element.39), channel_id=1, source_target_pairs={{0,1},{1,0},{2,3},{3,2},{4,5},{5,4},{6,7},{7,6},{8,9},{9,8},{10,11... | collective-permute-start | bytes 393224 | tf_op jit(solution)/shard_map/ppermute | solution.py:358
  34.2 13.3 %collective-permute-start.5 = (f32[2,128,128]{2,1,0:T(8,128)S(1)}, f32[2,128,128]{2,1,0:T(8,128)S(1)}, u32[]{:S(2)}, u32[]{:S(2)}) collective-permute-start(f32[2,128,128]{2,1,0:T(8,128)S(1)} %get-tuple-element.40), channel_id=1, source_target_pairs={{0,1},{1,0},{2,3},{3,2},{4,5},{5,4},{6,7},{7,6},{8,9},{9,8},{10,11... | collective-permute-start | bytes 393224 | tf_op jit(solution)/shard_map/ppermute | solution.py:358
  36.6 12.6 %collective-permute-start.14 = (f32[128,128]{1,0:T(8,128)S(1)}, f32[128,128]{1,0:T(8,128)S(1)}, u32[]{:S(2)}, u32[]{:S(2)}) collective-permute-start(f32[128,128]{1,0:T(8,128)S(1)} %fusion.7), channel_id=1, source_target_pairs={{0,2},{1,3},{2,0},{3,1},{4,6},{5,7},{6,4},{7,5},{8,10},{9,11},{10,... | collective-permute-start | bytes 196616 | tf_op jit(solution)/shard_map/ppermute | solution.py:358
  39.5 9.7 %collective-permute-start.16 = (f32[128,128]{1,0:T(8,128)S(1)}, f32[128,128]{1,0:T(8,128)S(1)}, u32[]{:S(2)}, u32[]{:S(2)}) collective-permute-start(f32[128,128]{1,0:T(8,128)S(1)} %fusion.5), channel_id=1, source_target_pairs={{0,2},{1,3},{2,0},{3,1},{4,6},{5,7},{6,4},{7,5},{8,10},{9,11},{10,... | collective-permute-start | bytes 196616 | tf_op jit(solution)/shard_map/ppermute | solution.py:358
  45.0 9.2 %collective-permute-start.4 = (f32[128,128]{1,0:T(8,128)S(1)}, f32[128,128]{1,0:T(8,128)S(1)}, u32[]{:S(2)}, u32[]{:S(2)}) collective-permute-start(f32[128,128]{1,0:T(8,128)S(1)} %fusion.11), channel_id=1, source_target_pairs={{0,2},{1,3},{2,0},{3,1},{4,6},{5,7},{6,4},{7,5},{8,10},{9,11},{10,... | collective-permute-start | bytes 196616 | tf_op jit(solution)/shard_map/ppermute | solution.py:358
  47.6 9.9 %collective-permute-start.6 = (f32[128,128]{1,0:T(8,128)S(1)}, f32[128,128]{1,0:T(8,128)S(1)}, u32[]{:S(2)}, u32[]{:S(2)}) collective-permute-start(f32[128,128]{1,0:T(8,128)S(1)} %fusion.9), channel_id=1, source_target_pairs={{0,2},{1,3},{2,0},{3,1},{4,6},{5,7},{6,4},{7,5},{8,10},{9,11},{10,... | collective-permute-start | bytes 196616 | tf_op jit(solution)/shard_map/ppermute | solution.py:358
  49.3 10.2 %collective-permute-start.17 = (bf16[2,128,128]{2,1,0:T(8,128)(2,1)S(1)}, bf16[2,128,128]{2,1,0:T(8,128)(2,1)S(1)}, u32[]{:S(2)}, u32[]{:S(2)}) collective-permute-start(bf16[2,128,128]{2,1,0:T(8,128)(2,1)S(1)} %pad_maximum_fusion.1.refs_4_), channel_id=1, source_target_pairs={{0,1},{1,0},{2,3},{3,2},{4,5},{5,4},{6,7},{7,6},{8,9},{9,8},{10,11... | collective-permute-start | bytes 196616 | tf_op jit(solution)/shard_map/ppermute | solution.py:389
  51.8 13.7 %collective-permute-start.18 = (bf16[2,128,128]{2,1,0:T(8,128)(2,1)S(1)}, bf16[2,128,128]{2,1,0:T(8,128)(2,1)S(1)}, u32[]{:S(2)}, u32[]{:S(2)}) collective-permute-start(bf16[2,128,128]{2,1,0:T(8,128)(2,1)S(1)} %pad_maximum_fusion.1.refs_4_), channel_id=1, source_target_pairs={{0,2},{1,3},{2,0},{3,1},{4,6},{5,7},{6,4},{7,5},{8,10},{9,11},{10,... | collective-permute-start | bytes 196616 | tf_op jit(solution)/shard_map/ppermute | solution.py:389
  53.5 12.1 %collective-permute-start.19 = (bf16[2,128,128]{2,1,0:T(8,128)(2,1)S(1)}, bf16[2,128,128]{2,1,0:T(8,128)(2,1)S(1)}, u32[]{:S(2)}, u32[]{:S(2)}) collective-permute-start(bf16[2,128,128]{2,1,0:T(8,128)(2,1)S(1)} %pad_maximum_fusion.1.refs_4_), channel_id=1, source_target_pairs={{0,3},{1,2},{2,1},{3,0},{4,7},{5,6},{6,5},{7,4},{8,11},{9,10},{10,... | collective-permute-start | bytes 196616 | tf_op jit(solution)/shard_map/ppermute | solution.py:389
  57.5 8.4 %copy-start.3 = (s32[2]{0:T(128)S(1)}, s32[2]{0:T(128)}, u32[]{:S(2)}) copy-start(s32[2]{0:T(128)} %pick_ref.1) | copy-start | bytes 28
  57.5 8.4 %copy-start.4 = (bf16[512,512]{1,0:T(8,128)(2,1)S(1)}, bf16[512,512]{1,0:T(8,128)(2,1)}, u32[]{:S(2)}) copy-start(bf16[512,512]{1,0:T(8,128)(2,1)} %constant.59.clone.table_ref) | copy-start | bytes 1572868
  57.5 8.0 %collective-permute-start.7 = (bf16[2,128,128]{2,1,0:T(8,128)(2,1)S(1)}, bf16[2,128,128]{2,1,0:T(8,128)(2,1)S(1)}, u32[]{:S(2)}, u32[]{:S(2)}) collective-permute-start(bf16[2,128,128]{2,1,0:T(8,128)(2,1)S(1)} %pad_maximum_fusion.refs_0_), channel_id=1, source_target_pairs={{0,1},{1,0},{2,3},{3,2},{4,5},{5,4},{6,7},{7,6},{8,9},{9,8},{10,11... | collective-permute-start | bytes 196616 | tf_op jit(solution)/shard_map/ppermute | solution.py:389
  57.6 8.3 %collective-permute-start.8 = (bf16[2,128,128]{2,1,0:T(8,128)(2,1)S(1)}, bf16[2,128,128]{2,1,0:T(8,128)(2,1)S(1)}, u32[]{:S(2)}, u32[]{:S(2)}) collective-permute-start(bf16[2,128,128]{2,1,0:T(8,128)(2,1)S(1)} %pad_maximum_fusion.refs_0_), channel_id=1, source_target_pairs={{0,2},{1,3},{2,0},{3,1},{4,6},{5,7},{6,4},{7,5},{8,10},{9,11},{10,... | collective-permute-start | bytes 196616 | tf_op jit(solution)/shard_map/ppermute | solution.py:389
  59.5 6.4 %collective-permute-start.9 = (bf16[2,128,128]{2,1,0:T(8,128)(2,1)S(1)}, bf16[2,128,128]{2,1,0:T(8,128)(2,1)S(1)}, u32[]{:S(2)}, u32[]{:S(2)}) collective-permute-start(bf16[2,128,128]{2,1,0:T(8,128)(2,1)S(1)} %pad_maximum_fusion.refs_0_), channel_id=1, source_target_pairs={{0,3},{1,2},{2,1},{3,0},{4,7},{5,6},{6,5},{7,4},{8,11},{9,10},{10,... | collective-permute-start | bytes 196616 | tf_op jit(solution)/shard_map/ppermute | solution.py:389

commit v6 on v5

--- a/solution.py
+++ b/solution.py
@@ -184,7 +184,7 @@
 
 def chunk_kernel(chunk, wides, place_ref, rest_ref, ramp_ref, own_ref, *refs):
     hops = wides // 2 - 1
-    targets, whole = refs[-5:-1], refs[-1]
+    targets = refs[-4:]
     rows_dev = targets[0].shape[-2]
     groups = SUBW // (2 * rows_dev)
     mine = place_ref[2] & 1
@@ -206,15 +206,16 @@
             ramp_s = ramp_ref[hop, shown, 1:2, lanes]
             part = jnp.dot(rest_ref[hop, shown], stacked[hop], preferred_element_type=jnp.float32)
             total = total + part * ramp_c + swap_halves(part) * ramp_s
-        whole[...] = total
         for group in range(groups):
             index = shown % SG_WIDE * groups + group
-            for half in range(2):
-                side = mine ^ (1 - half)
-                at = pl.multiple_of((2 * group + side) * rows_dev, rows_dev)
+            low, high = [
+                total[(2 * group + side) * rows_dev : (2 * group + side + 1) * rows_dev]
+                for side in range(2)
+            ]
+            for half, value in enumerate((jnp.where(mine == 1, low, high), jnp.where(mine == 1, high, low))):
                 for part in range(PARTS):
-                    targets[shown // SG_WIDE * 2 + half][part, index] = whole[
-                        pl.ds(at, rows_dev), part * PART : (part + 1) * PART
+                    targets[shown // SG_WIDE * 2 + half][part, index] = value[
+                        :, part * PART : (part + 1) * PART
                     ]
 
 
@@ -326,7 +327,6 @@
             out_shape=[jax.ShapeDtypeStruct((PARTS, pairs // 2, rows_dev, PART), jnp.float32)] * 4,
             in_specs=[in_smem] + [in_vmem] * (chips + 2),
             out_specs=[in_vmem] * 4,
-            scratch_shapes=[pltpu.VMEM((SUBW, LANES), jnp.float32)],
             compiler_params=params,
             cost_estimate=cost(2420000000),
             name="chunk_sums",

time: 69.5 us -> 69.3 us (level)
  no operation moved by 1% of the time
where the time goes in v6:
time: 69.3 us; the launch traced here: 69.1 us
  starting transfers between devices  25.9 us (37%)
  Pallas kernels  21.3 us (31%)
  waiting for transfers between devices  18.1 us (26%)
  local copies, waits for them, and re-layouts  3.3 us (5%)
    ppermute x8, starting transfers between devices, exchange(): lax.ppermute(passed, 'pair', [(p, p ^ 1 << bit) for p in range(pairs)])  12.6 us
    pallas_call x1, Pallas kernels, on_device(): pl.pallas_call(functools.partial(prep_kernel, wides), out_shape=[jax.Shap...  10.5 us
    ppermute x6, starting transfers between devices, on_device(): lax.ppermute(parts[0], 'pair', [(p, p ^ step) for p in range(pairs)])  9.43 us
    ppermute x8, waiting for transfers between devices, exchange(): lax.ppermute(passed, 'pair', [(p, p ^ 1 << bit) for p in range(pairs)])  9.32 us
    ppermute x2, waiting for transfers between devices, on_device(): lax.ppermute(part, 'wide', [(w, (w + 2 * hop) % wides) for w in range(wid...  8.47 us
    pallas_call x2, Pallas kernels, start_chunk(): pl.pallas_call(functools.partial(chunk_kernel, index, wides), out_shape=[...  3.82 us
    pallas_call x1, Pallas kernels, on_device(): pl.pallas_call(weight_kernel, out_shape=[jax.ShapeDtypeStruct((blocks, SU...  3.55 us
    pallas_call x1, Pallas kernels, on_device(): pl.pallas_call(functools.partial(degrid_kernel, pairs), out_shape=jax.Sha...  3.38 us
  transfers between devices with their start and end apart: 20, of which 7 were waited for; matrix products, arithmetic and copies ran while one was open for 2% of the time, Pallas kernels for 26%

profile of v6, /device:TPU:0, one launch (start us, length us, event | category | flops | bytes accessed | tf_op | source)
XLA Modules:
  0.0 69.1 jit_solution(18442428696462086823)
XLA Ops:
  0.0 1.3 %fusion.16 = (bf16[2,1024,128]{2,1,0:T(8,128)(2,1)S(1)}, bf16[2,1024,128]{2,1,0:T(8,128)(2,1)S(1)}) fusion(bf16[2,1024,256]{2,1,0:T(8,128)(2,1)} %bitcast.92), kind=kLoop, calls=%fused_computation.39 | loop fusion | bytes 2097152 | tf_op jit(solution)/shard_map/slice | solution.py:289
  1.3 3.0 %collective-permute-start.10 = (bf16[2,1024,128]{2,1,0:T(8,128)(2,1)S(1)}, bf16[2,1024,128]{2,1,0:T(8,128)(2,1)S(1)}, u32[]{:S(2)}, u32[]{:S(2)}) collective-permute-start(bf16[2,1024,128]{2,1,0:T(8,128)(2,1)S(1)} %get-tuple-element.33), channel_id=1, source_target_pairs={{0,8},{4,12},{8,0},{12,4},{1,9},{5,13},{9,1},{13,5},{2,10},{6,14},... | collective-permute-start | bytes 1572872 | tf_op jit(solution)/shard_map/ppermute | solution.py:292
  4.3 0.1 collective-permute-start
  4.4 0.8 %copy.7.offset_ref = s32[8,4,2]{2,1,0:T(4,128)S(1)} copy(s32[8,4,2]{0,2,1:T(2,128)} %param.7) | data formatting | bytes 512 | tf_op args[1]
  5.2 0.1 pad_add_fusion.place_ref
  5.3 1.2 %copy-done = bf16[1,2,1024,256]{3,2,1,0:T(8,128)(2,1)S(1)} copy-done((bf16[1,2,1024,256]{3,2,1,0:T(8,128)(2,1)S(1)}, bf16[1,2,1024,256]{3,2,1,0:T(8,128)(2,1)}, u32[]{:S(2)}) %copy-start) | copy-done | bytes 1048600
  6.5 10.5 %prepare.1 = (bf16[1,4,256,2048]{3,2,1,0:T(8,128)(2,1)S(1)}, f32[4,256,256]{2,1,0:T(8,128)S(1)}, f32[4,256,256]{2,1,0:T(8,128)S(1)}, f32[1,4,2,512]{3,2,1,0:T(2,128)S(1)}) custom-call(s32[8,4,2]{2,1,0:T(4,128)S(1)} %copy.7.offset_ref, s32[3]{0:T(128)S(1)} %pad_add_fusion.place_ref, bf16[2,1024,256]{2,1,0:T(8,128)(2,1)S(1)} %bitcast.93), custom_call_target="tpu_custom_call" | custom-call | flops 12099999744 | bytes 1048576 | tf_op jit(solution)/shard_map/prepare/pallas_call | solution.py:299
  17.0 0.1 collective-permute-done.10.refs_0_
  17.1 1.9 %chunk_sums.3 = (f32[2,2,128,128]{3,2,1,0:T(8,128)S(1)}, f32[2,2,128,128]{3,2,1,0:T(8,128)S(1)}, f32[2,2,128,128]{3,2,1,0:T(8,128)S(1)}, f32[2,2,128,128]{3,2,1,0:T(8,128)S(1)}) custom-call(s32[3]{0:T(128)S(1)} %pad_add_fusion.place_ref, bf16[1,4,256,2048]{3,2,1,0:T(8,128)(2,1)S(1)} %get-tuple-element.21.rest_ref, ...), custom_call_target="tpu_custom_call" | custom-call | flops 2420000000 | bytes 1048576 | tf_op jit(solution)/shard_map/chunk_sums/pallas_call | solution.py:325
  19.0 0.1 collective-permute-start.11
  19.1 8.4 %collective-permute-done.refs_0_ = bf16[2,1024,128]{2,1,0:T(8,128)(2,1)S(1)} collective-permute-done((bf16[2,1024,128]{2,1,0:T(8,128)(2,1)S(1)}, bf16[2,1024,128]{2,1,0:T(8,128)(2,1)S(1)}, u32[]{:S(2)}, u32[]{:S(2)}) %collective-permute-start) | collective-permute-done | bytes 524320 | tf_op jit(solution)/shard_map/ppermute | solution.py:292
  27.5 1.9 %chunk_sums.2 = (f32[2,2,128,128]{3,2,1,0:T(8,128)S(1)}, f32[2,2,128,128]{3,2,1,0:T(8,128)S(1)}, f32[2,2,128,128]{3,2,1,0:T(8,128)S(1)}, f32[2,2,128,128]{3,2,1,0:T(8,128)S(1)}) custom-call(s32[3]{0:T(128)S(1)} %pad_add_fusion.place_ref, bf16[1,4,256,2048]{3,2,1,0:T(8,128)(2,1)S(1)} %get-tuple-element.21.rest_ref, ...), custom_call_target="tpu_custom_call" | custom-call | flops 2420000000 | bytes 1048576 | tf_op jit(solution)/shard_map/chunk_sums/pallas_call | solution.py:325
  29.4 0.0 copy-start.1
  29.4 0.0 copy-start.2
  29.4 0.1 collective-permute-start.1
  29.5 0.5 collective-permute-start.13
  30.0 0.1 collective-permute-start.3
  30.1 0.0 collective-permute-done.11
  30.1 1.9 %collective-permute-start.12 = (f32[2,128,128]{2,1,0:T(8,128)S(1)}, f32[2,128,128]{2,1,0:T(8,128)S(1)}, u32[]{:S(2)}, u32[]{:S(2)}) collective-permute-start(f32[2,128,128]{2,1,0:T(8,128)S(1)} %get-tuple-element.35), channel_id=1, source_target_pairs={{0,1},{1,0},{2,3},{3,2},{4,5},{5,4},{6,7},{7,6},{8,9},{9,8},{10,11... | collective-permute-start | bytes 393224 | tf_op jit(solution)/shard_map/ppermute | solution.py:358
  32.0 0.2 collective-permute-start.15
  32.2 0.0 collective-permute-done.1
  32.2 1.9 %collective-permute-start.2 = (f32[2,128,128]{2,1,0:T(8,128)S(1)}, f32[2,128,128]{2,1,0:T(8,128)S(1)}, u32[]{:S(2)}, u32[]{:S(2)}) collective-permute-start(f32[2,128,128]{2,1,0:T(8,128)S(1)} %get-tuple-element.39), channel_id=1, source_target_pairs={{0,1},{1,0},{2,3},{3,2},{4,5},{5,4},{6,7},{7,6},{8,9},{9,8},{10,11... | collective-permute-start | bytes 393224 | tf_op jit(solution)/shard_map/ppermute | solution.py:358
  34.1 0.2 collective-permute-start.5
  34.4 0.0 collective-permute-done.3
  34.4 2.0 %collective-permute-done.12 = f32[2,128,128]{2,1,0:T(8,128)S(1)} collective-permute-done((f32[2,128,128]{2,1,0:T(8,128)S(1)}, f32[2,128,128]{2,1,0:T(8,128)S(1)}, u32[]{:S(2)}, u32[]{:S(2)}) %collective-permute-start.12) | collective-permute-done | bytes 131104 | tf_op jit(solution)/shard_map/ppermute | solution.py:358
  36.5 2.9 %collective-permute-start.14 = (f32[128,128]{1,0:T(8,128)S(1)}, f32[128,128]{1,0:T(8,128)S(1)}, u32[]{:S(2)}, u32[]{:S(2)}) collective-permute-start(f32[128,128]{1,0:T(8,128)S(1)} %fusion.7), channel_id=1, source_target_pairs={{0,2},{1,3},{2,0},{3,1},{4,6},{5,7},{6,4},{7,5},{8,10},{9,11},{10,... | collective-permute-start | bytes 196616 | tf_op jit(solution)/shard_map/ppermute | solution.py:358
  39.4 0.0 collective-permute-done.15
  39.4 2.8 %collective-permute-start.16 = (f32[128,128]{1,0:T(8,128)S(1)}, f32[128,128]{1,0:T(8,128)S(1)}, u32[]{:S(2)}, u32[]{:S(2)}) collective-permute-start(f32[128,128]{1,0:T(8,128)S(1)} %fusion.5), channel_id=1, source_target_pairs={{0,2},{1,3},{2,0},{3,1},{4,6},{5,7},{6,4},{7,5},{8,10},{9,11},{10,... | collective-permute-start | bytes 196616 | tf_op jit(solution)/shard_map/ppermute | solution.py:358
  42.2 2.7 %collective-permute-done.2 = f32[2,128,128]{2,1,0:T(8,128)S(1)} collective-permute-done((f32[2,128,128]{2,1,0:T(8,128)S(1)}, f32[2,128,128]{2,1,0:T(8,128)S(1)}, u32[]{:S(2)}, u32[]{:S(2)}) %collective-permute-start.2) | collective-permute-done | bytes 131104 | tf_op jit(solution)/shard_map/ppermute | solution.py:358
  44.9 1.1 %collective-permute-start.4 = (f32[128,128]{1,0:T(8,128)S(1)}, f32[128,128]{1,0:T(8,128)S(1)}, u32[]{:S(2)}, u32[]{:S(2)}) collective-permute-start(f32[128,128]{1,0:T(8,128)S(1)} %fusion.11), channel_id=1, source_target_pairs={{0,2},{1,3},{2,0},{3,1},{4,6},{5,7},{6,4},{7,5},{8,10},{9,11},{10,... | collective-permute-start | bytes 196616 | tf_op jit(solution)/shard_map/ppermute | solution.py:358
  46.0 1.4 %collective-permute-done.5 = f32[2,128,128]{2,1,0:T(8,128)S(1)} collective-permute-done((f32[2,128,128]{2,1,0:T(8,128)S(1)}, f32[2,128,128]{2,1,0:T(8,128)S(1)}, u32[]{:S(2)}, u32[]{:S(2)}) %collective-permute-start.5) | collective-permute-done | bytes 131104 | tf_op jit(solution)/shard_map/ppermute | solution.py:358
  47.5 1.6 %collective-permute-start.6 = (f32[128,128]{1,0:T(8,128)S(1)}, f32[128,128]{1,0:T(8,128)S(1)}, u32[]{:S(2)}, u32[]{:S(2)}) collective-permute-start(f32[128,128]{1,0:T(8,128)S(1)} %fusion.9), channel_id=1, source_target_pairs={{0,2},{1,3},{2,0},{3,1},{4,6},{5,7},{6,4},{7,5},{8,10},{9,11},{10,... | collective-permute-start | bytes 196616 | tf_op jit(solution)/shard_map/ppermute | solution.py:358
  49.0 0.0 collective-permute-done.14
  49.1 0.0 collective-permute-done.16
  49.1 2.5 %collective-permute-start.17 = (bf16[2,128,128]{2,1,0:T(8,128)(2,1)S(1)}, bf16[2,128,128]{2,1,0:T(8,128)(2,1)S(1)}, u32[]{:S(2)}, u32[]{:S(2)}) collective-permute-start(bf16[2,128,128]{2,1,0:T(8,128)(2,1)S(1)} %pad_maximum_fusion.1.refs_4_), channel_id=1, source_target_pairs={{0,1},{1,0},{2,3},{3,2},{4,5},{5,4},{6,7},{7,6},{8,9},{9,8},{10,11... | collective-permute-start | bytes 196616 | tf_op jit(solution)/shard_map/ppermute | solution.py:389
  51.7 1.6 %collective-permute-start.18 = (bf16[2,128,128]{2,1,0:T(8,128)(2,1)S(1)}, bf16[2,128,128]{2,1,0:T(8,128)(2,1)S(1)}, u32[]{:S(2)}, u32[]{:S(2)}) collective-permute-start(bf16[2,128,128]{2,1,0:T(8,128)(2,1)S(1)} %pad_maximum_fusion.1.refs_4_), channel_id=1, source_target_pairs={{0,2},{1,3},{2,0},{3,1},{4,6},{5,7},{6,4},{7,5},{8,10},{9,11},{10,... | collective-permute-start | bytes 196616 | tf_op jit(solution)/shard_map/ppermute | solution.py:389
  53.3 0.8 %collective-permute-start.19 = (bf16[2,128,128]{2,1,0:T(8,128)(2,1)S(1)}, bf16[2,128,128]{2,1,0:T(8,128)(2,1)S(1)}, u32[]{:S(2)}, u32[]{:S(2)}) collective-permute-start(bf16[2,128,128]{2,1,0:T(8,128)(2,1)S(1)} %pad_maximum_fusion.1.refs_4_), channel_id=1, source_target_pairs={{0,3},{1,2},{2,1},{3,0},{4,7},{5,6},{6,5},{7,4},{8,11},{9,10},{10,... | collective-permute-start | bytes 196616 | tf_op jit(solution)/shard_map/ppermute | solution.py:389
  54.1 3.2 %collective-permute-done.6 = f32[128,128]{1,0:T(8,128)S(1)} collective-permute-done((f32[128,128]{1,0:T(8,128)S(1)}, f32[128,128]{1,0:T(8,128)S(1)}, u32[]{:S(2)}, u32[]{:S(2)}) %collective-permute-start.6) | collective-permute-done | bytes 65568 | tf_op jit(solution)/shard_map/ppermute | solution.py:358
  57.4 0.0 copy-start.3
  57.4 0.0 copy-start.4
  57.4 0.1 collective-permute-start.7
  57.5 1.9 %collective-permute-start.8 = (bf16[2,128,128]{2,1,0:T(8,128)(2,1)S(1)}, bf16[2,128,128]{2,1,0:T(8,128)(2,1)S(1)}, u32[]{:S(2)}, u32[]{:S(2)}) collective-permute-start(bf16[2,128,128]{2,1,0:T(8,128)(2,1)S(1)} %pad_maximum_fusion.refs_0_), channel_id=1, source_target_pairs={{0,2},{1,3},{2,0},{3,1},{4,6},{5,7},{6,4},{7,5},{8,10},{9,11},{10,... | collective-permute-start | bytes 196616 | tf_op jit(solution)/shard_map/ppermute | solution.py:389
  59.4 2.5 %collective-permute-start.9 = (bf16[2,128,128]{2,1,0:T(8,128)(2,1)S(1)}, bf16[2,128,128]{2,1,0:T(8,128)(2,1)S(1)}, u32[]{:S(2)}, u32[]{:S(2)}) collective-permute-start(bf16[2,128,128]{2,1,0:T(8,128)(2,1)S(1)} %pad_maximum_fusion.refs_0_), channel_id=1, source_target_pairs={{0,3},{1,2},{2,1},{3,0},{4,7},{5,6},{6,5},{7,4},{8,11},{9,10},{10,... | collective-permute-start | bytes 196616 | tf_op jit(solution)/shard_map/ppermute | solution.py:389
  61.8 3.5 %weights.1 = (bf16[2,256,2048]{2,1,0:T(8,128)(2,1)S(1)}, f32[2,256,2048]{2,1,0:T(8,128)S(1)}) custom-call(s32[2,2]{1,0:T(2,128)S(1)} %copy-done.2, s32[2,2,2048]{2,1,0:T(2,128)S(1)} %copy-done.1), custom_call_target="tpu_custom_call" | custom-call | flops 5500000256 | bytes 1048576 | tf_op jit(solution)/shard_map/weights/pallas_call | solution.py:366
  65.4 0.0 collective-permute-done.19.refs_7_
  65.4 0.0 collective-permute-done.7.refs_1_
  65.4 0.3 collective-permute-done.8.refs_2_
  65.8 3.4 %degrid.1 = f32[2,2,2048]{2,1,0:T(2,128)} custom-call(s32[3]{0:T(128)S(1)} %pad_add_fusion.place_ref, s32[2]{0:T(128)S(1)} %copy-done.3, bf16[2,256,2048]{2,1,0:T(8,128)(2,1)S(1)} %get-tuple-element.19.row_ref, f32[2,256,2048]{2,1,0:T(8,128)S(1)} %get-tuple-element.20.col_ref, bf16[512,512]{1,0:T(8,128)(2,1)S(1)} %copy-done.4, ...), custom_call_target="tpu_custom_call" | custom-call | flops 3300000000 | bytes 1048576 | tf_op jit(solution)/shard_map/degrid/pallas_call | solution.py:392
  (24 shorter events, 0.3 us)
Async XLA Ops:
  1.3 15.8 %collective-permute-start.10 = (bf16[2,1024,128]{2,1,0:T(8,128)(2,1)S(1)}, bf16[2,1024,128]{2,1,0:T(8,128)(2,1)S(1)}, u32[]{:S(2)}, u32[]{:S(2)}) collective-permute-start(bf16[2,1024,128]{2,1,0:T(8,128)(2,1)S(1)} %get-tuple-element.33), channel_id=1, source_target_pairs={{0,8},{4,12},{8,0},{12,4},{1,9},{5,13},{9,1},{13,5},{2,10},{6,14},... | collective-permute-start | bytes 1572872 | tf_op jit(solution)/shard_map/ppermute | solution.py:292
  4.3 23.2 %collective-permute-start = (bf16[2,1024,128]{2,1,0:T(8,128)(2,1)S(1)}, bf16[2,1024,128]{2,1,0:T(8,128)(2,1)S(1)}, u32[]{:S(2)}, u32[]{:S(2)}) collective-permute-start(bf16[2,1024,128]{2,1,0:T(8,128)(2,1)S(1)} %get-tuple-element.34), channel_id=1, source_target_pairs={{0,8},{4,12},{8,0},{12,4},{1,9},{5,13},{9,1},{13,5},{2,10},{6,14},... | collective-permute-start | bytes 1572872 | tf_op jit(solution)/shard_map/ppermute | solution.py:292
  5.2 1.2 %copy-start = (bf16[1,2,1024,256]{3,2,1,0:T(8,128)(2,1)S(1)}, bf16[1,2,1024,256]{3,2,1,0:T(8,128)(2,1)}, u32[]{:S(2)}) copy-start(bf16[1,2,1024,256]{3,2,1,0:T(8,128)(2,1)} %param.6) | copy-start | bytes 3145732
  19.0 11.1 %collective-permute-start.11 = (f32[2,2,128,128]{3,2,1,0:T(8,128)S(1)}, f32[2,2,128,128]{3,2,1,0:T(8,128)S(1)}, u32[]{:S(2)}, u32[]{:S(2)}) collective-permute-start(f32[2,2,128,128]{3,2,1,0:T(8,128)S(1)} %get-tuple-element.30), channel_id=1, source_target_pairs={{0,4},{4,0},{8,12},{12,8},{1,5},{5,1},{9,13},{13,9},{2,6},{6,2},{1... | collective-permute-start | bytes 786440 | tf_op jit(solution)/shard_map/ppermute | solution.py:337
  29.4 32.5 %copy-start.1 = (s32[2,2,2048]{2,1,0:T(2,128)S(1)}, s32[2,2,2048]{2,1,0:T(2,128)}, u32[]{:S(2)}) copy-start(s32[2,2,2048]{2,1,0:T(2,128)} %cells_ref.1) | copy-start | bytes 98308
  29.4 32.5 %copy-start.2 = (s32[2,2]{1,0:T(2,128)S(1)}, s32[2,2]{1,0:T(2,128)}, u32[]{:S(2)}) copy-start(s32[2,2]{1,0:T(2,128)} %fraction_ref.1) | copy-start | bytes 52
  29.4 2.8 %collective-permute-start.1 = (f32[2,2,128,128]{3,2,1,0:T(8,128)S(1)}, f32[2,2,128,128]{3,2,1,0:T(8,128)S(1)}, u32[]{:S(2)}, u32[]{:S(2)}) collective-permute-start(f32[2,2,128,128]{3,2,1,0:T(8,128)S(1)} %get-tuple-element.25), channel_id=1, source_target_pairs={{0,4},{4,0},{8,12},{12,8},{1,5},{5,1},{9,13},{13,9},{2,6},{6,2},{1... | collective-permute-start | bytes 786440 | tf_op jit(solution)/shard_map/ppermute | solution.py:337
  29.5 4.6 %collective-permute-start.13 = (f32[2,2,128,128]{3,2,1,0:T(8,128)S(1)}, f32[2,2,128,128]{3,2,1,0:T(8,128)S(1)}, u32[]{:S(2)}, u32[]{:S(2)}) collective-permute-start(f32[2,2,128,128]{3,2,1,0:T(8,128)S(1)} %get-tuple-element.32), channel_id=1, source_target_pairs={{0,4},{4,0},{8,12},{12,8},{1,5},{5,1},{9,13},{13,9},{2,6},{6,2},{1... | collective-permute-start | bytes 786440 | tf_op jit(solution)/shard_map/ppermute | solution.py:338
  30.0 4.4 %collective-permute-start.3 = (f32[2,2,128,128]{3,2,1,0:T(8,128)S(1)}, f32[2,2,128,128]{3,2,1,0:T(8,128)S(1)}, u32[]{:S(2)}, u32[]{:S(2)}) collective-permute-start(f32[2,2,128,128]{3,2,1,0:T(8,128)S(1)} %get-tuple-element.27), channel_id=1, source_target_pairs={{0,4},{4,0},{8,12},{12,8},{1,5},{5,1},{9,13},{13,9},{2,6},{6,2},{1... | collective-permute-start | bytes 786440 | tf_op jit(solution)/shard_map/ppermute | solution.py:338
  30.1 6.4 %collective-permute-start.12 = (f32[2,128,128]{2,1,0:T(8,128)S(1)}, f32[2,128,128]{2,1,0:T(8,128)S(1)}, u32[]{:S(2)}, u32[]{:S(2)}) collective-permute-start(f32[2,128,128]{2,1,0:T(8,128)S(1)} %get-tuple-element.35), channel_id=1, source_target_pairs={{0,1},{1,0},{2,3},{3,2},{4,5},{5,4},{6,7},{7,6},{8,9},{9,8},{10,11... | collective-permute-start | bytes 393224 | tf_op jit(solution)/shard_map/ppermute | solution.py:358
  32.0 7.4 %collective-permute-start.15 = (f32[2,128,128]{2,1,0:T(8,128)S(1)}, f32[2,128,128]{2,1,0:T(8,128)S(1)}, u32[]{:S(2)}, u32[]{:S(2)}) collective-permute-start(f32[2,128,128]{2,1,0:T(8,128)S(1)} %get-tuple-element.36), channel_id=1, source_target_pairs={{0,1},{1,0},{2,3},{3,2},{4,5},{5,4},{6,7},{7,6},{8,9},{9,8},{10,11... | collective-permute-start | bytes 393224 | tf_op jit(solution)/shard_map/ppermute | solution.py:358
  32.2 12.6 %collective-permute-start.2 = (f32[2,128,128]{2,1,0:T(8,128)S(1)}, f32[2,128,128]{2,1,0:T(8,128)S(1)}, u32[]{:S(2)}, u32[]{:S(2)}) collective-permute-start(f32[2,128,128]{2,1,0:T(8,128)S(1)} %get-tuple-element.39), channel_id=1, source_target_pairs={{0,1},{1,0},{2,3},{3,2},{4,5},{5,4},{6,7},{7,6},{8,9},{9,8},{10,11... | collective-permute-start | bytes 393224 | tf_op jit(solution)/shard_map/ppermute | solution.py:358
  34.1 13.3 %collective-permute-start.5 = (f32[2,128,128]{2,1,0:T(8,128)S(1)}, f32[2,128,128]{2,1,0:T(8,128)S(1)}, u32[]{:S(2)}, u32[]{:S(2)}) collective-permute-start(f32[2,128,128]{2,1,0:T(8,128)S(1)} %get-tuple-element.40), channel_id=1, source_target_pairs={{0,1},{1,0},{2,3},{3,2},{4,5},{5,4},{6,7},{7,6},{8,9},{9,8},{10,11... | collective-permute-start | bytes 393224 | tf_op jit(solution)/shard_map/ppermute | solution.py:358
  36.5 12.6 %collective-permute-start.14 = (f32[128,128]{1,0:T(8,128)S(1)}, f32[128,128]{1,0:T(8,128)S(1)}, u32[]{:S(2)}, u32[]{:S(2)}) collective-permute-start(f32[128,128]{1,0:T(8,128)S(1)} %fusion.7), channel_id=1, source_target_pairs={{0,2},{1,3},{2,0},{3,1},{4,6},{5,7},{6,4},{7,5},{8,10},{9,11},{10,... | collective-permute-start | bytes 196616 | tf_op jit(solution)/shard_map/ppermute | solution.py:358
  39.4 9.7 %collective-permute-start.16 = (f32[128,128]{1,0:T(8,128)S(1)}, f32[128,128]{1,0:T(8,128)S(1)}, u32[]{:S(2)}, u32[]{:S(2)}) collective-permute-start(f32[128,128]{1,0:T(8,128)S(1)} %fusion.5), channel_id=1, source_target_pairs={{0,2},{1,3},{2,0},{3,1},{4,6},{5,7},{6,4},{7,5},{8,10},{9,11},{10,... | collective-permute-start | bytes 196616 | tf_op jit(solution)/shard_map/ppermute | solution.py:358
  44.9 9.2 %collective-permute-start.4 = (f32[128,128]{1,0:T(8,128)S(1)}, f32[128,128]{1,0:T(8,128)S(1)}, u32[]{:S(2)}, u32[]{:S(2)}) collective-permute-start(f32[128,128]{1,0:T(8,128)S(1)} %fusion.11), channel_id=1, source_target_pairs={{0,2},{1,3},{2,0},{3,1},{4,6},{5,7},{6,4},{7,5},{8,10},{9,11},{10,... | collective-permute-start | bytes 196616 | tf_op jit(solution)/shard_map/ppermute | solution.py:358
  47.5 9.9 %collective-permute-start.6 = (f32[128,128]{1,0:T(8,128)S(1)}, f32[128,128]{1,0:T(8,128)S(1)}, u32[]{:S(2)}, u32[]{:S(2)}) collective-permute-start(f32[128,128]{1,0:T(8,128)S(1)} %fusion.9), channel_id=1, source_target_pairs={{0,2},{1,3},{2,0},{3,1},{4,6},{5,7},{6,4},{7,5},{8,10},{9,11},{10,... | collective-permute-start | bytes 196616 | tf_op jit(solution)/shard_map/ppermute | solution.py:358
  49.1 10.2 %collective-permute-start.17 = (bf16[2,128,128]{2,1,0:T(8,128)(2,1)S(1)}, bf16[2,128,128]{2,1,0:T(8,128)(2,1)S(1)}, u32[]{:S(2)}, u32[]{:S(2)}) collective-permute-start(bf16[2,128,128]{2,1,0:T(8,128)(2,1)S(1)} %pad_maximum_fusion.1.refs_4_), channel_id=1, source_target_pairs={{0,1},{1,0},{2,3},{3,2},{4,5},{5,4},{6,7},{7,6},{8,9},{9,8},{10,11... | collective-permute-start | bytes 196616 | tf_op jit(solution)/shard_map/ppermute | solution.py:389
  51.7 13.7 %collective-permute-start.18 = (bf16[2,128,128]{2,1,0:T(8,128)(2,1)S(1)}, bf16[2,128,128]{2,1,0:T(8,128)(2,1)S(1)}, u32[]{:S(2)}, u32[]{:S(2)}) collective-permute-start(bf16[2,128,128]{2,1,0:T(8,128)(2,1)S(1)} %pad_maximum_fusion.1.refs_4_), channel_id=1, source_target_pairs={{0,2},{1,3},{2,0},{3,1},{4,6},{5,7},{6,4},{7,5},{8,10},{9,11},{10,... | collective-permute-start | bytes 196616 | tf_op jit(solution)/shard_map/ppermute | solution.py:389
  53.3 12.1 %collective-permute-start.19 = (bf16[2,128,128]{2,1,0:T(8,128)(2,1)S(1)}, bf16[2,128,128]{2,1,0:T(8,128)(2,1)S(1)}, u32[]{:S(2)}, u32[]{:S(2)}) collective-permute-start(bf16[2,128,128]{2,1,0:T(8,128)(2,1)S(1)} %pad_maximum_fusion.1.refs_4_), channel_id=1, source_target_pairs={{0,3},{1,2},{2,1},{3,0},{4,7},{5,6},{6,5},{7,4},{8,11},{9,10},{10,... | collective-permute-start | bytes 196616 | tf_op jit(solution)/shard_map/ppermute | solution.py:389
  57.4 8.4 %copy-start.3 = (s32[2]{0:T(128)S(1)}, s32[2]{0:T(128)}, u32[]{:S(2)}) copy-start(s32[2]{0:T(128)} %pick_ref.1) | copy-start | bytes 28
  57.4 8.4 %copy-start.4 = (bf16[512,512]{1,0:T(8,128)(2,1)S(1)}, bf16[512,512]{1,0:T(8,128)(2,1)}, u32[]{:S(2)}) copy-start(bf16[512,512]{1,0:T(8,128)(2,1)} %constant.59.clone.table_ref) | copy-start | bytes 1572868
  57.4 8.0 %collective-permute-start.7 = (bf16[2,128,128]{2,1,0:T(8,128)(2,1)S(1)}, bf16[2,128,128]{2,1,0:T(8,128)(2,1)S(1)}, u32[]{:S(2)}, u32[]{:S(2)}) collective-permute-start(bf16[2,128,128]{2,1,0:T(8,128)(2,1)S(1)} %pad_maximum_fusion.refs_0_), channel_id=1, source_target_pairs={{0,1},{1,0},{2,3},{3,2},{4,5},{5,4},{6,7},{7,6},{8,9},{9,8},{10,11... | collective-permute-start | bytes 196616 | tf_op jit(solution)/shard_map/ppermute | solution.py:389
  57.5 8.3 %collective-permute-start.8 = (bf16[2,128,128]{2,1,0:T(8,128)(2,1)S(1)}, bf16[2,128,128]{2,1,0:T(8,128)(2,1)S(1)}, u32[]{:S(2)}, u32[]{:S(2)}) collective-permute-start(bf16[2,128,128]{2,1,0:T(8,128)(2,1)S(1)} %pad_maximum_fusion.refs_0_), channel_id=1, source_target_pairs={{0,2},{1,3},{2,0},{3,1},{4,6},{5,7},{6,4},{7,5},{8,10},{9,11},{10,... | collective-permute-start | bytes 196616 | tf_op jit(solution)/shard_map/ppermute | solution.py:389
  59.4 6.4 %collective-permute-start.9 = (bf16[2,128,128]{2,1,0:T(8,128)(2,1)S(1)}, bf16[2,128,128]{2,1,0:T(8,128)(2,1)S(1)}, u32[]{:S(2)}, u32[]{:S(2)}) collective-permute-start(bf16[2,128,128]{2,1,0:T(8,128)(2,1)S(1)} %pad_maximum_fusion.refs_0_), channel_id=1, source_target_pairs={{0,3},{1,2},{2,1},{3,0},{4,7},{5,6},{6,5},{7,4},{8,11},{9,10},{10,... | collective-permute-start | bytes 196616 | tf_op jit(solution)/shard_map/ppermute | solution.py:389

commit v7 on v6

--- a/solution.py
+++ b/solution.py
@@ -222,6 +222,7 @@
 def weight_kernel(fraction_ref, cells_ref, row_ref, col_ref):
     width = 512
     scale = -1.0 / (2.88 * math.log(2.0))
+    half = (SUPPORT - 1) / 2.0
     ids = lax.broadcasted_iota(jnp.int32, (SUBW, width), 0).astype(jnp.float32)
     for block in range(cells_ref.shape[0]):
         for part, target in ((0, row_ref), (1, col_ref)):
@@ -229,10 +230,11 @@
 
             def one_part(step, carry):
                 lanes = pl.ds(pl.multiple_of(step * width, width), width)
-                distance = ids - cells_ref[block, part : part + 1, lanes].astype(jnp.float32)
-                offset = distance - centre
+                middle = cells_ref[block, part : part + 1, lanes].astype(jnp.float32) + half
+                distance = ids - middle
+                offset = distance - (centre - half)
                 values = jnp.exp2(offset * offset * scale + norm)
-                inside = jnp.abs(distance - (SUPPORT - 1) / 2.0) < SUPPORT / 2.0
+                inside = jnp.abs(distance) < SUPPORT / 2.0
                 target[block, :, lanes] = jnp.where(inside, values, 0.0).astype(target.dtype)
                 return carry
 

time: 69.3 us -> 69.3 us (level)
  no operation moved by 1% of the time
where the time goes in v7:
time: 69.3 us; the launch traced here: 69.1 us
  starting transfers between devices  25.9 us (37%)
  Pallas kernels  21 us (30%)
  waiting for transfers between devices  18.4 us (27%)
  local copies, waits for them, and re-layouts  3.3 us (5%)
    ppermute x8, starting transfers between devices, exchange(): lax.ppermute(passed, 'pair', [(p, p ^ 1 << bit) for p in range(pairs)])  12.6 us
    pallas_call x1, Pallas kernels, on_device(): pl.pallas_call(functools.partial(prep_kernel, wides), out_shape=[jax.Shap...  10.5 us
    ppermute x6, starting transfers between devices, on_device(): lax.ppermute(parts[0], 'pair', [(p, p ^ step) for p in range(pairs)])  9.43 us
    ppermute x8, waiting for transfers between devices, exchange(): lax.ppermute(passed, 'pair', [(p, p ^ 1 << bit) for p in range(pairs)])  9.32 us
    ppermute x2, waiting for transfers between devices, on_device(): lax.ppermute(part, 'wide', [(w, (w + 2 * hop) % wides) for w in range(wid...  8.47 us
    pallas_call x2, Pallas kernels, start_chunk(): pl.pallas_call(functools.partial(chunk_kernel, index, wides), out_shape=[...  3.82 us
    pallas_call x1, Pallas kernels, on_device(): pl.pallas_call(functools.partial(degrid_kernel, pairs), out_shape=jax.Sha...  3.38 us
    pallas_call x1, Pallas kernels, on_device(): pl.pallas_call(weight_kernel, out_shape=[jax.ShapeDtypeStruct((blocks, SU...  3.3 us
  transfers between devices with their start and end apart: 20, of which 7 were waited for; matrix products, arithmetic and copies ran while one was open for 2% of the time, Pallas kernels for 26%

profile of v7, /device:TPU:0, one launch (start us, length us, event | category | flops | bytes accessed | tf_op | source)
XLA Modules:
  0.0 69.1 jit_solution(13655868129098072351)
XLA Ops:
  0.0 1.3 %fusion.16 = (bf16[2,1024,128]{2,1,0:T(8,128)(2,1)S(1)}, bf16[2,1024,128]{2,1,0:T(8,128)(2,1)S(1)}) fusion(bf16[2,1024,256]{2,1,0:T(8,128)(2,1)} %bitcast.92), kind=kLoop, calls=%fused_computation.39 | loop fusion | bytes 2097152 | tf_op jit(solution)/shard_map/slice | solution.py:291
  1.3 3.0 %collective-permute-start.10 = (bf16[2,1024,128]{2,1,0:T(8,128)(2,1)S(1)}, bf16[2,1024,128]{2,1,0:T(8,128)(2,1)S(1)}, u32[]{:S(2)}, u32[]{:S(2)}) collective-permute-start(bf16[2,1024,128]{2,1,0:T(8,128)(2,1)S(1)} %get-tuple-element.33), channel_id=1, source_target_pairs={{0,8},{4,12},{8,0},{12,4},{1,9},{5,13},{9,1},{13,5},{2,10},{6,14},... | collective-permute-start | bytes 1572872 | tf_op jit(solution)/shard_map/ppermute | solution.py:294
  4.3 0.1 collective-permute-start
  4.4 0.8 %copy.7.offset_ref = s32[8,4,2]{2,1,0:T(4,128)S(1)} copy(s32[8,4,2]{0,2,1:T(2,128)} %param.7) | data formatting | bytes 512 | tf_op args[1]
  5.2 0.1 pad_add_fusion.place_ref
  5.3 1.2 %copy-done = bf16[1,2,1024,256]{3,2,1,0:T(8,128)(2,1)S(1)} copy-done((bf16[1,2,1024,256]{3,2,1,0:T(8,128)(2,1)S(1)}, bf16[1,2,1024,256]{3,2,1,0:T(8,128)(2,1)}, u32[]{:S(2)}) %copy-start) | copy-done | bytes 1048600
  6.5 10.5 %prepare.1 = (bf16[1,4,256,2048]{3,2,1,0:T(8,128)(2,1)S(1)}, f32[4,256,256]{2,1,0:T(8,128)S(1)}, f32[4,256,256]{2,1,0:T(8,128)S(1)}, f32[1,4,2,512]{3,2,1,0:T(2,128)S(1)}) custom-call(s32[8,4,2]{2,1,0:T(4,128)S(1)} %copy.7.offset_ref, s32[3]{0:T(128)S(1)} %pad_add_fusion.place_ref, bf16[2,1024,256]{2,1,0:T(8,128)(2,1)S(1)} %bitcast.93), custom_call_target="tpu_custom_call" | custom-call | flops 12099999744 | bytes 1048576 | tf_op jit(solution)/shard_map/prepare/pallas_call | solution.py:301
  17.0 0.1 collective-permute-done.10.refs_0_
  17.1 1.9 %chunk_sums.3 = (f32[2,2,128,128]{3,2,1,0:T(8,128)S(1)}, f32[2,2,128,128]{3,2,1,0:T(8,128)S(1)}, f32[2,2,128,128]{3,2,1,0:T(8,128)S(1)}, f32[2,2,128,128]{3,2,1,0:T(8,128)S(1)}) custom-call(s32[3]{0:T(128)S(1)} %pad_add_fusion.place_ref, bf16[1,4,256,2048]{3,2,1,0:T(8,128)(2,1)S(1)} %get-tuple-element.21.rest_ref, ...), custom_call_target="tpu_custom_call" | custom-call | flops 2420000000 | bytes 1048576 | tf_op jit(solution)/shard_map/chunk_sums/pallas_call | solution.py:327
  19.0 0.1 collective-permute-start.11
  19.1 8.4 %collective-permute-done.refs_0_ = bf16[2,1024,128]{2,1,0:T(8,128)(2,1)S(1)} collective-permute-done((bf16[2,1024,128]{2,1,0:T(8,128)(2,1)S(1)}, bf16[2,1024,128]{2,1,0:T(8,128)(2,1)S(1)}, u32[]{:S(2)}, u32[]{:S(2)}) %collective-permute-start) | collective-permute-done | bytes 524320 | tf_op jit(solution)/shard_map/ppermute | solution.py:294
  27.5 1.9 %chunk_sums.2 = (f32[2,2,128,128]{3,2,1,0:T(8,128)S(1)}, f32[2,2,128,128]{3,2,1,0:T(8,128)S(1)}, f32[2,2,128,128]{3,2,1,0:T(8,128)S(1)}, f32[2,2,128,128]{3,2,1,0:T(8,128)S(1)}) custom-call(s32[3]{0:T(128)S(1)} %pad_add_fusion.place_ref, bf16[1,4,256,2048]{3,2,1,0:T(8,128)(2,1)S(1)} %get-tuple-element.21.rest_ref, ...), custom_call_target="tpu_custom_call" | custom-call | flops 2420000000 | bytes 1048576 | tf_op jit(solution)/shard_map/chunk_sums/pallas_call | solution.py:327
  29.4 0.0 copy-start.1
  29.4 0.0 copy-start.2
  29.4 0.1 collective-permute-start.1
  29.5 0.5 collective-permute-start.13
  30.0 0.1 collective-permute-start.3
  30.1 0.0 collective-permute-done.11
  30.1 1.9 %collective-permute-start.12 = (f32[2,128,128]{2,1,0:T(8,128)S(1)}, f32[2,128,128]{2,1,0:T(8,128)S(1)}, u32[]{:S(2)}, u32[]{:S(2)}) collective-permute-start(f32[2,128,128]{2,1,0:T(8,128)S(1)} %get-tuple-element.35), channel_id=1, source_target_pairs={{0,1},{1,0},{2,3},{3,2},{4,5},{5,4},{6,7},{7,6},{8,9},{9,8},{10,11... | collective-permute-start | bytes 393224 | tf_op jit(solution)/shard_map/ppermute | solution.py:360
  32.0 0.2 collective-permute-start.15
  32.2 0.0 collective-permute-done.1
  32.2 1.9 %collective-permute-start.2 = (f32[2,128,128]{2,1,0:T(8,128)S(1)}, f32[2,128,128]{2,1,0:T(8,128)S(1)}, u32[]{:S(2)}, u32[]{:S(2)}) collective-permute-start(f32[2,128,128]{2,1,0:T(8,128)S(1)} %get-tuple-element.39), channel_id=1, source_target_pairs={{0,1},{1,0},{2,3},{3,2},{4,5},{5,4},{6,7},{7,6},{8,9},{9,8},{10,11... | collective-permute-start | bytes 393224 | tf_op jit(solution)/shard_map/ppermute | solution.py:360
  34.1 0.2 collective-permute-start.5
  34.4 0.0 collective-permute-done.3
  34.4 2.0 %collective-permute-done.12 = f32[2,128,128]{2,1,0:T(8,128)S(1)} collective-permute-done((f32[2,128,128]{2,1,0:T(8,128)S(1)}, f32[2,128,128]{2,1,0:T(8,128)S(1)}, u32[]{:S(2)}, u32[]{:S(2)}) %collective-permute-start.12) | collective-permute-done | bytes 131104 | tf_op jit(solution)/shard_map/ppermute | solution.py:360
  36.5 2.9 %collective-permute-start.14 = (f32[128,128]{1,0:T(8,128)S(1)}, f32[128,128]{1,0:T(8,128)S(1)}, u32[]{:S(2)}, u32[]{:S(2)}) collective-permute-start(f32[128,128]{1,0:T(8,128)S(1)} %fusion.7), channel_id=1, source_target_pairs={{0,2},{1,3},{2,0},{3,1},{4,6},{5,7},{6,4},{7,5},{8,10},{9,11},{10,... | collective-permute-start | bytes 196616 | tf_op jit(solution)/shard_map/ppermute | solution.py:360
  39.4 0.0 collective-permute-done.15
  39.4 2.8 %collective-permute-start.16 = (f32[128,128]{1,0:T(8,128)S(1)}, f32[128,128]{1,0:T(8,128)S(1)}, u32[]{:S(2)}, u32[]{:S(2)}) collective-permute-start(f32[128,128]{1,0:T(8,128)S(1)} %fusion.5), channel_id=1, source_target_pairs={{0,2},{1,3},{2,0},{3,1},{4,6},{5,7},{6,4},{7,5},{8,10},{9,11},{10,... | collective-permute-start | bytes 196616 | tf_op jit(solution)/shard_map/ppermute | solution.py:360
  42.2 2.7 %collective-permute-done.2 = f32[2,128,128]{2,1,0:T(8,128)S(1)} collective-permute-done((f32[2,128,128]{2,1,0:T(8,128)S(1)}, f32[2,128,128]{2,1,0:T(8,128)S(1)}, u32[]{:S(2)}, u32[]{:S(2)}) %collective-permute-start.2) | collective-permute-done | bytes 131104 | tf_op jit(solution)/shard_map/ppermute | solution.py:360
  44.9 1.1 %collective-permute-start.4 = (f32[128,128]{1,0:T(8,128)S(1)}, f32[128,128]{1,0:T(8,128)S(1)}, u32[]{:S(2)}, u32[]{:S(2)}) collective-permute-start(f32[128,128]{1,0:T(8,128)S(1)} %fusion.11), channel_id=1, source_target_pairs={{0,2},{1,3},{2,0},{3,1},{4,6},{5,7},{6,4},{7,5},{8,10},{9,11},{10,... | collective-permute-start | bytes 196616 | tf_op jit(solution)/shard_map/ppermute | solution.py:360
  46.0 1.4 %collective-permute-done.5 = f32[2,128,128]{2,1,0:T(8,128)S(1)} collective-permute-done((f32[2,128,128]{2,1,0:T(8,128)S(1)}, f32[2,128,128]{2,1,0:T(8,128)S(1)}, u32[]{:S(2)}, u32[]{:S(2)}) %collective-permute-start.5) | collective-permute-done | bytes 131104 | tf_op jit(solution)/shard_map/ppermute | solution.py:360
  47.5 1.6 %collective-permute-start.6 = (f32[128,128]{1,0:T(8,128)S(1)}, f32[128,128]{1,0:T(8,128)S(1)}, u32[]{:S(2)}, u32[]{:S(2)}) collective-permute-start(f32[128,128]{1,0:T(8,128)S(1)} %fusion.9), channel_id=1, source_target_pairs={{0,2},{1,3},{2,0},{3,1},{4,6},{5,7},{6,4},{7,5},{8,10},{9,11},{10,... | collective-permute-start | bytes 196616 | tf_op jit(solution)/shard_map/ppermute | solution.py:360
  49.0 0.0 collective-permute-done.14
  49.1 0.0 collective-permute-done.16
  49.1 2.5 %collective-permute-start.17 = (bf16[2,128,128]{2,1,0:T(8,128)(2,1)S(1)}, bf16[2,128,128]{2,1,0:T(8,128)(2,1)S(1)}, u32[]{:S(2)}, u32[]{:S(2)}) collective-permute-start(bf16[2,128,128]{2,1,0:T(8,128)(2,1)S(1)} %pad_maximum_fusion.1.refs_4_), channel_id=1, source_target_pairs={{0,1},{1,0},{2,3},{3,2},{4,5},{5,4},{6,7},{7,6},{8,9},{9,8},{10,11... | collective-permute-start | bytes 196616 | tf_op jit(solution)/shard_map/ppermute | solution.py:391
  51.7 1.6 %collective-permute-start.18 = (bf16[2,128,128]{2,1,0:T(8,128)(2,1)S(1)}, bf16[2,128,128]{2,1,0:T(8,128)(2,1)S(1)}, u32[]{:S(2)}, u32[]{:S(2)}) collective-permute-start(bf16[2,128,128]{2,1,0:T(8,128)(2,1)S(1)} %pad_maximum_fusion.1.refs_4_), channel_id=1, source_target_pairs={{0,2},{1,3},{2,0},{3,1},{4,6},{5,7},{6,4},{7,5},{8,10},{9,11},{10,... | collective-permute-start | bytes 196616 | tf_op jit(solution)/shard_map/ppermute | solution.py:391
  53.3 0.8 %collective-permute-start.19 = (bf16[2,128,128]{2,1,0:T(8,128)(2,1)S(1)}, bf16[2,128,128]{2,1,0:T(8,128)(2,1)S(1)}, u32[]{:S(2)}, u32[]{:S(2)}) collective-permute-start(bf16[2,128,128]{2,1,0:T(8,128)(2,1)S(1)} %pad_maximum_fusion.1.refs_4_), channel_id=1, source_target_pairs={{0,3},{1,2},{2,1},{3,0},{4,7},{5,6},{6,5},{7,4},{8,11},{9,10},{10,... | collective-permute-start | bytes 196616 | tf_op jit(solution)/shard_map/ppermute | solution.py:391
  54.1 3.2 %collective-permute-done.6 = f32[128,128]{1,0:T(8,128)S(1)} collective-permute-done((f32[128,128]{1,0:T(8,128)S(1)}, f32[128,128]{1,0:T(8,128)S(1)}, u32[]{:S(2)}, u32[]{:S(2)}) %collective-permute-start.6) | collective-permute-done | bytes 65568 | tf_op jit(solution)/shard_map/ppermute | solution.py:360
  57.4 0.0 copy-start.3
  57.4 0.0 copy-start.4
  57.4 0.1 collective-permute-start.7
  57.5 1.9 %collective-permute-start.8 = (bf16[2,128,128]{2,1,0:T(8,128)(2,1)S(1)}, bf16[2,128,128]{2,1,0:T(8,128)(2,1)S(1)}, u32[]{:S(2)}, u32[]{:S(2)}) collective-permute-start(bf16[2,128,128]{2,1,0:T(8,128)(2,1)S(1)} %pad_maximum_fusion.refs_0_), channel_id=1, source_target_pairs={{0,2},{1,3},{2,0},{3,1},{4,6},{5,7},{6,4},{7,5},{8,10},{9,11},{10,... | collective-permute-start | bytes 196616 | tf_op jit(solution)/shard_map/ppermute | solution.py:391
  59.4 2.5 %collective-permute-start.9 = (bf16[2,128,128]{2,1,0:T(8,128)(2,1)S(1)}, bf16[2,128,128]{2,1,0:T(8,128)(2,1)S(1)}, u32[]{:S(2)}, u32[]{:S(2)}) collective-permute-start(bf16[2,128,128]{2,1,0:T(8,128)(2,1)S(1)} %pad_maximum_fusion.refs_0_), channel_id=1, source_target_pairs={{0,3},{1,2},{2,1},{3,0},{4,7},{5,6},{6,5},{7,4},{8,11},{9,10},{10,... | collective-permute-start | bytes 196616 | tf_op jit(solution)/shard_map/ppermute | solution.py:391
  61.8 3.3 %weights.1 = (bf16[2,256,2048]{2,1,0:T(8,128)(2,1)S(1)}, f32[2,256,2048]{2,1,0:T(8,128)S(1)}) custom-call(s32[2,2]{1,0:T(2,128)S(1)} %copy-done.2, s32[2,2,2048]{2,1,0:T(2,128)S(1)} %copy-done.1), custom_call_target="tpu_custom_call" | custom-call | flops 5500000256 | bytes 1048576 | tf_op jit(solution)/shard_map/weights/pallas_call | solution.py:368
  65.2 0.0 collective-permute-done.7.refs_1_
  65.2 0.6 collective-permute-done.8.refs_2_
  65.8 0.0 collective-permute-done.9.refs_3_
  65.8 3.4 %degrid.1 = f32[2,2,2048]{2,1,0:T(2,128)} custom-call(s32[3]{0:T(128)S(1)} %pad_add_fusion.place_ref, s32[2]{0:T(128)S(1)} %copy-done.3, bf16[2,256,2048]{2,1,0:T(8,128)(2,1)S(1)} %get-tuple-element.19.row_ref, f32[2,256,2048]{2,1,0:T(8,128)S(1)} %get-tuple-element.20.col_ref, bf16[512,512]{1,0:T(8,128)(2,1)S(1)} %copy-done.4, ...), custom_call_target="tpu_custom_call" | custom-call | flops 3300000000 | bytes 1048576 | tf_op jit(solution)/shard_map/degrid/pallas_call | solution.py:394
  (24 shorter events, 0.3 us)
Async XLA Ops:
  1.3 15.8 %collective-permute-start.10 = (bf16[2,1024,128]{2,1,0:T(8,128)(2,1)S(1)}, bf16[2,1024,128]{2,1,0:T(8,128)(2,1)S(1)}, u32[]{:S(2)}, u32[]{:S(2)}) collective-permute-start(bf16[2,1024,128]{2,1,0:T(8,128)(2,1)S(1)} %get-tuple-element.33), channel_id=1, source_target_pairs={{0,8},{4,12},{8,0},{12,4},{1,9},{5,13},{9,1},{13,5},{2,10},{6,14},... | collective-permute-start | bytes 1572872 | tf_op jit(solution)/shard_map/ppermute | solution.py:294
  4.3 23.2 %collective-permute-start = (bf16[2,1024,128]{2,1,0:T(8,128)(2,1)S(1)}, bf16[2,1024,128]{2,1,0:T(8,128)(2,1)S(1)}, u32[]{:S(2)}, u32[]{:S(2)}) collective-permute-start(bf16[2,1024,128]{2,1,0:T(8,128)(2,1)S(1)} %get-tuple-element.34), channel_id=1, source_target_pairs={{0,8},{4,12},{8,0},{12,4},{1,9},{5,13},{9,1},{13,5},{2,10},{6,14},... | collective-permute-start | bytes 1572872 | tf_op jit(solution)/shard_map/ppermute | solution.py:294
  5.2 1.2 %copy-start = (bf16[1,2,1024,256]{3,2,1,0:T(8,128)(2,1)S(1)}, bf16[1,2,1024,256]{3,2,1,0:T(8,128)(2,1)}, u32[]{:S(2)}) copy-start(bf16[1,2,1024,256]{3,2,1,0:T(8,128)(2,1)} %param.6) | copy-start | bytes 3145732
  19.0 11.1 %collective-permute-start.11 = (f32[2,2,128,128]{3,2,1,0:T(8,128)S(1)}, f32[2,2,128,128]{3,2,1,0:T(8,128)S(1)}, u32[]{:S(2)}, u32[]{:S(2)}) collective-permute-start(f32[2,2,128,128]{3,2,1,0:T(8,128)S(1)} %get-tuple-element.30), channel_id=1, source_target_pairs={{0,4},{4,0},{8,12},{12,8},{1,5},{5,1},{9,13},{13,9},{2,6},{6,2},{1... | collective-permute-start | bytes 786440 | tf_op jit(solution)/shard_map/ppermute | solution.py:339
  29.4 32.5 %copy-start.1 = (s32[2,2,2048]{2,1,0:T(2,128)S(1)}, s32[2,2,2048]{2,1,0:T(2,128)}, u32[]{:S(2)}) copy-start(s32[2,2,2048]{2,1,0:T(2,128)} %cells_ref.1) | copy-start | bytes 98308
  29.4 32.5 %copy-start.2 = (s32[2,2]{1,0:T(2,128)S(1)}, s32[2,2]{1,0:T(2,128)}, u32[]{:S(2)}) copy-start(s32[2,2]{1,0:T(2,128)} %fraction_ref.1) | copy-start | bytes 52
  29.4 2.8 %collective-permute-start.1 = (f32[2,2,128,128]{3,2,1,0:T(8,128)S(1)}, f32[2,2,128,128]{3,2,1,0:T(8,128)S(1)}, u32[]{:S(2)}, u32[]{:S(2)}) collective-permute-start(f32[2,2,128,128]{3,2,1,0:T(8,128)S(1)} %get-tuple-element.25), channel_id=1, source_target_pairs={{0,4},{4,0},{8,12},{12,8},{1,5},{5,1},{9,13},{13,9},{2,6},{6,2},{1... | collective-permute-start | bytes 786440 | tf_op jit(solution)/shard_map/ppermute | solution.py:339
  29.5 4.6 %collective-permute-start.13 = (f32[2,2,128,128]{3,2,1,0:T(8,128)S(1)}, f32[2,2,128,128]{3,2,1,0:T(8,128)S(1)}, u32[]{:S(2)}, u32[]{:S(2)}) collective-permute-start(f32[2,2,128,128]{3,2,1,0:T(8,128)S(1)} %get-tuple-element.32), channel_id=1, source_target_pairs={{0,4},{4,0},{8,12},{12,8},{1,5},{5,1},{9,13},{13,9},{2,6},{6,2},{1... | collective-permute-start | bytes 786440 | tf_op jit(solution)/shard_map/ppermute | solution.py:340
  30.0 4.4 %collective-permute-start.3 = (f32[2,2,128,128]{3,2,1,0:T(8,128)S(1)}, f32[2,2,128,128]{3,2,1,0:T(8,128)S(1)}, u32[]{:S(2)}, u32[]{:S(2)}) collective-permute-start(f32[2,2,128,128]{3,2,1,0:T(8,128)S(1)} %get-tuple-element.27), channel_id=1, source_target_pairs={{0,4},{4,0},{8,12},{12,8},{1,5},{5,1},{9,13},{13,9},{2,6},{6,2},{1... | collective-permute-start | bytes 786440 | tf_op jit(solution)/shard_map/ppermute | solution.py:340
  30.1 6.4 %collective-permute-start.12 = (f32[2,128,128]{2,1,0:T(8,128)S(1)}, f32[2,128,128]{2,1,0:T(8,128)S(1)}, u32[]{:S(2)}, u32[]{:S(2)}) collective-permute-start(f32[2,128,128]{2,1,0:T(8,128)S(1)} %get-tuple-element.35), channel_id=1, source_target_pairs={{0,1},{1,0},{2,3},{3,2},{4,5},{5,4},{6,7},{7,6},{8,9},{9,8},{10,11... | collective-permute-start | bytes 393224 | tf_op jit(solution)/shard_map/ppermute | solution.py:360
  32.0 7.4 %collective-permute-start.15 = (f32[2,128,128]{2,1,0:T(8,128)S(1)}, f32[2,128,128]{2,1,0:T(8,128)S(1)}, u32[]{:S(2)}, u32[]{:S(2)}) collective-permute-start(f32[2,128,128]{2,1,0:T(8,128)S(1)} %get-tuple-element.36), channel_id=1, source_target_pairs={{0,1},{1,0},{2,3},{3,2},{4,5},{5,4},{6,7},{7,6},{8,9},{9,8},{10,11... | collective-permute-start | bytes 393224 | tf_op jit(solution)/shard_map/ppermute | solution.py:360
  32.2 12.6 %collective-permute-start.2 = (f32[2,128,128]{2,1,0:T(8,128)S(1)}, f32[2,128,128]{2,1,0:T(8,128)S(1)}, u32[]{:S(2)}, u32[]{:S(2)}) collective-permute-start(f32[2,128,128]{2,1,0:T(8,128)S(1)} %get-tuple-element.39), channel_id=1, source_target_pairs={{0,1},{1,0},{2,3},{3,2},{4,5},{5,4},{6,7},{7,6},{8,9},{9,8},{10,11... | collective-permute-start | bytes 393224 | tf_op jit(solution)/shard_map/ppermute | solution.py:360
  34.1 13.3 %collective-permute-start.5 = (f32[2,128,128]{2,1,0:T(8,128)S(1)}, f32[2,128,128]{2,1,0:T(8,128)S(1)}, u32[]{:S(2)}, u32[]{:S(2)}) collective-permute-start(f32[2,128,128]{2,1,0:T(8,128)S(1)} %get-tuple-element.40), channel_id=1, source_target_pairs={{0,1},{1,0},{2,3},{3,2},{4,5},{5,4},{6,7},{7,6},{8,9},{9,8},{10,11... | collective-permute-start | bytes 393224 | tf_op jit(solution)/shard_map/ppermute | solution.py:360
  36.5 12.6 %collective-permute-start.14 = (f32[128,128]{1,0:T(8,128)S(1)}, f32[128,128]{1,0:T(8,128)S(1)}, u32[]{:S(2)}, u32[]{:S(2)}) collective-permute-start(f32[128,128]{1,0:T(8,128)S(1)} %fusion.7), channel_id=1, source_target_pairs={{0,2},{1,3},{2,0},{3,1},{4,6},{5,7},{6,4},{7,5},{8,10},{9,11},{10,... | collective-permute-start | bytes 196616 | tf_op jit(solution)/shard_map/ppermute | solution.py:360
  39.4 9.7 %collective-permute-start.16 = (f32[128,128]{1,0:T(8,128)S(1)}, f32[128,128]{1,0:T(8,128)S(1)}, u32[]{:S(2)}, u32[]{:S(2)}) collective-permute-start(f32[128,128]{1,0:T(8,128)S(1)} %fusion.5), channel_id=1, source_target_pairs={{0,2},{1,3},{2,0},{3,1},{4,6},{5,7},{6,4},{7,5},{8,10},{9,11},{10,... | collective-permute-start | bytes 196616 | tf_op jit(solution)/shard_map/ppermute | solution.py:360
  44.9 9.2 %collective-permute-start.4 = (f32[128,128]{1,0:T(8,128)S(1)}, f32[128,128]{1,0:T(8,128)S(1)}, u32[]{:S(2)}, u32[]{:S(2)}) collective-permute-start(f32[128,128]{1,0:T(8,128)S(1)} %fusion.11), channel_id=1, source_target_pairs={{0,2},{1,3},{2,0},{3,1},{4,6},{5,7},{6,4},{7,5},{8,10},{9,11},{10,... | collective-permute-start | bytes 196616 | tf_op jit(solution)/shard_map/ppermute | solution.py:360
  47.5 9.9 %collective-permute-start.6 = (f32[128,128]{1,0:T(8,128)S(1)}, f32[128,128]{1,0:T(8,128)S(1)}, u32[]{:S(2)}, u32[]{:S(2)}) collective-permute-start(f32[128,128]{1,0:T(8,128)S(1)} %fusion.9), channel_id=1, source_target_pairs={{0,2},{1,3},{2,0},{3,1},{4,6},{5,7},{6,4},{7,5},{8,10},{9,11},{10,... | collective-permute-start | bytes 196616 | tf_op jit(solution)/shard_map/ppermute | solution.py:360
  49.1 10.2 %collective-permute-start.17 = (bf16[2,128,128]{2,1,0:T(8,128)(2,1)S(1)}, bf16[2,128,128]{2,1,0:T(8,128)(2,1)S(1)}, u32[]{:S(2)}, u32[]{:S(2)}) collective-permute-start(bf16[2,128,128]{2,1,0:T(8,128)(2,1)S(1)} %pad_maximum_fusion.1.refs_4_), channel_id=1, source_target_pairs={{0,1},{1,0},{2,3},{3,2},{4,5},{5,4},{6,7},{7,6},{8,9},{9,8},{10,11... | collective-permute-start | bytes 196616 | tf_op jit(solution)/shard_map/ppermute | solution.py:391
  51.7 13.5 %collective-permute-start.18 = (bf16[2,128,128]{2,1,0:T(8,128)(2,1)S(1)}, bf16[2,128,128]{2,1,0:T(8,128)(2,1)S(1)}, u32[]{:S(2)}, u32[]{:S(2)}) collective-permute-start(bf16[2,128,128]{2,1,0:T(8,128)(2,1)S(1)} %pad_maximum_fusion.1.refs_4_), channel_id=1, source_target_pairs={{0,2},{1,3},{2,0},{3,1},{4,6},{5,7},{6,4},{7,5},{8,10},{9,11},{10,... | collective-permute-start | bytes 196616 | tf_op jit(solution)/shard_map/ppermute | solution.py:391
  53.3 11.8 %collective-permute-start.19 = (bf16[2,128,128]{2,1,0:T(8,128)(2,1)S(1)}, bf16[2,128,128]{2,1,0:T(8,128)(2,1)S(1)}, u32[]{:S(2)}, u32[]{:S(2)}) collective-permute-start(bf16[2,128,128]{2,1,0:T(8,128)(2,1)S(1)} %pad_maximum_fusion.1.refs_4_), channel_id=1, source_target_pairs={{0,3},{1,2},{2,1},{3,0},{4,7},{5,6},{6,5},{7,4},{8,11},{9,10},{10,... | collective-permute-start | bytes 196616 | tf_op jit(solution)/shard_map/ppermute | solution.py:391
  57.4 8.4 %copy-start.3 = (s32[2]{0:T(128)S(1)}, s32[2]{0:T(128)}, u32[]{:S(2)}) copy-start(s32[2]{0:T(128)} %pick_ref.1) | copy-start | bytes 28
  57.4 8.4 %copy-start.4 = (bf16[512,512]{1,0:T(8,128)(2,1)S(1)}, bf16[512,512]{1,0:T(8,128)(2,1)}, u32[]{:S(2)}) copy-start(bf16[512,512]{1,0:T(8,128)(2,1)} %constant.59.clone.table_ref) | copy-start | bytes 1572868
  57.4 7.8 %collective-permute-start.7 = (bf16[2,128,128]{2,1,0:T(8,128)(2,1)S(1)}, bf16[2,128,128]{2,1,0:T(8,128)(2,1)S(1)}, u32[]{:S(2)}, u32[]{:S(2)}) collective-permute-start(bf16[2,128,128]{2,1,0:T(8,128)(2,1)S(1)} %pad_maximum_fusion.refs_0_), channel_id=1, source_target_pairs={{0,1},{1,0},{2,3},{3,2},{4,5},{5,4},{6,7},{7,6},{8,9},{9,8},{10,11... | collective-permute-start | bytes 196616 | tf_op jit(solution)/shard_map/ppermute | solution.py:391
  57.5 8.3 %collective-permute-start.8 = (bf16[2,128,128]{2,1,0:T(8,128)(2,1)S(1)}, bf16[2,128,128]{2,1,0:T(8,128)(2,1)S(1)}, u32[]{:S(2)}, u32[]{:S(2)}) collective-permute-start(bf16[2,128,128]{2,1,0:T(8,128)(2,1)S(1)} %pad_maximum_fusion.refs_0_), channel_id=1, source_target_pairs={{0,2},{1,3},{2,0},{3,1},{4,6},{5,7},{6,4},{7,5},{8,10},{9,11},{10,... | collective-permute-start | bytes 196616 | tf_op jit(solution)/shard_map/ppermute | solution.py:391
  59.4 6.4 %collective-permute-start.9 = (bf16[2,128,128]{2,1,0:T(8,128)(2,1)S(1)}, bf16[2,128,128]{2,1,0:T(8,128)(2,1)S(1)}, u32[]{:S(2)}, u32[]{:S(2)}) collective-permute-start(bf16[2,128,128]{2,1,0:T(8,128)(2,1)S(1)} %pad_maximum_fusion.refs_0_), channel_id=1, source_target_pairs={{0,3},{1,2},{2,1},{3,0},{4,7},{5,6},{6,5},{7,4},{8,11},{9,10},{10,... | collective-permute-start | bytes 196616 | tf_op jit(solution)/shard_map/ppermute | solution.py:391
